TPU v7x, 32 devices: a whole 2x2x4 slice. The times are simulated.
32 devices in a mesh: rep: 8 (over z, y), shard: 4 (over x, core).
Axes of the slice: x: 2, y: 2, z: 4, core: 2. Of those that a mesh axis runs over, the one named last changes fastest.
Arguments:
- images: bfloat16 [32, 8, 32, 640], P(('rep', 'shard')), may hold values from -6 to 6
- conv_weight: bfloat16 [5760, 640], P('shard'), may hold values from -0.078125 to 0.078125
- skip_weight: bfloat16 [640, 1280], P('shard'), may hold values from -0.25 to 0.25
- cotangent: bfloat16 [32, 4, 16, 1280], P(('rep', 'shard')), may hold values from -6 to 6
- hidden_cot: bfloat16 [32, 8, 32, 640], P(('rep', 'shard')), may hold values from -6 to 6
Outputs:
- hidden: bfloat16 [32, 8, 32, 640], P(('rep', 'shard'))
- projected: bfloat16 [32, 4, 16, 1280], P(('rep', 'shard'))
- input_grad: bfloat16 [32, 8, 32, 640], P(('rep', 'shard'))
- conv_grad: float32 [5760, 640], P('shard')
- skip_grad: float32 [640, 1280], P('shard')
All inputs are finite; a program needn't handle non-finite values.
Results may differ from a plain program's by a relative error of at most 0.0052.
Values may be sent and summed in bfloat16 or wider, within the bound.
No kernel may reach another device: no remote copies, remote signals or barrier semaphores. Data moves between devices by JAX's collectives and lax.ppermute only.
A program may use at most 128 MiB of HBM per device.

v0:
```python
import math

import jax
import jax.numpy as jnp
from jax import lax
from jax.sharding import PartitionSpec as P


def columns(channel_slab):
    number, height, width_cells, channels = channel_slab.shape
    padded = jnp.pad(channel_slab, ((0, 0), (1, 1), (1, 1), (0, 0)))
    shifts = [
        padded[:, row_off : row_off + height, col_off : col_off + width_cells, :]
        for row_off in range(3)
        for col_off in range(3)
    ]
    return jnp.stack(shifts, axis=-1).reshape(number * height * width_cells, channels * 9)


def scatter_back(pieces):
    height, width_cells = (pieces.shape[0], pieces.shape[1])
    running = jnp.zeros((height + 2, width_cells + 2, pieces.shape[2]), jnp.float32)
    for row_off in range(3):
        for col_off in range(3):
            running = running + jnp.pad(
                pieces[..., row_off * 3 + col_off],
                ((row_off, 2 - row_off), (col_off, 2 - col_off), (0, 0)),
            )
    return running[1:-1, 1:-1]


def spread_even(back_sub):
    blanks = jnp.zeros_like(back_sub)
    half_rows, half_cols, channels = back_sub.shape
    rowwise = jnp.stack([back_sub, blanks], axis=2).reshape(half_rows, 2 * half_cols, channels)
    return jnp.stack([rowwise, jnp.zeros_like(rowwise)], axis=1).reshape(
        2 * half_rows, 2 * half_cols, channels
    )


def block_channels():
    return 128


def on_device(images, conv_weight, skip_weight, cotangent, hidden_cot):
    source = images[0]
    height, width_cells, channels = source.shape
    wide_chans = skip_weight.shape[1]
    filters_all, skip_all = (
        lax.all_gather(conv_weight, "shard", axis=0, tiled=True),
        lax.all_gather(skip_weight, "shard", axis=0, tiled=True),
    )
    source_f = source.astype(jnp.float32)
    activated = jax.nn.silu(source_f).astype(jnp.bfloat16)
    step_chans = block_channels()
    convolved = jnp.zeros((height * width_cells, channels), jnp.float32)
    for block_index in range(channels // step_chans):
        first_chan = block_index * step_chans
        patches = columns(activated[None, :, :, first_chan : first_chan + step_chans])
        convolved = convolved + jnp.dot(
            patches,
            filters_all[first_chan * 9 : (first_chan + step_chans) * 9],
            preferred_element_type=jnp.float32,
        )
    hidden = (source_f + convolved.reshape(height, width_cells, channels)).astype(jnp.bfloat16)
    subsampled = hidden[::2, ::2].reshape(-1, channels)
    grad_rows = cotangent[0].reshape(-1, wide_chans)
    projected = (
        jnp.dot(subsampled, skip_all, preferred_element_type=jnp.float32)
        .astype(jnp.bfloat16)
        .reshape(cotangent.shape)
    )
    skip_term = lax.dot_general(
        subsampled, grad_rows, (((0,), (0,)), ((), ())), preferred_element_type=jnp.float32
    )
    back_sub = lax.dot_general(
        grad_rows, skip_all, (((1,), (1,)), ((), ())), preferred_element_type=jnp.float32
    ).astype(jnp.bfloat16)
    spread = spread_even(back_sub.reshape(height // 2, width_cells // 2, channels))
    hidden_grad = (hidden_cot[0].astype(jnp.float32) + spread.astype(jnp.float32)).astype(
        jnp.bfloat16
    )
    hidden_flat = hidden_grad.reshape(-1, channels)
    side_blocks = []
    for block_index in range(channels // step_chans):
        first_chan = block_index * step_chans
        rows_block = filters_all[first_chan * 9 : (first_chan + step_chans) * 9]
        tap_grads = lax.dot_general(
            hidden_flat, rows_block, (((1,), (1,)), ((), ())), preferred_element_type=jnp.float32
        )
        side_blocks.append(scatter_back(tap_grads.reshape(height, width_cells, step_chans, 9)))
    input_side = jnp.concatenate(side_blocks, axis=2)
    sigmoid = jax.nn.sigmoid(source_f)
    slope = sigmoid * (1.0 + source_f * (1.0 - sigmoid))
    input_grad = (hidden_grad.astype(jnp.float32) + slope * input_side).astype(jnp.bfloat16)[None]
    patches = columns(activated[None])
    conv_part = lax.psum_scatter(
        lax.dot_general(
            patches, hidden_flat, (((0,), (0,)), ((), ())), preferred_element_type=jnp.float32
        ),
        "shard",
        scatter_dimension=0,
        tiled=True,
    )
    skip_part = lax.psum_scatter(skip_term, "shard", scatter_dimension=0, tiled=True)
    conv_sum, skip_sum = lax.psum((conv_part, skip_part), "rep")
    grad_factor = 1.0 / math.sqrt(
        lax.axis_size("rep") * lax.axis_size("shard") * (height // 2) * (width_cells // 2)
    )
    return (hidden[None], projected, input_grad, conv_sum * grad_factor, skip_sum * grad_factor)


def solution(mesh):
    placed = (
        P(("rep", "shard"), None, None, None),
        P("shard", None),
        P("shard", None),
        P(("rep", "shard"), None, None, None),
        P(("rep", "shard"), None, None, None),
    )
    return jax.shard_map(
        on_device,
        mesh=mesh,
        in_specs=placed,
        out_specs=(
            P(("rep", "shard"), None, None, None),
            P(("rep", "shard"), None, None, None),
            P(("rep", "shard"), None, None, None),
            P("shard", None),
            P("shard", None),
        ),
        check_vma=False,
    )
```

profile of v0, /device:TPU:1, one launch (start us, length us, event | category | flops | bytes accessed | tf_op | source)
XLA Modules:
  0.0 457.5 jit_solution(9545784966886984699)
XLA Ops:
  13.2 2.7 copy.111
  16.0 2.4 reshape.136
  18.4 2.8 copy.112
  21.1 2.4 reshape.137
  28.0 2.7 copy.113
  30.7 2.4 reshape.138
  33.1 2.7 copy.114
  35.9 2.4 reshape.139
  38.3 1.4 copy.115
  39.8 2.4 reshape.140
  42.2 2.3 convolution_convert_fusion.1
  44.7 41.5 %all-gather.3.cloned.1.call-done = bf16[5760,640]{1,0:T(8,128)(2,1)} async-done(((bf16[1440,640]{1,0:T(8,128)(2,1)}), bf16[5760,640]{1,0:T(8,128)(2,1)}) %all-gather.3.cloned.1.call-update) | async-done | bytes 7372816 | tf_op jit(solution)/shard_map/all_gather | solution.py:50
  86.3 6.3 %fusion.114 = (bf16[1152,640]{1,0:T(8,128)(2,1)}, bf16[1152,640]{1,0:T(8,128)(2,1)}, bf16[1152,640]{1,0:T(8,128)(2,1)}, bf16[1152,640]{1,0:T(8,128)(2,1)}, bf16[1152,640]{1,0:T(8,128)(2,1)}) fusion(bf16[5760,640]{1,0:T(8,128)(2,1)} %all-gather.3.cloned.1.call-done), kind=kLoop, calls=%fused_computation.307 | loop fusion | bytes 14745600 | tf_op jit(solution)/shard_map/slice | solution.py:62
  92.5 2.5 dot_general.59
  95.1 2.3 fusion.112
  97.4 2.1 convolution_add_fusion.3
  99.6 2.1 convolution_add_fusion.2
  101.7 2.1 convolution_add_fusion.1
  103.8 2.1 convolution_add_fusion
  107.0 2.3 fusion.116
  109.4 1.7 fusion.8
  111.1 3.9 dot_general.61
  115.0 1.8 dot_general.63
  116.8 1.8 dot_general.65
  118.6 2.6 dot_general.67
  121.2 1.6 slice_bitcast_fusion.44
  131.8 10.7 %copy.167 = bf16[1,8,32,640,9]{2,1,4,3,0:T(8,128)(2,1)} copy(bf16[1,8,32,640,9]{3,2,1,4,0:T(8,128)(2,1)S(1)} %fusion.52) | data formatting | bytes 5898240 | tf_op jit(solution)/shard_map/stack | solution.py:17
  142.5 13.5 %reshape.145 = bf16[256,5760]{0,1:T(8,128)(2,1)S(1)} reshape(bf16[1,8,32,640,9]{2,1,4,3,0:T(8,128)(2,1)} %copy.167) | data formatting | bytes 5898240 | tf_op jit(solution)/shard_map/reshape | solution.py:17
  156.0 7.7 %fusion.115 = f32[5760,640]{1,0:T(8,128)} fusion(bf16[256,5760]{0,1:T(8,128)(2,1)S(1)} %reshape.145, bf16[256,640]{1,0:T(8,128)(2,1)S(1)} %bitcast.448), kind=kOutput, calls=%fused_computation.308 | convolution fusion | flops 1887436800 | bytes 18022400 | tf_op jit(solution)/shard_map/dot_general | solution.py:98
  163.8 113.3 %reduce-scatter.3.cloned.1.call-done = f32[1440,640]{1,0:T(8,128)} async-done(((f32[5760,640]{1,0:T(8,128)}), f32[1440,640]{1,0:T(8,128)}) %reduce-scatter.3.cloned.1.call-update) | async-done | bytes 3686416 | tf_op jit(solution)/shard_map/reduce_scatter | solution.py:97
  278.1 167.6 %all-reduce.56.cloned.1.call-done = (f32[1440,640]{1,0:T(8,128)}, f32[160,1280]{1,0:T(8,128)}) async-done(((f32[1440,640]{1,0:T(8,128)}, f32[160,1280]{1,0:T(8,128)}), (f32[1440,640]{1,0:T(8,128)}, f32[160,1280]{1,0:T(8,128)})) %all-reduce.56.cloned.1.call-update) | async-done | bytes 4505616 | tf_op jit(solution)/shard_map/psum | solution.py:106
  445.7 4.3 broadcast_multiply_fusion
  (134 shorter events, 22.8 us)
Async XLA Ops:
  7.2 35.0 %copy-start = (bf16[1,4,16,1280]{3,2,1,0:T(8,128)(2,1)S(1)}, bf16[1,4,16,1280]{3,2,1,0:T(8,128)(2,1)}, u32[]{:S(2)}) copy-start(bf16[1,4,16,1280]{3,2,1,0:T(8,128)(2,1)} %param.8) | copy-start | bytes 491524
  7.2 35.0 %all-gather.5.cloned.1.call-start = ((), (), s32[]{:S(2)}) async-start(), calls=%async_computation.3 | async-start | bytes 2048000 | tf_op jit(solution)/shard_map/all_gather | solution.py:51
  7.9 78.3 %all-gather.3.cloned.1.call-start = ((), (), s32[]{:S(2)}) async-start(), calls=%async_computation.2 | async-start | bytes 9216000 | tf_op jit(solution)/shard_map/all_gather | solution.py:50
  8.7 155.1 %reduce-scatter.5.cloned.1.call-start = ((), (), s32[]{:S(2)}) async-start(), calls=%async_computation.5 | async-start | bytes 4096000 | tf_op jit(solution)/shard_map/reduce_scatter | solution.py:105
  10.6 0.8 copy-start.15
  10.6 1.0 copy-start.16
  11.6 0.8 copy-start.13
  12.4 0.8 copy-start.14
  39.8 4.9 %copy-start.21 = (bf16[1,8,32,640]{3,2,1,0:T(8,128)(2,1)S(1)}, bf16[1,8,32,640]{3,2,1,0:T(8,128)(2,1)}, u32[]{:S(2)}) copy-start(bf16[1,8,32,640]{3,2,1,0:T(8,128)(2,1)} %param.9) | copy-start | bytes 983044
  95.0 2.4 copy-start.17
  95.1 4.5 copy-start.18
  97.4 4.3 copy-start.19
  99.5 4.3 copy-start.20
  101.7 5.0 %copy-start.8 = (bf16[1,8,32,640]{3,2,1,0:T(8,128)(2,1)S(1)}, bf16[1,8,32,640]{3,2,1,0:T(8,128)(2,1)}, u32[]{:S(2)}) copy-start(bf16[1,8,32,640]{3,2,1,0:T(8,128)(2,1)} %param.5) | copy-start | bytes 983044
  105.9 0.8 copy-start.10
  109.3 167.7 %reduce-scatter.3.cloned.1.call-start = ((), (), s32[]{:S(2)}) async-start(), calls=%async_computation.4 | async-start | bytes 18432000 | tf_op jit(solution)/shard_map/reduce_scatter | solution.py:97
  111.1 3.9 copy-start.7
  115.0 1.8 copy-start.6
  121.2 2.2 copy-start.4
  123.4 1.7 copy-start.3
  125.1 1.7 copy-start.2
  128.5 1.0 copy-start.9
  128.5 1.2 copy-start.11
  163.7 113.4 %copy-start.5 = (bf16[640,1280]{1,0:T(8,128)(2,1)S(1)}, bf16[640,1280]{1,0:T(8,128)(2,1)}, u32[]{:S(2)}) copy-start(bf16[640,1280]{1,0:T(8,128)(2,1)} %all-gather.5.cloned.1.call-done) | copy-start | bytes 4915204
  163.7 282.0 %all-reduce.56.cloned.1.call-start = ((), (), s32[]{:S(2)}) async-start(), calls=%async_computation.6 | async-start | bytes 9011200 | tf_op jit(solution)/shard_map/psum | solution.py:106
  445.7 4.3 copy-start.12
  445.7 5.3 %copy-start.1 = (bf16[1,4,16,1280]{3,2,1,0:T(8,128)(2,1)S(1)}, bf16[1,4,16,1280]{3,2,1,0:T(8,128)(2,1)}, u32[]{:S(2)}) copy-start(bf16[1,4,16,1280]{3,2,1,0:T(8,128)(2,1)} %param.8) | copy-start | bytes 491524
Sparse Core Ops, SparseCore 0:
  9.6 22.4 all-gather.4
  33.7 52.5 all-gather.2
  109.5 38.3 reduce-scatter.4
  163.8 113.1 reduce-scatter.2
  281.1 164.5 all-reduce.55
where the time goes:
time: 459 us; the launch traced here: 457 us
  waiting for transfers between devices  324 us (71%)
  local copies, waits for them, and re-layouts  82 us (18%)
  matrix products  28.5 us (6%)
  between operations  14.4 us (3%)
  other arithmetic  8.62 us (2%)
    psum x1, waiting for transfers between devices, on_device(): conv_sum, skip_sum = lax.psum((conv_part, skip_part), 'rep')  168 us
    reduce_scatter x1, waiting for transfers between devices, on_device(): lax.psum_scatter(lax.dot_general(patches, hidden_flat, (((0,), (0,)), (()...  113 us
    all_gather x1, waiting for transfers between devices, on_device(): lax.all_gather(conv_weight, 'shard', axis=0, tiled=True)  41.5 us
    reshape x6, local copies, waits for them, and re-layouts, columns(): jnp.stack(shifts, axis=-1)  25.4 us
    another operation x10, local copies, waits for them, and re-layouts, columns(): jnp.stack(shifts, axis=-1)  24 us
    dot_general x5, local copies, waits for them, and re-layouts, on_device(): lax.dot_general(hidden_flat, rows_block, (((1,), (1,)), ((), ())), prefer...  12.6 us
    unnamed x87, local copies, waits for them, and re-layouts  11.5 us
    dot_general x5, matrix products, on_device(): jnp.dot(patches, filters_all[first_chan * 9:(first_chan + step_chans) * 9...  10.7 us
  transfers between devices with their start and end apart: 5, of which 3 were waited for; matrix products, arithmetic and copies ran while one was open for 19% of the time, Pallas kernels for 0%

commit v1 on v0

v1 whole, which is shorter than its diff:
```python
import functools
import math

import jax
import jax.numpy as jnp
from jax import lax
from jax.experimental import pallas as pl
from jax.experimental.pallas import tpu as pltpu
from jax.sharding import PartitionSpec as P

BF = jnp.bfloat16
F32 = jnp.float32
VMEM_LIMIT = 48 << 20
LANES = 128


def dot(a, b, dims):
    return lax.dot_general(a, b, (dims, ((), ())), preferred_element_type=F32)


def call(body, outs, scratch, flops, moved, *args, smem=()):
    specs = [
        pl.BlockSpec(memory_space=pltpu.SMEM if i in smem else pltpu.VMEM)
        for i in range(len(args))
    ]
    return pl.pallas_call(
        body,
        out_shape=outs,
        in_specs=specs,
        out_specs=jax.tree.map(lambda _: pl.BlockSpec(memory_space=pltpu.VMEM), outs),
        scratch_shapes=scratch,
        compiler_params=pltpu.CompilerParams(vmem_limit_bytes=VMEM_LIMIT),
        cost_estimate=pl.CostEstimate(flops=flops, bytes_accessed=moved, transcendentals=0),
    )(*args)


def shape(dims, kind):
    return jax.ShapeDtypeStruct(dims, kind)


def tap_major(conv_weight):
    rows, chans = conv_weight.shape
    own = rows // 9

    def body(w_ref, o_ref, wide):
        for k in range(chans // LANES):
            cols = slice(k * LANES, (k + 1) * LANES)
            wide[k] = w_ref[:, cols].astype(F32)
            for t in range(9):
                o_ref[t, :, cols] = wide[k, pl.ds(t, own, stride=9), :].astype(BF)

    return call(
        body,
        shape((9, own, chans), BF),
        [pltpu.VMEM((chans // LANES, rows, LANES), F32)],
        0,
        4 * rows * chans,
        conv_weight,
    )


def column_mask(pixels, width, own, dx):
    x = lax.broadcasted_iota(jnp.int32, (pixels, own), 0) % width
    return x >= 1 if dx == 0 else x <= width - 2


def forward(own_images, w_tap, height, width):
    number, pixels, own = own_images.shape
    chans = w_tap.shape[2]

    def body(img_ref, w_ref, o_ref, s_ref):
        for m in range(number):
            v = img_ref[m].astype(F32)
            act = (v / (1.0 + jnp.exp(-v))).astype(BF).astype(F32)
            for dx in range(3):
                moved = act
                if dx != 1:
                    moved = pltpu.roll(act, (1 - dx) % pixels, 0)
                    moved = jnp.where(column_mask(pixels, width, own, dx), moved, 0.0)
                s_ref[dx, m, 1 : height + 1] = moved.astype(BF).reshape(height, width, own)
                s_ref[dx, m, 0] = jnp.zeros((width, own), BF)
                s_ref[dx, m, height + 1] = jnp.zeros((width, own), BF)
        for m in range(number):
            acc = jnp.zeros((pixels, chans), F32)
            for dy in range(3):
                for dx in range(3):
                    slab = s_ref[dx, m, dy : dy + height].reshape(pixels, own)
                    acc = acc + dot(slab, w_ref[3 * dy + dx], ((1,), (0,)))
            o_ref[m] = acc

    return call(
        body,
        [shape((number, pixels, chans), F32), shape((3, number, height + 2, width, own), BF)],
        [],
        2 * 9 * number * pixels * own * chans,
        number * pixels * chans * 4 + 9 * own * chans * 2,
        own_images,
        w_tap,
    )


def filter_grad(shifted, hidden_grad, total_rows):
    _, number, padded, width, own = shifted.shape
    height = padded - 2
    pixels = height * width
    chans = hidden_grad.shape[2]

    def body(s_ref, h_ref, o_ref):
        hid = h_ref[...].reshape(number * pixels, chans)
        for dy in range(3):
            for dx in range(3):
                t = 3 * dy + dx
                slab = s_ref[dx, :, dy : dy + height].reshape(number * pixels, own)
                o_ref[t * own : (t + 1) * own] = dot(slab, hid, ((0,), (0,)))
        if total_rows > 9 * own:
            o_ref[9 * own :] = jnp.zeros((total_rows - 9 * own, chans), F32)

    return call(
        body,
        shape((total_rows, chans), F32),
        [],
        2 * 9 * number * pixels * own * chans,
        total_rows * chans * 4 + number * pixels * chans * 2,
        shifted,
        hidden_grad,
    )


def image_grad(hidden_grad, own_grad, own_images, w_tap, height, width):
    number, pixels, own = own_images.shape
    chans = w_tap.shape[2]

    def body(h_ref, g_ref, img_ref, w_ref, o_ref, acc):
        for m in range(number):
            acc[...] = jnp.zeros_like(acc)
            hid = h_ref[m]
            for dy in range(3):
                for dx in range(3):
                    part = dot(hid, w_ref[3 * dy + dx], ((1,), (1,)))
                    acc[dx, dy : dy + height] += part.reshape(height, width, own)
            side = acc[1, 1 : height + 1].reshape(pixels, own)
            for dx in (0, 2):
                part = acc[dx, 1 : height + 1].reshape(pixels, own)
                part = pltpu.roll(part, (dx - 1) % pixels, 0)
                side = side + jnp.where(column_mask(pixels, width, own, 2 - dx), part, 0.0)
            v = img_ref[m].astype(F32)
            sig = 1.0 / (1.0 + jnp.exp(-v))
            slope = sig * (1.0 + v * (1.0 - sig))
            o_ref[m] = (g_ref[m].astype(F32) + slope * side).astype(BF)

    return call(
        body,
        shape((number, pixels, own), BF),
        [pltpu.VMEM((3, height + 2, width, own), F32)],
        2 * 9 * number * pixels * own * chans,
        number * pixels * chans * 2 + 9 * own * chans * 2,
        hidden_grad,
        own_grad,
        own_images,
        w_tap,
    )


def pick(pixels, width):
    few = pixels // 4
    row = lax.broadcasted_iota(jnp.int32, (few, pixels), 0)
    col = lax.broadcasted_iota(jnp.int32, (few, pixels), 1)
    half = width // 2
    return (col == (row // half) * (2 * width) + (row % half) * 2).astype(BF)


def add_spread(hidden_cot, back_sub, me, width):
    number, pixels, chans = hidden_cot.shape
    few, own = back_sub.shape[2:]

    def body(me_ref, c_ref, b_ref, o_ref):
        here = me_ref[0]
        one_hot = pick(pixels, width)
        for m in range(number):
            for a in range(number):
                j = here ^ a
                spread = dot(one_hot, b_ref[j, m ^ j], ((0,), (0,)))
                cols = slice(a * own, (a + 1) * own)
                o_ref[m, :, cols] = (c_ref[m, :, cols].astype(F32) + spread).astype(BF)

    return call(
        body,
        shape((number, pixels, chans), BF),
        [],
        2 * number * pixels * few * chans,
        number * pixels * chans * 4,
        me,
        hidden_cot,
        back_sub,
        smem=(0,),
    )


def place_grad(first, second, where, own, scale):
    ranks, rows_a, chans = first.shape
    rows_b = second.shape[1]
    chunk = rows_a + rows_b

    def body(w_ref, a_ref, b_ref, o_ref, wide):
        for c in range(ranks):
            for ref, k, low, rows in ((a_ref, 0, 0, rows_a), (b_ref, 1, rows_a, rows_b)):
                if rows == 0:
                    continue
                start = c * chunk + low
                at = w_ref[k * ranks + c]
                for t in range(9):
                    lo, hi = max(start, t * own), min(start + rows, (t + 1) * own)
                    if lo < hi:
                        piece = ref[at, lo - start : hi - start, :].astype(F32) * scale
                        strided = pl.ds((lo - t * own) * 9 + t, hi - lo, stride=9)
                        for k in range(chans // LANES):
                            wide[k, strided, :] = piece[:, k * LANES : (k + 1) * LANES]
        for k in range(chans // LANES):
            o_ref[:, k * LANES : (k + 1) * LANES] = wide[k]

    return call(
        body,
        shape((9 * own, chans), F32),
        [pltpu.VMEM((chans // LANES, 9 * own, LANES), F32)],
        0,
        9 * own * chans * 6,
        where,
        first,
        second,
        smem=(0,),
    )


def flip(value, axis, bit):
    return lax.ppermute(value, axis, [(i, i ^ bit) for i in range(lax.axis_size(axis))])


def high_bits(count):
    return [1 << k for k in reversed(range(count.bit_length() - 1))]


def gather(value, axis):
    found = {0: value}
    for bit in high_bits(lax.axis_size(axis)):
        for j, held in list(found.items()):
            found[j ^ bit] = flip(held, axis, bit)
    return jnp.stack([found[j] for j in range(len(found))])


def exchange(blocks, axis, me):
    got = []
    for j in range(lax.axis_size(axis)):
        mine = lax.dynamic_index_in_dim(blocks, me ^ j, 0, keepdims=False)
        got.append(flip(mine, axis, j) if j else mine)
    return jnp.stack(got)


def sum_scatter(parts, axis):
    held = {j: parts[j] for j in range(lax.axis_size(axis))}
    for bit in reversed(high_bits(lax.axis_size(axis))):
        keep = [j for j in held if not j & bit]
        send = jnp.stack([held[j ^ bit].astype(BF) for j in keep])
        got = flip(send, axis, bit).astype(F32)
        held = {j: held[j] + got[n] for n, j in enumerate(keep)}
    return held[0]


def sum_everywhere(parts, axis, me, bits):
    count = lax.axis_size(axis)
    depth = count.bit_length() - 1
    held = parts.reshape((2,) * depth + parts.shape[1:])
    left = high_bits(count)
    for bit in bits:
        at = left.index(bit)
        mine = (me // bit) % 2
        send = lax.dynamic_index_in_dim(held, 1 - mine, at, keepdims=False).astype(BF)
        keep = lax.dynamic_index_in_dim(held, mine, at, keepdims=False)
        held = keep + flip(send, axis, bit).astype(F32)
        left.remove(bit)
    done = held.astype(BF)[None]
    order = [0]
    for bit in reversed(bits):
        done = jnp.concatenate([done, flip(done, axis, bit)])
        order = order + [j ^ bit for j in order]
    place = [order.index(j) for j in range(count)]
    where = jnp.asarray(place, jnp.int32)[jnp.arange(count, dtype=jnp.int32) ^ me]
    return done, where


def bit_orders(count):
    up = list(reversed(high_bits(count)))
    return up, up[1::-1] + up[2:]


def round_up(value, step):
    return -(-value // step) * step


def on_device(images, conv_weight, skip_weight, cotangent, hidden_cot):
    _, height, width, chans = images.shape
    own = skip_weight.shape[0]
    wide = skip_weight.shape[1]
    pixels, few = height * width, (height // 2) * (width // 2)
    group, ranks = lax.axis_size("shard"), lax.axis_size("rep")
    me = lax.axis_index("shard").astype(jnp.int32)
    rep = lax.axis_index("rep").astype(jnp.int32)
    me_ref = me.reshape(1)
    source = images.reshape(pixels, chans)

    cots = gather(cotangent.reshape(few, wide), "shard").reshape(group * few, wide)
    blocks = source.reshape(pixels, group, own).transpose(1, 0, 2)
    own_images = exchange(blocks, "shard", me)
    hid_cots = gather(hidden_cot.reshape(pixels, chans), "shard")
    w_tap = tap_major(conv_weight)

    back = dot(cots, skip_weight, ((1,), (1,))).astype(BF)
    backs = gather(back.reshape(group, few, own), "shard")
    hidden_grad = add_spread(hid_cots, backs, me_ref, width)

    partial, shifted = forward(own_images, w_tap, height, width)
    hidden = (source.astype(F32) + sum_scatter(partial, "shard")).astype(BF)

    rows = 9 * own
    chunk = round_up(-(-rows // ranks), 8)
    term = filter_grad(shifted, hidden_grad, chunk * ranks).reshape(ranks, chunk, chans)
    cut = round_up(chunk // 2, 8)
    order_a, order_b = bit_orders(ranks)
    sum_a, where_a = sum_everywhere(term[:, :cut], "rep", rep, order_a)
    sum_b, where_b = sum_everywhere(term[:, cut:], "rep", rep, order_b)
    factor = 1.0 / math.sqrt(ranks * group * few)
    conv_grad = place_grad(sum_a, sum_b, jnp.concatenate([where_a, where_b]), own, factor)

    sub = hidden.reshape(height // 2, 2, width // 2, 2, chans)[:, 0, :, 0].reshape(few, chans)
    sub_blocks = sub.reshape(few, group, own).transpose(1, 0, 2)
    own_subs = exchange(sub_blocks, "shard", me).reshape(group * few, own)
    skip_term = dot(own_subs, cots, ((0,), (0,)))
    halves = 2
    split = skip_term.reshape(ranks // halves, -1, halves, wide // halves).transpose(0, 2, 1, 3)
    split = split.reshape(ranks, -1, wide // halves)
    skip_sum, where_s = sum_everywhere(split, "rep", rep, order_a)
    skip_sum = skip_sum[where_s].reshape(ranks // halves, halves, -1, wide // halves)
    skip_grad = skip_sum.transpose(0, 2, 1, 3).reshape(own, wide).astype(F32) * factor

    skips = gather(skip_weight, "shard")
    skips = skips[jnp.arange(group, dtype=jnp.int32) ^ me].reshape(chans, wide)
    projected = dot(sub, skips, ((1,), (0,))).astype(BF).reshape(cotangent.shape)

    own_grad = lax.dynamic_slice_in_dim(hidden_grad, me * own, own, axis=2)
    own_input = image_grad(hidden_grad, own_grad, own_images, w_tap, height, width)
    got = [own_input[0]] + [flip(own_input[j], "shard", j) for j in range(1, group)]
    got = jnp.stack(got)[jnp.arange(group, dtype=jnp.int32) ^ me]
    input_grad = got.transpose(1, 0, 2).reshape(images.shape)

    return hidden.reshape(images.shape), projected, input_grad, conv_grad, skip_grad


def solution(mesh):
    placed = (
        P(("rep", "shard"), None, None, None),
        P("shard", None),
        P("shard", None),
        P(("rep", "shard"), None, None, None),
        P(("rep", "shard"), None, None, None),
    )
    return jax.shard_map(
        on_device,
        mesh=mesh,
        in_specs=placed,
        out_specs=(
            P(("rep", "shard"), None, None, None),
            P(("rep", "shard"), None, None, None),
            P(("rep", "shard"), None, None, None),
            P("shard", None),
            P("shard", None),
        ),
        check_vma=False,
    )
```

time: 459 us -> 153 us (0.33)
  the two profiles are of different devices: /device:TPU:1 before, /device:TPU:0 now
where the time goes in v1:
time: 153 us; the launch traced here: 152 us
  waiting for transfers between devices  45.8 us (30%)
  starting transfers between devices  39.9 us (26%)
  local copies, waits for them, and re-layouts  23.1 us (15%)
  other arithmetic  20.6 us (13%)
  Pallas kernels  18.8 us (12%)
  matrix products  2.78 us (2%)
    ppermute x41, waiting for transfers between devices, flip(): lax.ppermute(value, axis, [(i, i ^ bit) for i in range(lax.axis_size(axis...  45.8 us
    ppermute x41, starting transfers between devices, flip(): lax.ppermute(value, axis, [(i, i ^ bit) for i in range(lax.axis_size(axis...  39.9 us
    pallas_call x6, Pallas kernels, call(): pl.pallas_call(body, out_shape=outs, in_specs=specs, out_specs=jax.tree.m...  18.8 us
    unnamed x34, local copies, waits for them, and re-layouts  4.54 us
    another operation x4, other arithmetic, gather(): return jnp.stack([found[j] for j in range(len(found))])  4.16 us
  transfers between devices with their start and end apart: 41, of which 17 were waited for; matrix products, arithmetic and copies ran while one was open for 26% of the time, Pallas kernels for 10%

profile of v1, /device:TPU:0, one launch (start us, length us, event | category | flops | bytes accessed | tf_op | source)
XLA Modules:
  0.0 152.1 jit_solution(15707274361108214756)
XLA Ops:
  3.2 2.4 %collective-permute-start.2 = (bf16[256,160]{1,0:T(8,128)(2,1)S(1)}, bf16[256,160]{1,0:T(8,128)(2,1)S(1)}, u32[]{:S(2)}, u32[]{:S(2)}) collective-permute-start(bf16[256,160]{1,0:T(8,128)(2,1)S(1)} %bitcast.196), channel_id=1, source_target_pairs={{0,3},{1,2},{2,1},{3,0},{4,7},{5,6},{6,5},{7,4},{8,11},{9,10},{10,... | collective-permute-start | bytes 245768 | tf_op jit(solution)/shard_map/ppermute | solution.py:235
  6.5 1.7 %collective-permute-start.9 = (bf16[256,640]{1,0:T(8,128)(2,1)}, bf16[256,640]{1,0:T(8,128)(2,1)}, u32[]{:S(2)}, u32[]{:S(2)}) collective-permute-start(bf16[256,640]{1,0:T(8,128)(2,1)} %bitcast.20), channel_id=1, source_target_pairs={{0,2},{1,3},{2,0},{3,1},{4,6},{5,7},{6,4},{7,5},{8,10},{9,11},{10,... | collective-permute-start | bytes 983048 | tf_op jit(solution)/shard_map/ppermute | solution.py:235
  13.8 1.7 %collective-permute-start.6 = (bf16[160,1280]{1,0:T(8,128)(2,1)}, bf16[160,1280]{1,0:T(8,128)(2,1)}, u32[]{:S(2)}, u32[]{:S(2)}) collective-permute-start(bf16[160,1280]{1,0:T(8,128)(2,1)} %param.10), channel_id=1, source_target_pairs={{0,2},{1,3},{2,0},{3,1},{4,6},{5,7},{6,4},{7,5},{8,10},{9,11},{10,... | collective-permute-start | bytes 1228808 | tf_op jit(solution)/shard_map/ppermute | solution.py:235
  16.6 7.1 %collective-permute-done.12 = bf16[64,1280]{1,0:T(8,128)(2,1)S(1)} collective-permute-done((bf16[64,1280]{1,0:T(8,128)(2,1)S(1)}, bf16[64,1280]{1,0:T(8,128)(2,1)S(1)}, u32[]{:S(2)}, u32[]{:S(2)}) %collective-permute-start.12) | collective-permute-done | bytes 163872 | tf_op jit(solution)/shard_map/ppermute | solution.py:235
  25.2 5.5 %shard_map.120 = (f32[4,256,640]{2,1,0:T(8,128)}, bf16[3,4,10,32,160]{4,3,2,1,0:T(8,128)(2,1)S(1)}) custom-call(bf16[4,256,160]{2,1,0:T(8,128)(2,1)S(1)} %pad_maximum_fusion.6.img_ref, bf16[9,160,640]{2,1,0:T(8,128)(2,1)S(1)} %copy-done.2), custom_call_target="tpu_custom_call" | custom-call | flops 1887436800 | bytes 4464640 | tf_op jit(solution)/shard_map/pallas_call | solution.py:26
  30.7 3.0 %convert.5 = bf16[4,256,640]{2,1,0:T(8,128)(2,1)} convert(f32[4,256,640]{2,1,0:T(8,128)} %get-tuple-element.7) | non-fusion elementwise | flops 655360 | bytes 3932160 | tf_op jit(solution)/shard_map/convert.2
  35.2 1.8 %collective-permute-start.15 = (bf16[4,64,160]{2,1,0:T(8,128)(2,1)S(1)}, bf16[4,64,160]{2,1,0:T(8,128)(2,1)S(1)}, u32[]{:S(2)}, u32[]{:S(2)}) collective-permute-start(bf16[4,64,160]{2,1,0:T(8,128)(2,1)S(1)} %bitcast.180), channel_id=1, source_target_pairs={{0,2},{1,3},{2,0},{3,1},{4,6},{5,7},{6,4},{7,5},{8,10},{9,11},{10,... | collective-permute-start | bytes 245768 | tf_op jit(solution)/shard_map/ppermute | solution.py:235
  38.8 2.5 %collective-permute-done.15 = bf16[4,64,160]{2,1,0:T(8,128)(2,1)S(1)} collective-permute-done((bf16[4,64,160]{2,1,0:T(8,128)(2,1)S(1)}, bf16[4,64,160]{2,1,0:T(8,128)(2,1)S(1)}, u32[]{:S(2)}, u32[]{:S(2)}) %collective-permute-start.15) | collective-permute-done | bytes 81952 | tf_op jit(solution)/shard_map/ppermute | solution.py:235
  47.9 4.3 %shard_map.123 = f32[1472,640]{1,0:T(8,128)} custom-call(bf16[3,4,10,32,160]{4,3,2,1,0:T(8,128)(2,1)S(1)} %get-tuple-element.8.s_ref, bf16[4,256,640]{2,1,0:T(8,128)(2,1)S(1)} %shard_map.121.h_ref), custom_call_target="tpu_custom_call" | custom-call | flops 1887436800 | bytes 5079040 | tf_op jit(solution)/shard_map/pallas_call | solution.py:26
  52.2 1.7 %slice.74 = f32[8,96,640]{2,1,0:T(8,128)S(1)} slice(f32[8,184,640]{2,1,0:T(8,128)} %bitcast.162), slice={[0:8], [0:96], [0:640]} | slice | bytes 3932160 | tf_op jit(solution)/shard_map/slice | solution.py:328
  53.9 2.5 %slice.75 = f32[8,88,640]{2,1,0:T(8,128)S(1)} slice(f32[8,184,640]{2,1,0:T(8,128)} %bitcast.163), slice={[0:8], [96:184], [0:640]} | slice | bytes 3604480 | tf_op jit(solution)/shard_map/slice | solution.py:329
  56.7 4.3 %shard_map.122 = bf16[4,256,160]{2,1,0:T(8,128)(2,1)S(1)} custom-call(bf16[4,256,640]{2,1,0:T(8,128)(2,1)S(1)} %shard_map.121.h_ref, bf16[4,256,160]{2,1,0:T(8,128)(2,1)S(1)} %constant_dynamic-slice_fusion.8.g_ref, bf16[4,256,160]{2,1,0:T(8,128)(2,1)S(1)} %pad_maximum_fusion.6.img_ref, bf16[9,160,640]{2,1,0:T(8,128)(2,1)S(1)} %copy-done.3), custom_call_target="tpu_custom_call" | custom-call | flops 1887436800 | bytes 3153920 | tf_op jit(solution)/shard_map/pallas_call | solution.py:26
  65.9 2.1 %fusion = bf16[1,256,640]{2,1,0:T(8,128)(2,1)} fusion(f32[2,256,640]{2,1,0:T(8,128)} %convert_element_type.134, f32[4,256,640]{2,1,0:T(8,128)} %get-tuple-element.7), kind=kLoop, calls=%fused_computation.17 | loop fusion | flops 327680 | bytes 1638400 | tf_op jit(solution)/shard_map/convert_element_type | solution.py:262
  68.0 1.7 %collective-permute-start.20 = (bf16[2,2,96,640]{3,2,0,1:T(8,128)(2,1)}, bf16[2,2,96,640]{3,2,0,1:T(8,128)(2,1)}, u32[]{:S(2)}, u32[]{:S(2)}) collective-permute-start(bf16[2,2,96,640]{3,2,0,1:T(8,128)(2,1)} %fusion.2), channel_id=1, source_target_pairs={{0,4},{4,0},{8,12},{12,8},{16,20},{20,16},{24,28},{28,24},{1,5},{5... | collective-permute-start | bytes 1474568 | tf_op jit(solution)/shard_map/ppermute | solution.py:235
  69.8 1.8 %collective-permute-start.26 = (bf16[2,2,88,640]{3,2,0,1:T(8,128)(2,1)}, bf16[2,2,88,640]{3,2,0,1:T(8,128)(2,1)}, u32[]{:S(2)}, u32[]{:S(2)}) collective-permute-start(bf16[2,2,88,640]{3,2,0,1:T(8,128)(2,1)} %fusion.3), channel_id=1, source_target_pairs={{0,8},{4,12},{8,0},{12,4},{16,24},{20,28},{24,16},{28,20},{1,9},{5... | collective-permute-start | bytes 1351688 | tf_op jit(solution)/shard_map/ppermute | solution.py:235
  76.0 1.6 %pad_maximum_fusion = bf16[4,160,1280]{2,1,0:T(8,128)(2,1)S(1)} fusion(bf16[1,160,1280]{2,1,0:T(8,128)(2,1)} %bitcast.14, bf16[1,160,1280]{2,1,0:T(8,128)(2,1)} %bitcast.13, bf16[1,160,1280]{2,1,0:T(8,128)(2,1)} %bitcast.183, bf16[1,160,1280]{2,1,0:T(8,128)(2,1)} %bitcast.11), kind=kLoop, calls=%fused_computation.6 | loop fusion | flops 2457600 | bytes 3276800 | tf_op jit(solution)/shard_map/stack | solution.py:247
  78.2 2.9 %collective-permute-done.4 = bf16[1,256,640]{2,1,0:T(8,128)(2,1)} collective-permute-done((bf16[1,256,640]{2,1,0:T(8,128)(2,1)}, bf16[1,256,640]{2,1,0:T(8,128)(2,1)}, u32[]{:S(2)}, u32[]{:S(2)}) %collective-permute-start.4) | collective-permute-done | bytes 327712 | tf_op jit(solution)/shard_map/ppermute | solution.py:235
  82.9 1.6 %fusion.21 = (bf16[4,16,640]{2,1,0:T(8,128)(2,1)S(1)}, bf16[4,1,16,1,640]{4,3,2,1,0:T(2,128)(2,1)S(1)}) fusion(f32[4,2,16,2,640]{4,3,2,1,0:T(2,128)S(1)} %add.192, f32[4,2,16,2,640]{4,3,2,1,0:T(2,128)} %reshape.177), kind=kLoop, calls=%fused_computation.98 | loop fusion | flops 81920 | bytes 491520 | tf_op jit(solution)/shard_map/slice | solution.py:333
  89.7 1.6 %collective-permute-start.35 = (bf16[2,2,40,640]{3,2,1,0:T(8,128)(2,1)S(1)}, bf16[2,2,40,640]{3,2,1,0:T(8,128)(2,1)S(1)}, u32[]{:S(2)}, u32[]{:S(2)}) collective-permute-start(bf16[2,2,40,640]{3,2,1,0:T(8,128)(2,1)S(1)} %fusion.8), channel_id=1, source_target_pairs={{0,4},{4,0},{8,12},{12,8},{16,20},{20,16},{24,28},{28,24},{1,5},{5... | collective-permute-start | bytes 614408 | tf_op jit(solution)/shard_map/ppermute | solution.py:235
  95.0 2.7 %collective-permute-done.35 = bf16[2,2,40,640]{3,2,1,0:T(8,128)(2,1)S(1)} collective-permute-done((bf16[2,2,40,640]{3,2,1,0:T(8,128)(2,1)S(1)}, bf16[2,2,40,640]{3,2,1,0:T(8,128)(2,1)S(1)}, u32[]{:S(2)}, u32[]{:S(2)}) %collective-permute-start.35) | collective-permute-done | bytes 204832 | tf_op jit(solution)/shard_map/ppermute | solution.py:235
  98.1 3.8 %collective-permute-done.27 = bf16[2,88,640]{2,1,0:T(8,128)(2,1)S(1)} collective-permute-done((bf16[2,88,640]{2,1,0:T(8,128)(2,1)S(1)}, bf16[2,88,640]{2,1,0:T(8,128)(2,1)S(1)}, u32[]{:S(2)}, u32[]{:S(2)}) %collective-permute-start.27) | collective-permute-done | bytes 225312 | tf_op jit(solution)/shard_map/ppermute | solution.py:235
  102.0 2.6 %collective-permute-start.28 = (bf16[88,640]{1,0:T(8,128)(2,1)S(1)}, bf16[88,640]{1,0:T(8,128)(2,1)S(1)}, u32[]{:S(2)}, u32[]{:S(2)}) collective-permute-start(bf16[88,640]{1,0:T(8,128)(2,1)S(1)} %fusion.12), channel_id=1, source_target_pairs={{0,16},{4,20},{8,24},{12,28},{16,0},{20,4},{24,8},{28,12},{1,17},{... | collective-permute-start | bytes 337928 | tf_op jit(solution)/shard_map/ppermute | solution.py:235
  104.7 3.6 %collective-permute-start.37 = (bf16[40,640]{1,0:T(8,128)(2,1)S(1)}, bf16[40,640]{1,0:T(8,128)(2,1)S(1)}, u32[]{:S(2)}, u32[]{:S(2)}) collective-permute-start(bf16[40,640]{1,0:T(8,128)(2,1)S(1)} %fusion.16), channel_id=1, source_target_pairs={{0,16},{4,20},{8,24},{12,28},{16,0},{20,4},{24,8},{28,12},{1,17},{... | collective-permute-start | bytes 153608 | tf_op jit(solution)/shard_map/ppermute | solution.py:235
  108.5 7.3 %collective-permute-done.28 = bf16[88,640]{1,0:T(8,128)(2,1)S(1)} collective-permute-done((bf16[88,640]{1,0:T(8,128)(2,1)S(1)}, bf16[88,640]{1,0:T(8,128)(2,1)S(1)}, u32[]{:S(2)}, u32[]{:S(2)}) %collective-permute-start.28) | collective-permute-done | bytes 112672 | tf_op jit(solution)/shard_map/ppermute | solution.py:235
  116.9 2.0 %collective-permute-start.38 = (bf16[1,40,640]{2,1,0:T(8,128)(2,1)S(1)}, bf16[1,40,640]{2,1,0:T(8,128)(2,1)S(1)}, u32[]{:S(2)}, u32[]{:S(2)}) collective-permute-start(bf16[1,40,640]{2,1,0:T(8,128)(2,1)S(1)} %fusion.17), channel_id=1, source_target_pairs={{0,16},{4,20},{8,24},{12,28},{16,0},{20,4},{24,8},{28,12},{1,17},{... | collective-permute-start | bytes 153608 | tf_op jit(solution)/shard_map/ppermute | solution.py:235
  120.2 6.6 %collective-permute-done.38 = bf16[1,40,640]{2,1,0:T(8,128)(2,1)S(1)} collective-permute-done((bf16[1,40,640]{2,1,0:T(8,128)(2,1)S(1)}, bf16[1,40,640]{2,1,0:T(8,128)(2,1)S(1)}, u32[]{:S(2)}, u32[]{:S(2)}) %collective-permute-start.38) | collective-permute-done | bytes 51232 | tf_op jit(solution)/shard_map/ppermute | solution.py:235
  127.9 1.5 %collective-permute-start.30 = (bf16[2,88,640]{2,1,0:T(8,128)(2,1)S(1)}, bf16[2,88,640]{2,1,0:T(8,128)(2,1)S(1)}, u32[]{:S(2)}, u32[]{:S(2)}) collective-permute-start(bf16[2,88,640]{2,1,0:T(8,128)(2,1)S(1)} %pad_maximum_fusion.13), channel_id=1, source_target_pairs={{0,4},{4,0},{8,12},{12,8},{16,20},{20,16},{24,28},{28,24},{1,5},{5... | collective-permute-start | bytes 675848 | tf_op jit(solution)/shard_map/ppermute | solution.py:235
  129.5 2.1 %collective-permute-start.24 = (bf16[2,96,640]{2,1,0:T(8,128)(2,1)S(1)}, bf16[2,96,640]{2,1,0:T(8,128)(2,1)S(1)}, u32[]{:S(2)}, u32[]{:S(2)}) collective-permute-start(bf16[2,96,640]{2,1,0:T(8,128)(2,1)S(1)} %pad_maximum_fusion.12), channel_id=1, source_target_pairs={{0,8},{4,12},{8,0},{12,4},{16,24},{20,28},{24,16},{28,20},{1,9},{5... | collective-permute-start | bytes 737288 | tf_op jit(solution)/shard_map/ppermute | solution.py:235
  134.2 1.9 %collective-permute-done.30 = bf16[2,88,640]{2,1,0:T(8,128)(2,1)S(1)} collective-permute-done((bf16[2,88,640]{2,1,0:T(8,128)(2,1)S(1)}, bf16[2,88,640]{2,1,0:T(8,128)(2,1)S(1)}, u32[]{:S(2)}, u32[]{:S(2)}) %collective-permute-start.30) | collective-permute-done | bytes 225312 | tf_op jit(solution)/shard_map/ppermute | solution.py:235
  142.0 4.0 %collective-permute-done.31 = bf16[4,88,640]{2,1,0:T(8,128)(2,1)S(1)} collective-permute-done((bf16[4,88,640]{2,1,0:T(8,128)(2,1)}, bf16[4,88,640]{2,1,0:T(8,128)(2,1)S(1)}, u32[]{:S(2)}, u32[]{:S(2)}) %collective-permute-start.31) | collective-permute-done | bytes 450592 | tf_op jit(solution)/shard_map/ppermute | solution.py:235
  146.1 2.9 %collective-permute-done.25 = bf16[4,96,640]{2,1,0:T(8,128)(2,1)S(1)} collective-permute-done((bf16[4,96,640]{2,1,0:T(8,128)(2,1)S(1)}, bf16[4,96,640]{2,1,0:T(8,128)(2,1)S(1)}, u32[]{:S(2)}, u32[]{:S(2)}) %collective-permute-start.25) | collective-permute-done | bytes 491552 | tf_op jit(solution)/shard_map/ppermute | solution.py:235
  149.1 3.0 %shard_map.124 = f32[1440,640]{1,0:T(8,128)} custom-call(s32[16]{0:T(128)S(1)} %pad_add_fusion.w_ref, bf16[8,96,640]{2,1,0:T(8,128)(2,1)S(1)} %pad_maximum_fusion.2.a_ref, bf16[8,88,640]{2,1,0:T(8,128)(2,1)S(1)} %pad_maximum_fusion.3.b_ref), custom_call_target="tpu_custom_call" | custom-call | bytes 5529600 | tf_op jit(solution)/shard_map/pallas_call | solution.py:26
  (169 shorter events, 55.1 us)
Async XLA Ops:
  3.2 10.1 %collective-permute-start.2 = (bf16[256,160]{1,0:T(8,128)(2,1)S(1)}, bf16[256,160]{1,0:T(8,128)(2,1)S(1)}, u32[]{:S(2)}, u32[]{:S(2)}) collective-permute-start(bf16[256,160]{1,0:T(8,128)(2,1)S(1)} %bitcast.196), channel_id=1, source_target_pairs={{0,3},{1,2},{2,1},{3,0},{4,7},{5,6},{6,5},{7,4},{8,11},{9,10},{10,... | collective-permute-start | bytes 245768 | tf_op jit(solution)/shard_map/ppermute | solution.py:235
  5.7 7.7 %collective-permute-start.1 = (bf16[256,160]{1,0:T(8,128)(2,1)S(1)}, bf16[256,160]{1,0:T(8,128)(2,1)S(1)}, u32[]{:S(2)}, u32[]{:S(2)}) collective-permute-start(bf16[256,160]{1,0:T(8,128)(2,1)S(1)} %bitcast.195), channel_id=1, source_target_pairs={{0,2},{1,3},{2,0},{3,1},{4,6},{5,7},{6,4},{7,5},{8,10},{9,11},{10,... | collective-permute-start | bytes 245768 | tf_op jit(solution)/shard_map/ppermute | solution.py:235
  6.3 7.5 %collective-permute-start = (bf16[256,160]{1,0:T(8,128)(2,1)S(1)}, bf16[256,160]{1,0:T(8,128)(2,1)}, u32[]{:S(2)}, u32[]{:S(2)}) collective-permute-start(bf16[256,160]{1,0:T(8,128)(2,1)S(1)} %bitcast.194), channel_id=1, source_target_pairs={{0,1},{1,0},{2,3},{3,2},{4,5},{5,4},{6,7},{7,6},{8,9},{9,8},{10,11... | collective-permute-start | bytes 245768 | tf_op jit(solution)/shard_map/ppermute | solution.py:235
  6.5 30.5 %collective-permute-start.9 = (bf16[256,640]{1,0:T(8,128)(2,1)}, bf16[256,640]{1,0:T(8,128)(2,1)}, u32[]{:S(2)}, u32[]{:S(2)}) collective-permute-start(bf16[256,640]{1,0:T(8,128)(2,1)} %bitcast.20), channel_id=1, source_target_pairs={{0,2},{1,3},{2,0},{3,1},{4,6},{5,7},{6,4},{7,5},{8,10},{9,11},{10,... | collective-permute-start | bytes 983048 | tf_op jit(solution)/shard_map/ppermute | solution.py:235
  8.2 15.4 %collective-permute-start.12 = (bf16[64,1280]{1,0:T(8,128)(2,1)S(1)}, bf16[64,1280]{1,0:T(8,128)(2,1)S(1)}, u32[]{:S(2)}, u32[]{:S(2)}) collective-permute-start(bf16[64,1280]{1,0:T(8,128)(2,1)S(1)} %bitcast.188), channel_id=1, source_target_pairs={{0,2},{1,3},{2,0},{3,1},{4,6},{5,7},{6,4},{7,5},{8,10},{9,11},{10,... | collective-permute-start | bytes 491528 | tf_op jit(solution)/shard_map/ppermute | solution.py:235
  13.3 32.0 %collective-permute-start.8 = (bf16[256,640]{1,0:T(8,128)(2,1)}, bf16[256,640]{1,0:T(8,128)(2,1)}, u32[]{:S(2)}, u32[]{:S(2)}) collective-permute-start(bf16[256,640]{1,0:T(8,128)(2,1)} %bitcast.20), channel_id=1, source_target_pairs={{0,1},{1,0},{2,3},{3,2},{4,5},{5,4},{6,7},{7,6},{8,9},{9,8},{10,11... | collective-permute-start | bytes 983048 | tf_op jit(solution)/shard_map/ppermute | solution.py:235
  13.3 20.3 %collective-permute-start.11 = (bf16[64,1280]{1,0:T(8,128)(2,1)S(1)}, bf16[64,1280]{1,0:T(8,128)(2,1)S(1)}, u32[]{:S(2)}, u32[]{:S(2)}) collective-permute-start(bf16[64,1280]{1,0:T(8,128)(2,1)S(1)} %bitcast.189), channel_id=1, source_target_pairs={{0,1},{1,0},{2,3},{3,2},{4,5},{5,4},{6,7},{7,6},{8,9},{9,8},{10,11... | collective-permute-start | bytes 491528 | tf_op jit(solution)/shard_map/ppermute | solution.py:235
  13.8 29.4 %collective-permute-start.6 = (bf16[160,1280]{1,0:T(8,128)(2,1)}, bf16[160,1280]{1,0:T(8,128)(2,1)}, u32[]{:S(2)}, u32[]{:S(2)}) collective-permute-start(bf16[160,1280]{1,0:T(8,128)(2,1)} %param.10), channel_id=1, source_target_pairs={{0,2},{1,3},{2,0},{3,1},{4,6},{5,7},{6,4},{7,5},{8,10},{9,11},{10,... | collective-permute-start | bytes 1228808 | tf_op jit(solution)/shard_map/ppermute | solution.py:235
  23.7 10.0 %collective-permute-start.13 = (bf16[64,1280]{1,0:T(8,128)(2,1)S(1)}, bf16[64,1280]{1,0:T(8,128)(2,1)S(1)}, u32[]{:S(2)}, u32[]{:S(2)}) collective-permute-start(bf16[64,1280]{1,0:T(8,128)(2,1)S(1)} %collective-permute-done.12), channel_id=1, source_target_pairs={{0,1},{1,0},{2,3},{3,2},{4,5},{5,4},{6,7},{7,6},{8,9},{9,8},{10,11... | collective-permute-start | bytes 491528 | tf_op jit(solution)/shard_map/ppermute | solution.py:235
  37.0 8.3 %collective-permute-start.10 = (bf16[256,640]{1,0:T(8,128)(2,1)}, bf16[256,640]{1,0:T(8,128)(2,1)}, u32[]{:S(2)}, u32[]{:S(2)}) collective-permute-start(bf16[256,640]{1,0:T(8,128)(2,1)} %collective-permute-done.9), channel_id=1, source_target_pairs={{0,1},{1,0},{2,3},{3,2},{4,5},{5,4},{6,7},{7,6},{8,9},{9,8},{10,11... | collective-permute-start | bytes 983048 | tf_op jit(solution)/shard_map/ppermute | solution.py:235
  43.2 32.0 %collective-permute-start.5 = (bf16[160,1280]{1,0:T(8,128)(2,1)}, bf16[160,1280]{1,0:T(8,128)(2,1)S(1)}, u32[]{:S(2)}, u32[]{:S(2)}) collective-permute-start(bf16[160,1280]{1,0:T(8,128)(2,1)} %param.10), channel_id=1, source_target_pairs={{0,1},{1,0},{2,3},{3,2},{4,5},{5,4},{6,7},{7,6},{8,9},{9,8},{10,11... | collective-permute-start | bytes 1228808 | tf_op jit(solution)/shard_map/ppermute | solution.py:235
  43.8 20.8 %collective-permute-start.3 = (bf16[2,256,640]{2,1,0:T(8,128)(2,1)}, bf16[2,256,640]{2,1,0:T(8,128)(2,1)S(1)}, u32[]{:S(2)}, u32[]{:S(2)}) collective-permute-start(bf16[2,256,640]{2,1,0:T(8,128)(2,1)} %pad_maximum_fusion.4), channel_id=1, source_target_pairs={{0,1},{1,0},{2,3},{3,2},{4,5},{5,4},{6,7},{7,6},{8,9},{9,8},{10,11... | collective-permute-start | bytes 1966088 | tf_op jit(solution)/shard_map/ppermute | solution.py:235
  43.8 31.4 %collective-permute-start.7 = (bf16[160,1280]{1,0:T(8,128)(2,1)}, bf16[160,1280]{1,0:T(8,128)(2,1)}, u32[]{:S(2)}, u32[]{:S(2)}) collective-permute-start(bf16[160,1280]{1,0:T(8,128)(2,1)} %collective-permute-done.6), channel_id=1, source_target_pairs={{0,1},{1,0},{2,3},{3,2},{4,5},{5,4},{6,7},{7,6},{8,9},{9,8},{10,11... | collective-permute-start | bytes 1228808 | tf_op jit(solution)/shard_map/ppermute | solution.py:235
  62.5 7.3 %collective-permute-start.18 = (bf16[256,160]{1,0:T(8,128)(2,1)S(1)}, bf16[256,160]{1,0:T(8,128)(2,1)S(1)}, u32[]{:S(2)}, u32[]{:S(2)}) collective-permute-start(bf16[256,160]{1,0:T(8,128)(2,1)S(1)} %get-tuple-element.15), channel_id=1, source_target_pairs={{0,2},{1,3},{2,0},{3,1},{4,6},{5,7},{6,4},{7,5},{8,10},{9,11},{10,... | collective-permute-start | bytes 245768 | tf_op jit(solution)/shard_map/ppermute | solution.py:235
  64.6 7.0 %collective-permute-start.17 = (bf16[256,160]{1,0:T(8,128)(2,1)S(1)}, bf16[256,160]{1,0:T(8,128)(2,1)S(1)}, u32[]{:S(2)}, u32[]{:S(2)}) collective-permute-start(bf16[256,160]{1,0:T(8,128)(2,1)S(1)} %get-tuple-element.16), channel_id=1, source_target_pairs={{0,1},{1,0},{2,3},{3,2},{4,5},{5,4},{6,7},{7,6},{8,9},{9,8},{10,11... | collective-permute-start | bytes 245768 | tf_op jit(solution)/shard_map/ppermute | solution.py:235
  68.0 25.4 %collective-permute-start.20 = (bf16[2,2,96,640]{3,2,0,1:T(8,128)(2,1)}, bf16[2,2,96,640]{3,2,0,1:T(8,128)(2,1)}, u32[]{:S(2)}, u32[]{:S(2)}) collective-permute-start(bf16[2,2,96,640]{3,2,0,1:T(8,128)(2,1)} %fusion.2), channel_id=1, source_target_pairs={{0,4},{4,0},{8,12},{12,8},{16,20},{20,16},{24,28},{28,24},{1,5},{5... | collective-permute-start | bytes 1474568 | tf_op jit(solution)/shard_map/ppermute | solution.py:235
  69.8 21.5 %collective-permute-start.26 = (bf16[2,2,88,640]{3,2,0,1:T(8,128)(2,1)}, bf16[2,2,88,640]{3,2,0,1:T(8,128)(2,1)}, u32[]{:S(2)}, u32[]{:S(2)}) collective-permute-start(bf16[2,2,88,640]{3,2,0,1:T(8,128)(2,1)} %fusion.3), channel_id=1, source_target_pairs={{0,8},{4,12},{8,0},{12,4},{16,24},{20,28},{24,16},{28,20},{1,9},{5... | collective-permute-start | bytes 1351688 | tf_op jit(solution)/shard_map/ppermute | solution.py:235
  71.6 9.5 %collective-permute-start.4 = (bf16[1,256,640]{2,1,0:T(8,128)(2,1)}, bf16[1,256,640]{2,1,0:T(8,128)(2,1)}, u32[]{:S(2)}, u32[]{:S(2)}) collective-permute-start(bf16[1,256,640]{2,1,0:T(8,128)(2,1)} %fusion), channel_id=1, source_target_pairs={{0,2},{1,3},{2,0},{3,1},{4,6},{5,7},{6,4},{7,5},{8,10},{9,11},{10,... | collective-permute-start | bytes 983048 | tf_op jit(solution)/shard_map/ppermute | solution.py:235
  89.7 8.0 %collective-permute-start.35 = (bf16[2,2,40,640]{3,2,1,0:T(8,128)(2,1)S(1)}, bf16[2,2,40,640]{3,2,1,0:T(8,128)(2,1)S(1)}, u32[]{:S(2)}, u32[]{:S(2)}) collective-permute-start(bf16[2,2,40,640]{3,2,1,0:T(8,128)(2,1)S(1)} %fusion.8), channel_id=1, source_target_pairs={{0,4},{4,0},{8,12},{12,8},{16,20},{20,16},{24,28},{28,24},{1,5},{5... | collective-permute-start | bytes 614408 | tf_op jit(solution)/shard_map/ppermute | solution.py:235
  92.7 9.2 %collective-permute-start.27 = (bf16[2,88,640]{2,1,0:T(8,128)(2,1)S(1)}, bf16[2,88,640]{2,1,0:T(8,128)(2,1)S(1)}, u32[]{:S(2)}, u32[]{:S(2)}) collective-permute-start(bf16[2,88,640]{2,1,0:T(8,128)(2,1)S(1)} %fusion.6), channel_id=1, source_target_pairs={{0,4},{4,0},{8,12},{12,8},{16,20},{20,16},{24,28},{28,24},{1,5},{5... | collective-permute-start | bytes 675848 | tf_op jit(solution)/shard_map/ppermute | solution.py:235
  94.5 13.8 %collective-permute-start.21 = (bf16[2,96,640]{2,1,0:T(8,128)(2,1)S(1)}, bf16[2,96,640]{2,1,0:T(8,128)(2,1)S(1)}, u32[]{:S(2)}, u32[]{:S(2)}) collective-permute-start(bf16[2,96,640]{2,1,0:T(8,128)(2,1)S(1)} %fusion.4), channel_id=1, source_target_pairs={{0,8},{4,12},{8,0},{12,4},{16,24},{20,28},{24,16},{28,20},{1,9},{5... | collective-permute-start | bytes 737288 | tf_op jit(solution)/shard_map/ppermute | solution.py:235
  102.0 13.8 %collective-permute-start.28 = (bf16[88,640]{1,0:T(8,128)(2,1)S(1)}, bf16[88,640]{1,0:T(8,128)(2,1)S(1)}, u32[]{:S(2)}, u32[]{:S(2)}) collective-permute-start(bf16[88,640]{1,0:T(8,128)(2,1)S(1)} %fusion.12), channel_id=1, source_target_pairs={{0,16},{4,20},{8,24},{12,28},{16,0},{20,4},{24,8},{28,12},{1,17},{... | collective-permute-start | bytes 337928 | tf_op jit(solution)/shard_map/ppermute | solution.py:235
  104.7 12.2 %collective-permute-start.37 = (bf16[40,640]{1,0:T(8,128)(2,1)S(1)}, bf16[40,640]{1,0:T(8,128)(2,1)S(1)}, u32[]{:S(2)}, u32[]{:S(2)}) collective-permute-start(bf16[40,640]{1,0:T(8,128)(2,1)S(1)} %fusion.16), channel_id=1, source_target_pairs={{0,16},{4,20},{8,24},{12,28},{16,0},{20,4},{24,8},{28,12},{1,17},{... | collective-permute-start | bytes 153608 | tf_op jit(solution)/shard_map/ppermute | solution.py:235
  108.4 11.7 %collective-permute-start.22 = (bf16[96,640]{1,0:T(8,128)(2,1)S(1)}, bf16[96,640]{1,0:T(8,128)(2,1)S(1)}, u32[]{:S(2)}, u32[]{:S(2)}) collective-permute-start(bf16[96,640]{1,0:T(8,128)(2,1)S(1)} %fusion.10), channel_id=1, source_target_pairs={{0,16},{4,20},{8,24},{12,28},{16,0},{20,4},{24,8},{28,12},{1,17},{... | collective-permute-start | bytes 368648 | tf_op jit(solution)/shard_map/ppermute | solution.py:235
  115.8 12.1 %collective-permute-start.29 = (bf16[1,88,640]{2,1,0:T(8,128)(2,1)S(1)}, bf16[1,88,640]{2,1,0:T(8,128)(2,1)S(1)}, u32[]{:S(2)}, u32[]{:S(2)}) collective-permute-start(bf16[1,88,640]{2,1,0:T(8,128)(2,1)S(1)} %fusion.13), channel_id=1, source_target_pairs={{0,16},{4,20},{8,24},{12,28},{16,0},{20,4},{24,8},{28,12},{1,17},{... | collective-permute-start | bytes 337928 | tf_op jit(solution)/shard_map/ppermute | solution.py:235
  116.9 9.9 %collective-permute-start.38 = (bf16[1,40,640]{2,1,0:T(8,128)(2,1)S(1)}, bf16[1,40,640]{2,1,0:T(8,128)(2,1)S(1)}, u32[]{:S(2)}, u32[]{:S(2)}) collective-permute-start(bf16[1,40,640]{2,1,0:T(8,128)(2,1)S(1)} %fusion.17), channel_id=1, source_target_pairs={{0,16},{4,20},{8,24},{12,28},{16,0},{20,4},{24,8},{28,12},{1,17},{... | collective-permute-start | bytes 153608 | tf_op jit(solution)/shard_map/ppermute | solution.py:235
  120.1 9.3 %collective-permute-start.23 = (bf16[1,96,640]{2,1,0:T(8,128)(2,1)S(1)}, bf16[1,96,640]{2,1,0:T(8,128)(2,1)S(1)}, u32[]{:S(2)}, u32[]{:S(2)}) collective-permute-start(bf16[1,96,640]{2,1,0:T(8,128)(2,1)S(1)} %fusion.11), channel_id=1, source_target_pairs={{0,16},{4,20},{8,24},{12,28},{16,0},{20,4},{24,8},{28,12},{1,17},{... | collective-permute-start | bytes 368648 | tf_op jit(solution)/shard_map/ppermute | solution.py:235
  127.9 8.2 %collective-permute-start.30 = (bf16[2,88,640]{2,1,0:T(8,128)(2,1)S(1)}, bf16[2,88,640]{2,1,0:T(8,128)(2,1)S(1)}, u32[]{:S(2)}, u32[]{:S(2)}) collective-permute-start(bf16[2,88,640]{2,1,0:T(8,128)(2,1)S(1)} %pad_maximum_fusion.13), channel_id=1, source_target_pairs={{0,4},{4,0},{8,12},{12,8},{16,20},{20,16},{24,28},{28,24},{1,5},{5... | collective-permute-start | bytes 675848 | tf_op jit(solution)/shard_map/ppermute | solution.py:235
  129.5 9.0 %collective-permute-start.24 = (bf16[2,96,640]{2,1,0:T(8,128)(2,1)S(1)}, bf16[2,96,640]{2,1,0:T(8,128)(2,1)S(1)}, u32[]{:S(2)}, u32[]{:S(2)}) collective-permute-start(bf16[2,96,640]{2,1,0:T(8,128)(2,1)S(1)} %pad_maximum_fusion.12), channel_id=1, source_target_pairs={{0,8},{4,12},{8,0},{12,4},{16,24},{20,28},{24,16},{28,20},{1,9},{5... | collective-permute-start | bytes 737288 | tf_op jit(solution)/shard_map/ppermute | solution.py:235
  132.6 7.2 %collective-permute-start.40 = (bf16[4,40,640]{2,1,0:T(8,128)(2,1)S(1)}, bf16[4,40,640]{2,1,0:T(8,128)(2,1)S(1)}, u32[]{:S(2)}, u32[]{:S(2)}) collective-permute-start(bf16[4,40,640]{2,1,0:T(8,128)(2,1)S(1)} %pad_maximum_fusion.14), channel_id=1, source_target_pairs={{0,4},{4,0},{8,12},{12,8},{16,20},{20,16},{24,28},{28,24},{1,5},{5... | collective-permute-start | bytes 614408 | tf_op jit(solution)/shard_map/ppermute | solution.py:235
  136.9 9.1 %collective-permute-start.31 = (bf16[4,88,640]{2,1,0:T(8,128)(2,1)}, bf16[4,88,640]{2,1,0:T(8,128)(2,1)S(1)}, u32[]{:S(2)}, u32[]{:S(2)}) collective-permute-start(bf16[4,88,640]{2,1,0:T(8,128)(2,1)} %pad_maximum_fusion.10), channel_id=1, source_target_pairs={{0,8},{4,12},{8,0},{12,4},{16,24},{20,28},{24,16},{28,20},{1,9},{5... | collective-permute-start | bytes 1351688 | tf_op jit(solution)/shard_map/ppermute | solution.py:235
  138.5 10.5 %collective-permute-start.25 = (bf16[4,96,640]{2,1,0:T(8,128)(2,1)S(1)}, bf16[4,96,640]{2,1,0:T(8,128)(2,1)S(1)}, u32[]{:S(2)}, u32[]{:S(2)}) collective-permute-start(bf16[4,96,640]{2,1,0:T(8,128)(2,1)S(1)} %pad_maximum_fusion.9), channel_id=1, source_target_pairs={{0,4},{4,0},{8,12},{12,8},{16,20},{20,16},{24,28},{28,24},{1,5},{5... | collective-permute-start | bytes 1474568 | tf_op jit(solution)/shard_map/ppermute | solution.py:235
  (23 other events, 134.1 us)

commit v2 on v0

v2 whole, which is shorter than its diff:
```python
import math

import jax
import jax.numpy as jnp
from jax import lax
from jax.experimental import pallas as pl
from jax.experimental.pallas import tpu as pltpu
from jax.sharding import PartitionSpec as P

BF = jnp.bfloat16
F32 = jnp.float32
VMEM_LIMIT = 56 << 20
LANES = 128
BLOCK = 4


def dot(a, b, dims=((1,), (0,))):
    return lax.dot_general(a, b, (dims, ((), ())), preferred_element_type=F32)


NT = ((1,), (1,))
TN = ((0,), (0,))


def call(name, body, outs, scratch, flops, moved, args, scalars=0):
    specs = [
        pl.BlockSpec(memory_space=pltpu.SMEM if i < scalars else pltpu.VMEM)
        for i in range(len(args))
    ]
    return pl.pallas_call(
        body,
        out_shape=outs,
        in_specs=specs,
        out_specs=jax.tree.map(lambda _: pl.BlockSpec(memory_space=pltpu.VMEM), outs),
        scratch_shapes=scratch,
        compiler_params=pltpu.CompilerParams(vmem_limit_bytes=VMEM_LIMIT),
        cost_estimate=pl.CostEstimate(flops=flops, bytes_accessed=moved, transcendentals=0),
        name=name,
    )(*args)


def shape(dims, kind):
    return jax.ShapeDtypeStruct(dims, kind)


def rows_at(start, size, step):
    return pl.ds(pl.multiple_of(start, step), size)


def round_up(value, step):
    return -(-value // step) * step


def turn_filters(conv_weight):
    rows, chans = conv_weight.shape
    own = rows // 9

    def body(w_ref, o_ref, t_ref, wide):
        for k in range(chans // LANES):
            cols = slice(k * LANES, (k + 1) * LANES)
            wide[k] = w_ref[:, cols].astype(F32)
            for t in range(9):
                piece = wide[k, pl.ds(t, own, stride=9), :]
                o_ref[t * own : (t + 1) * own, cols] = piece.astype(BF)
        t_ref[...] = o_ref[...].T

    return call(
        "turn_filters",
        body,
        [shape((rows, chans), BF), shape((chans, rows), BF)],
        [pltpu.VMEM((chans // LANES, rows, LANES), F32)],
        0,
        6 * rows * chans,
        [conv_weight],
    )


def col_sets(chans):
    rest = (chans - BLOCK * LANES) // BLOCK
    return BLOCK * LANES, rest


def turn_images(ids, source, hidden_cot, group, own):
    pixels, chans = source.shape
    base, rest = col_sets(chans)
    cols = LANES + rest

    def body(id_ref, i_ref, h_ref, img_ref, full_ref, set_ref, wide):
        wide[...] = i_ref[...].astype(F32).T
        for j in range(group):
            img_ref[j] = wide[rows_at((id_ref[0] ^ j) * own, own, 8), :].astype(BF)
        wide[...] = h_ref[...].astype(F32).T
        full_ref[...] = wide[...].astype(BF)
        for k in range(BLOCK):
            q = id_ref[1] ^ k
            set_ref[k, :LANES] = wide[rows_at(q * LANES, LANES, 8), :].astype(BF)
            set_ref[k, LANES:] = wide[rows_at(base + q * rest, rest, 8), :].astype(BF)

    return call(
        "turn_images",
        body,
        [
            shape((group, own, pixels), BF),
            shape((chans, pixels), BF),
            shape((BLOCK, cols, pixels), BF),
        ],
        [pltpu.VMEM((chans, pixels), F32)],
        0,
        10 * pixels * chans,
        [ids, source, hidden_cot],
        1,
    )


def activate(own_images):
    group = number = len(own_images)
    own, pixels = own_images[0].shape[1:]

    def body(*refs):
        for m in range(number):
            v = refs[m][0].astype(F32)
            refs[number][m] = (v / (1.0 + jnp.exp(-v))).astype(BF)

    return call(
        "activate",
        body,
        shape((group, own, pixels), BF),
        [],
        0,
        4 * group * own * pixels,
        own_images,
    )


def back_product(ids, cots, skip_weight):
    few, wide_chans = cots[0].shape
    own = skip_weight.shape[0]
    group = len(cots)

    def body(id_ref, s_ref, *refs):
        o_ref, held = refs[group:]
        for j in range(group):
            held[rows_at((id_ref[0] ^ j) * few, few, 16), :] = refs[j][...]
        o_ref[...] = dot(s_ref[...], held[...], NT).astype(BF)

    return call(
        "back_product",
        body,
        shape((own, group * few), BF),
        [pltpu.VMEM((group * few, wide_chans), BF)],
        2 * own * group * few * wide_chans,
        group * few * wide_chans * 2,
        [ids, skip_weight, *cots],
        1,
    )


def back_sets(ids, backs, chans):
    own, few_all = backs[0].shape
    group = len(backs)
    base, rest = col_sets(chans)

    def body(id_ref, *refs):
        full_ref, set_ref, held = refs[group:]
        for j in range(group):
            held[rows_at((id_ref[0] ^ j) * own, own, 8), :] = refs[j][...].astype(F32)
        full_ref[...] = held[...].astype(BF)
        for k in range(BLOCK):
            q = id_ref[1] ^ k
            set_ref[k, :LANES] = held[rows_at(q * LANES, LANES, 8), :].astype(BF)
            set_ref[k, LANES:] = held[rows_at(base + q * rest, rest, 8), :].astype(BF)

    return call(
        "back_sets",
        body,
        [shape((chans, few_all), BF), shape((BLOCK, LANES + rest, few_all), BF)],
        [pltpu.VMEM((chans, few_all), F32)],
        0,
        6 * chans * few_all,
        [ids, *backs],
        1,
    )


def pixel_parts(pixels, width):
    at = lax.broadcasted_iota(jnp.int32, (1, pixels), 1)
    return at // width, at % width


def neighbours(value, pixels, width):
    height = pixels // width
    y, x = pixel_parts(pixels, width)
    for dy in range(3):
        for dx in range(3):
            off = (dy - 1) * width + dx - 1
            if off == 0:
                yield value
                continue
            inside = (y >= 1 - dy) & (y < height + 1 - dy) & (x >= 1 - dx) & (x < width + 1 - dx)
            yield jnp.where(inside, pltpu.roll(value, -off % pixels, 1), 0.0)


def spread_matrix(few_all, few, pixels, width):
    y, x = pixel_parts(pixels, width)
    coarse = (y // 2) * (width // 2) + x // 2
    even = (y % 2 == 0) & (x % 2 == 0)
    row = lax.broadcasted_iota(jnp.int32, (few_all, pixels), 0)
    for d in range(few_all // few):
        yield jnp.where(even & (row == d * few + coarse), 1.0, 0.0).astype(BF)


def forward(act, w_turned, width):
    group, own, pixels = act.shape
    chans, rows = w_turned.shape

    def body(a_ref, w_ref, keep_ref, send_ref, patch):
        def image(m):
            value = a_ref[m].astype(F32)
            for t, moved in enumerate(neighbours(value, pixels, width)):
                patch[t * own : (t + 1) * own] = moved.astype(BF)
            return dot(w_ref[...], patch[...])

        @pl.loop(0, group // 2)
        def _(i):
            send_ref[i] = image(2 * i + 1).astype(BF)
            keep_ref[i] = image(2 * i)

    return call(
        "forward",
        body,
        [
            shape((group // 2, chans, pixels), F32),
            shape((group // 2, chans, pixels), BF),
        ],
        [pltpu.VMEM((rows, pixels), BF)],
        2 * group * pixels * rows * chans,
        group * chans * pixels * 3,
        [act, w_turned],
    )


def filter_grad(ids, acts, coarse, sets, backs, width, few, cut):
    group = len(sets)
    own, pixels = acts[0].shape[2:]
    cols = sets[0].shape[1]
    few_all = backs[0].shape[1]
    rows = 9 * own
    rest = cols - LANES
    part = round_up(-(-rows // BLOCK), 8)
    n_acts = len(acts)

    def body(id_ref, *refs):
        act_refs = refs[:n_acts]
        set_refs = refs[n_acts : n_acts + group]
        back_refs = refs[n_acts + group : n_acts + group + BLOCK]
        a_out, b_out, act_all, back_all, one_hot, hid, patch, total = refs[-8:]
        for ref, (members, first) in zip(act_refs, coarse):
            for n, k in enumerate(members):
                act_all[k, first : first + ref.shape[1]] = ref[n]
        for k in range(BLOCK):
            back_all[k] = back_refs[k][...]
        for d, matrix in enumerate(spread_matrix(few_all, few, pixels, width)):
            one_hot[d] = matrix
        hid[cols:] = jnp.zeros((hid.shape[0] - cols, group * pixels), BF)
        total[...] = jnp.zeros_like(total)

        @pl.loop(0, BLOCK)
        def _(k):
            for j in range(group):
                here = slice(j * pixels, (j + 1) * pixels)
                spread = dot(back_all[k], one_hot[id_ref[0] ^ j])
                hid[:cols, here] = (set_refs[j][k].astype(F32) + spread).astype(BF)
                value = act_all[k, j].astype(F32)
                for t, moved in enumerate(neighbours(value, pixels, width)):
                    patch[t * own : (t + 1) * own, here] = moved.astype(BF)
            total[...] += dot(patch[...], hid[...], NT)

        last = jnp.zeros((part, LANES), F32)
        for i in range(BLOCK):
            size = min(part, rows - i * part)
            piece = total[i * part : i * part + size, LANES:]
            if size < part:
                piece = jnp.concatenate([piece, jnp.zeros((part - size, LANES), F32)])
            last = last + (pltpu.roll(piece, rest * i, 1) if i else piece)
        a_out[...] = total[:cut, :LANES].astype(BF)
        b_out[: rows - cut] = total[cut:, :LANES].astype(BF)
        b_out[rows - cut :] = last.astype(BF)

    return call(
        "filter_grad",
        body,
        [shape((cut, LANES), BF), shape((rows + part - cut, LANES), BF)],
        [
            pltpu.VMEM((BLOCK, group, own, pixels), BF),
            pltpu.VMEM((BLOCK, cols, few_all), BF),
            pltpu.VMEM((group, few_all, pixels), BF),
            pltpu.VMEM((2 * LANES, group * pixels), BF),
            pltpu.VMEM((rows, group * pixels), BF),
            pltpu.VMEM((rows, 2 * LANES), F32),
        ],
        2 * BLOCK * group * pixels * rows * cols,
        BLOCK * group * pixels * (own + cols) * 2,
        [ids, *acts, *sets, *backs],
        1,
    )


def place_grad(ids, firsts, seconds, own, chans, scale):
    rows = 9 * own
    part = round_up(-(-rows // BLOCK), 8)
    cut = firsts[0][1].shape[1]
    base, rest = col_sets(chans)
    arrays = [array for _, array in firsts + seconds]

    def body(id_ref, *refs):
        o_ref, wide, last = refs[-3:]
        lane = lax.broadcasted_iota(jnp.int32, (part, LANES), 1) // rest

        def store(where, low, piece):
            high = low + piece.shape[0]
            for t in range(9):
                lo, hi = max(low, t * own), min(high, (t + 1) * own)
                if lo < hi:
                    wide[where, pl.ds((lo - t * own) * 9 + t, hi - lo, stride=9), :] = piece[
                        lo - low : hi - low
                    ]

        last[...] = jnp.zeros_like(last)
        for n, (members, _) in enumerate(firsts + seconds):
            first = n < len(firsts)
            for at, k in enumerate(members):
                q = id_ref[1] ^ k
                if first:
                    store(q, 0, refs[n][at].astype(F32) * scale)
                    continue
                store(q, cut, refs[n][at, : rows - cut, :].astype(F32) * scale)
                share = refs[n][at, rows - cut :, :].astype(F32) * scale
                for i in range(BLOCK):
                    turn = ((q - i + BLOCK) % BLOCK) * rest
                    last[i] += jnp.where(lane == q, pltpu.roll(share, turn, 1), 0.0)
        for i in range(BLOCK):
            store(BLOCK, i * part, last[i, : min(part, rows - i * part), :])
        for k in range(chans // LANES):
            o_ref[:, k * LANES : (k + 1) * LANES] = wide[k]

    return call(
        "place_grad",
        body,
        shape((rows, chans), F32),
        [pltpu.VMEM((chans // LANES, rows, LANES), F32), pltpu.VMEM((BLOCK, part, LANES), F32)],
        0,
        rows * chans * 6,
        [ids, *arrays],
        1,
    )


def finish_hidden(ids, source, held, got, group, width):
    pixels, chans = source.shape
    few, own = pixels // 4, chans // group

    def body(id_ref, s_ref, k_ref, g_ref, o_ref, sub_ref, set_ref, wide):
        total = (k_ref[0] + g_ref[0].astype(F32)).T
        hidden = (s_ref[...].astype(F32) + total).astype(BF)
        o_ref[...] = hidden
        (one_hot,) = spread_matrix(few, few, pixels, width)
        sub = dot(one_hot, hidden)
        sub_ref[...] = sub.astype(BF)
        wide[...] = sub.T
        for j in range(group):
            set_ref[j] = wide[rows_at((id_ref[0] ^ j) * own, own, 8), :].astype(BF)

    return call(
        "finish_hidden",
        body,
        [
            shape((pixels, chans), BF),
            shape((few, chans), BF),
            shape((group, own, few), BF),
        ],
        [pltpu.VMEM((chans, few), F32)],
        2 * few * pixels * chans,
        pixels * chans * 10,
        [ids, source, held, got],
        1,
    )


def skip_grad_term(ids, subs, cots):
    own, few = subs[0].shape
    wide_chans = cots[0].shape[1]
    group = len(subs)
    part = own // BLOCK

    def body(id_ref, *refs):
        o_ref, total = refs[-2:]
        term = dot(refs[0][...], refs[group][...])
        for j in range(1, group):
            term = term + dot(refs[j][...], refs[group + j][...])
        for i in range(BLOCK):
            total[i] = term[i * part : (i + 1) * part]
        for k in range(BLOCK):
            o_ref[k] = total[id_ref[1] ^ k]

    return call(
        "skip_grad_term",
        body,
        shape((BLOCK, part, wide_chans), F32),
        [pltpu.VMEM((BLOCK, part, wide_chans), F32)],
        2 * own * few * group * wide_chans,
        own * wide_chans * 4,
        [ids, *subs, *cots],
        1,
    )


def project(sub_sets, skips):
    group, own, few = sub_sets.shape
    wide_chans = skips[0].shape[1]

    def body(s_ref, *refs):
        total = dot(s_ref[0], refs[0][...], TN)
        for j in range(1, group):
            total = total + dot(s_ref[j], refs[j][...], TN)
        refs[group][...] = total.astype(BF)

    return call(
        "project",
        body,
        shape((few, wide_chans), BF),
        [],
        2 * few * group * own * wide_chans,
        group * own * wide_chans * 2,
        [sub_sets, *skips],
    )


def image_grad(ids, cots, back_full, own_images, w_tap, width, few):
    group = len(cots)
    chans, pixels = cots[0].shape
    rows = w_tap.shape[0]
    own = rows // 9
    height = pixels // width
    few_all = back_full.shape[1]

    def body(id_ref, b_ref, w_ref, *refs):
        cot_refs, img_refs = refs[:group], refs[group : 2 * group]
        o_ref, one_hot, hid, tap = refs[2 * group :]
        y, x = pixel_parts(pixels, width)
        for d, matrix in enumerate(spread_matrix(few_all, few, pixels, width)):
            one_hot[d] = matrix
        for j in range(group):
            spread = dot(b_ref[...], one_hot[id_ref[0] ^ j])
            hid[...] = cot_refs[j][...].astype(F32) + spread
            tap[...] = dot(w_ref[...], hid[...].astype(BF))
            side = tap[4 * own : 5 * own]
            for dy in range(3):
                for dx in range(3):
                    off = (dy - 1) * width + dx - 1
                    if off == 0:
                        continue
                    inside = (y >= dy - 1) & (y < height + dy - 1)
                    inside = inside & (x >= dx - 1) & (x < width + dx - 1)
                    t = 3 * dy + dx
                    moved = pltpu.roll(tap[t * own : (t + 1) * own], off % pixels, 1)
                    side = side + jnp.where(inside, moved, 0.0)
            v = img_refs[j][0].astype(F32)
            sig = 1.0 / (1.0 + jnp.exp(-v))
            slope = sig * (1.0 + v * (1.0 - sig))
            mine = hid[rows_at(id_ref[0] * own, own, 8), :].astype(BF).astype(F32)
            o_ref[j] = (mine + slope * side).astype(BF)

    return call(
        "image_grad",
        body,
        shape((group, own, pixels), BF),
        [
            pltpu.VMEM((group, few_all, pixels), BF),
            pltpu.VMEM((chans, pixels), F32),
            pltpu.VMEM((rows, pixels), F32),
        ],
        2 * group * pixels * rows * chans,
        group * pixels * chans * 2,
        [ids, back_full, w_tap, *cots, *own_images],
        1,
    )


def finish_images(ids, pieces, chans):
    group = len(pieces)
    own, pixels = pieces[0].shape[1:]

    def body(id_ref, *refs):
        o_ref, wide = refs[group:]
        for j in range(group):
            wide[rows_at((id_ref[0] ^ j) * own, own, 8), :] = refs[j][0].astype(F32)
        o_ref[...] = wide[...].T.astype(BF)

    return call(
        "finish_images",
        body,
        shape((pixels, chans), BF),
        [pltpu.VMEM((chans, pixels), F32)],
        0,
        pixels * chans * 4,
        [ids, *pieces],
        1,
    )


def flip(value, axis, bit):
    return lax.ppermute(value, axis, [(i, i ^ bit) for i in range(lax.axis_size(axis))])


def after(value, *others):
    return lax.optimization_barrier((value, *others))[0]


def high_bits(count):
    return [1 << k for k in reversed(range(count.bit_length() - 1))]


def gather(value, axis):
    found = {0: value}
    for bit in high_bits(lax.axis_size(axis)):
        for j, held in list(found.items()):
            found[j ^ bit] = flip(held, axis, bit)
    return [found[j] for j in range(len(found))]


def exchange(blocks, axis, count):
    return [flip(blocks[j : j + 1], axis, j) if j else blocks[:1] for j in range(count)]


def both_orders(first, second):
    pairs = []
    for value, bits in ((first, (1, 2)), (second, (2, 1))):
        pair = jnp.stack([value, flip(value, "rep", bits[0])])
        members = (0, bits[0])
        others = tuple(m ^ bits[1] for m in members)
        pairs.append([(members, pair), (others, flip(pair, "rep", bits[1]))])
    return pairs


def add_beyond_block(value):
    for bit in reversed(high_bits(lax.axis_size("rep"))):
        if bit >= BLOCK:
            got = flip(value, "rep", bit)
            value = (value.astype(F32) + got.astype(F32)).astype(BF)
    return value


def sum_scatter(keep, send):
    bits = list(reversed(high_bits(lax.axis_size("shard"))))
    for bit in bits[:-1]:
        total = keep + flip(send, "shard", bit).astype(F32)
        keep, send = total[0::2], total[1::2].astype(BF)
    return keep, flip(send, "shard", bits[-1])


def on_device(images, conv_weight, skip_weight, cotangent, hidden_cot):
    _, height, width, chans = images.shape
    own, wide = skip_weight.shape
    pixels, few = height * width, (height // 2) * (width // 2)
    group, ranks = lax.axis_size("shard"), lax.axis_size("rep")
    ids = jnp.stack([lax.axis_index("shard"), lax.axis_index("rep") % BLOCK]).astype(jnp.int32)
    source = images.reshape(pixels, chans)

    cots = gather(cotangent.reshape(few, wide), "shard")
    img_sets, cot_full, cot_sets = turn_images(
        ids, source, hidden_cot.reshape(pixels, chans), group, own
    )
    own_images = exchange(img_sets, "shard", group)
    cot_sets = jnp.concatenate(exchange(cot_sets, "rep", BLOCK))
    cot_sets = gather(cot_sets, "shard")
    w_tap, w_turned = turn_filters(conv_weight)
    act = activate(own_images)
    half = group // 2
    act_a, act_b = both_orders(act[:half], act[half:])

    backs = gather(back_product(ids, cots, skip_weight), "shard")
    back_full, back_set = back_sets(ids, backs, chans)
    back_set = [piece[0] for piece in exchange(back_set, "rep", BLOCK)]

    rows = 9 * own
    part = round_up(-(-rows // BLOCK), 8)
    cut = round_up((rows + part) // 2, 8)
    coarse = [(members, 0) for members, _ in act_a] + [(members, half) for members, _ in act_b]
    acts = [array for _, array in act_a + act_b]
    term_a, term_b = filter_grad(ids, acts, coarse, cot_sets, back_set, width, few, cut)
    sum_a, sum_b = both_orders(add_beyond_block(term_a), add_beyond_block(term_b))
    factor = 1.0 / math.sqrt(ranks * group * few)
    conv_grad = place_grad(ids, sum_a, sum_b, own, chans, factor)

    keep, send = forward(after(act, back_set[0]), w_turned, width)
    keep, got = sum_scatter(keep, send)
    hidden, _, sub_sets = finish_hidden(ids, source, keep, got, group, width)

    subs = [piece[0] for piece in exchange(sub_sets, "shard", group)]
    term = skip_grad_term(ids, subs, cots)
    term = term[:2] + flip(term[2:].astype(BF), "rep", 2).astype(F32)
    term = (term[0] + flip(term[1].astype(BF), "rep", 1).astype(F32)).astype(BF)
    term = add_beyond_block(term)[None]
    term = jnp.concatenate([term, flip(term, "rep", 1)])
    term = jnp.concatenate([term, flip(term, "rep", 2)])
    term = term[jnp.arange(BLOCK, dtype=jnp.int32) ^ ids[1]]
    skip_grad = term.reshape(own, wide).astype(F32) * factor

    skips = gather(after(skip_weight, back_full), "shard")
    projected = project(sub_sets, skips).reshape(cotangent.shape)

    cot_all = gather(after(cot_full, back_full), "shard")
    own_input = image_grad(
        ids, cot_all, after(back_full, term_a), own_images, w_tap, width, few
    )
    input_grad = finish_images(ids, exchange(own_input, "shard", group), chans)

    return (
        hidden.reshape(images.shape),
        projected,
        input_grad.reshape(images.shape),
        conv_grad,
        skip_grad,
    )


def solution(mesh):
    placed = (
        P(("rep", "shard"), None, None, None),
        P("shard", None),
        P("shard", None),
        P(("rep", "shard"), None, None, None),
        P(("rep", "shard"), None, None, None),
    )
    return jax.shard_map(
        on_device,
        mesh=mesh,
        in_specs=placed,
        out_specs=(
            P(("rep", "shard"), None, None, None),
            P(("rep", "shard"), None, None, None),
            P(("rep", "shard"), None, None, None),
            P("shard", None),
            P("shard", None),
        ),
        check_vma=False,
    )
```

time: 459 us -> 153 us (0.33)
  the two profiles are of different devices: /device:TPU:1 before, /device:TPU:0 now
where the time goes in v2:
time: 153 us; the launch traced here: 152 us
  Pallas kernels  47.3 us (31%)
  starting transfers between devices  43.7 us (29%)
  waiting for transfers between devices  43.2 us (28%)
  local copies, waits for them, and re-layouts  14.5 us (9%)
  other arithmetic  2.22 us (1%)
    pallas_call x13, Pallas kernels, call(): pl.pallas_call(body, out_shape=outs, in_specs=specs, out_specs=jax.tree.m...  47.3 us
    ppermute x47, starting transfers between devices, flip(): lax.ppermute(value, axis, [(i, i ^ bit) for i in range(lax.axis_size(axis...  43.7 us
    ppermute x47, waiting for transfers between devices, flip(): lax.ppermute(value, axis, [(i, i ^ bit) for i in range(lax.axis_size(axis...  43.2 us
    unnamed x94, local copies, waits for them, and re-layouts  7.48 us
    slice x4, local copies, waits for them, and re-layouts, exchange(): blocks[j:j + 1]  4.43 us
  transfers between devices with their start and end apart: 47, of which 17 were waited for; matrix products, arithmetic and copies ran while one was open for 5% of the time, Pallas kernels for 30%

profile of v2, /device:TPU:0, one launch (start us, length us, event | category | flops | bytes accessed | tf_op | source)
XLA Modules:
  0.0 152.1 jit_solution(14645247311416594231)
XLA Ops:
  0.6 3.0 %collective-permute-start.4 = (bf16[64,1280]{1,0:T(8,128)(2,1)}, bf16[64,1280]{1,0:T(8,128)(2,1)S(1)}, u32[]{:S(2)}, u32[]{:S(2)}) collective-permute-start(bf16[64,1280]{1,0:T(8,128)(2,1)} %bitcast.46), channel_id=1, source_target_pairs={{0,2},{1,3},{2,0},{3,1},{4,6},{5,7},{6,4},{7,5},{8,10},{9,11},{10,... | collective-permute-start | bytes 491528 | tf_op jit(solution)/shard_map/ppermute | solution.py:512
  3.6 4.4 %collective-permute-done.4.refs_2_.refs_6_ = bf16[64,1280]{1,0:T(8,128)(2,1)S(1)} collective-permute-done((bf16[64,1280]{1,0:T(8,128)(2,1)}, bf16[64,1280]{1,0:T(8,128)(2,1)S(1)}, u32[]{:S(2)}, u32[]{:S(2)}) %collective-permute-start.4) | collective-permute-done | bytes 163872 | tf_op jit(solution)/shard_map/ppermute | solution.py:512
  8.7 2.3 %turn_images.1 = (bf16[4,160,256]{2,1,0:T(8,128)(2,1)}, bf16[640,256]{1,0:T(8,128)(2,1)}, bf16[4,160,256]{2,1,0:T(8,128)(2,1)}) custom-call(s32[2]{0:T(128)} %pad_add_fusion.id_ref, bf16[256,640]{1,0:T(8,128)(2,1)} %bitcast.41, bf16[256,640]{1,0:T(8,128)(2,1)} %bitcast.50), custom_call_target="tpu_custom_call" | custom-call | bytes 1638400 | tf_op jit(solution)/shard_map/turn_images/pallas_call | solution.py:30
  12.3 2.3 %back_product.1.refs_0_ = bf16[160,256]{1,0:T(8,128)(2,1)} custom-call(s32[2]{0:T(128)} %pad_add_fusion.id_ref, bf16[160,1280]{1,0:T(8,128)(2,1)} %refs_0_, bf16[64,1280]{1,0:T(8,128)(2,1)} %bitcast.48, bf16[64,1280]{1,0:T(8,128)(2,1)} %copy-done.7, bf16[64,1280]{1,0:T(8,128)(2,1)} %copy-done.6, bf16[64,1280]{1,0:T(8,128)(2,1)} %copy-done.8), custom_call_target="tpu_custom_call" | custom-call | flops 104857600 | bytes 655360 | tf_op jit(solution)/shard_map/back_product/pallas_call | solution.py:30
  14.6 1.7 %collective-permute-start.7 = (bf16[160,256]{1,0:T(8,128)(2,1)}, bf16[160,256]{1,0:T(8,128)(2,1)S(1)}, u32[]{:S(2)}, u32[]{:S(2)}) collective-permute-start(bf16[160,256]{1,0:T(8,128)(2,1)} %back_product.1.refs_0_), channel_id=1, source_target_pairs={{0,2},{1,3},{2,0},{3,1},{4,6},{5,7},{6,4},{7,5},{8,10},{9,11},{10,... | collective-permute-start | bytes 245768 | tf_op jit(solution)/shard_map/ppermute | solution.py:512
  19.7 4.1 %turn_filters.1 = (bf16[1440,640]{1,0:T(8,128)(2,1)}, bf16[640,1440]{1,0:T(8,128)(2,1)}) custom-call(bf16[1440,640]{1,0:T(8,128)(2,1)} %w_ref.1), custom_call_target="tpu_custom_call" | custom-call | bytes 5529600 | tf_op jit(solution)/shard_map/turn_filters/pallas_call | solution.py:30
  23.9 2.8 %collective-permute-start.20 = (bf16[1,160,256]{2,1,0:T(8,128)(2,1)S(1)}, bf16[1,160,256]{2,1,0:T(8,128)(2,1)S(1)}, u32[]{:S(2)}, u32[]{:S(2)}) collective-permute-start(bf16[1,160,256]{2,1,0:T(8,128)(2,1)S(1)} %get-tuple-element.48), channel_id=1, source_target_pairs={{0,12},{4,8},{8,4},{12,0},{16,28},{20,24},{24,20},{28,16},{1,13},{... | collective-permute-start | bytes 245768 | tf_op jit(solution)/shard_map/ppermute | solution.py:512
  27.7 1.9 %activate.1.a_ref = bf16[4,160,256]{2,1,0:T(8,128)(2,1)} custom-call(bf16[1,160,256]{2,1,0:T(8,128)(2,1)} %get-tuple-element.58.refs_0_.refs_4_, bf16[1,160,256]{2,1,0:T(8,128)(2,1)} %copy-done.23, bf16[1,160,256]{2,1,0:T(8,128)(2,1)} %copy-done.24, bf16[1,160,256]{2,1,0:T(8,128)(2,1)} %copy-done.25), custom_call_target="tpu_custom_call" | custom-call | bytes 655360 | tf_op jit(solution)/shard_map/activate/pallas_call | solution.py:30
  30.9 2.0 %back_sets.1 = (bf16[640,256]{1,0:T(8,128)(2,1)}, bf16[4,160,256]{2,1,0:T(8,128)(2,1)}) custom-call(s32[2]{0:T(128)} %pad_add_fusion.id_ref, bf16[160,256]{1,0:T(8,128)(2,1)} %back_product.1.refs_0_, bf16[160,256]{1,0:T(8,128)(2,1)} %copy-done.28, bf16[160,256]{1,0:T(8,128)(2,1)} %copy-done.26, bf16[160,256]{1,0:T(8,128)(2,1)} %copy-done.30), custom_call_target="tpu_custom_call" | custom-call | bytes 983040 | tf_op jit(solution)/shard_map/back_sets/pallas_call | solution.py:30
  34.5 5.6 %forward.1 = (f32[2,640,256]{2,1,0:T(8,128)}, bf16[2,640,256]{2,1,0:T(8,128)(2,1)}) custom-call(bf16[4,160,256]{2,1,0:T(8,128)(2,1)} %activate.1.a_ref, bf16[640,1440]{1,0:T(8,128)(2,1)} %get-tuple-element.25.w_ref), custom_call_target="tpu_custom_call" | custom-call | flops 1887436800 | bytes 1966080 | tf_op jit(solution)/shard_map/forward/pallas_call | solution.py:30
  41.7 1.9 %collective-permute-start.22 = (bf16[4,160,256]{2,1,0:T(8,128)(2,1)S(1)}, bf16[4,160,256]{2,1,0:T(8,128)(2,1)S(1)}, u32[]{:S(2)}, u32[]{:S(2)}) collective-permute-start(bf16[4,160,256]{2,1,0:T(8,128)(2,1)S(1)} %pad_maximum_fusion.5.refs_4_), channel_id=1, source_target_pairs={{0,2},{1,3},{2,0},{3,1},{4,6},{5,7},{6,4},{7,5},{8,10},{9,11},{10,... | collective-permute-start | bytes 983048 | tf_op jit(solution)/shard_map/ppermute | solution.py:512
  48.5 2.1 %collective-permute-done.16 = bf16[2,160,256]{2,1,0:T(8,128)(2,1)S(1)} collective-permute-done((bf16[2,160,256]{2,1,0:T(8,128)(2,1)S(1)}, bf16[2,160,256]{2,1,0:T(8,128)(2,1)S(1)}, u32[]{:S(2)}, u32[]{:S(2)}) %collective-permute-start.16) | collective-permute-done | bytes 163872 | tf_op jit(solution)/shard_map/ppermute | solution.py:512
  54.7 6.8 %collective-permute-done.24 = bf16[1,160,256]{2,1,0:T(8,128)(2,1)S(1)} collective-permute-done((bf16[1,160,256]{2,1,0:T(8,128)(2,1)S(1)}, bf16[1,160,256]{2,1,0:T(8,128)(2,1)S(1)}, u32[]{:S(2)}, u32[]{:S(2)}) %collective-permute-start.24) | collective-permute-done | bytes 81952 | tf_op jit(solution)/shard_map/ppermute | solution.py:512
  61.5 1.7 %collective-permute-start.26 = (bf16[1,160,256]{2,1,0:T(8,128)(2,1)S(1)}, bf16[1,160,256]{2,1,0:T(8,128)(2,1)S(1)}, u32[]{:S(2)}, u32[]{:S(2)}) collective-permute-start(bf16[1,160,256]{2,1,0:T(8,128)(2,1)S(1)} %get-tuple-element.43), channel_id=1, source_target_pairs={{0,12},{4,8},{8,4},{12,0},{16,28},{20,24},{24,20},{28,16},{1,13},{... | collective-permute-start | bytes 245768 | tf_op jit(solution)/shard_map/ppermute | solution.py:512
  63.2 3.7 %collective-permute-done.26 = bf16[1,160,256]{2,1,0:T(8,128)(2,1)S(1)} collective-permute-done((bf16[1,160,256]{2,1,0:T(8,128)(2,1)S(1)}, bf16[1,160,256]{2,1,0:T(8,128)(2,1)S(1)}, u32[]{:S(2)}, u32[]{:S(2)}) %collective-permute-start.26) | collective-permute-done | bytes 81952 | tf_op jit(solution)/shard_map/ppermute | solution.py:512
  66.9 1.9 %collective-permute-start.12 = (bf16[160,1280]{1,0:T(8,128)(2,1)S(1)}, bf16[160,1280]{1,0:T(8,128)(2,1)S(1)}, u32[]{:S(2)}, u32[]{:S(2)}) collective-permute-start(bf16[160,1280]{1,0:T(8,128)(2,1)S(1)} %copy-done.3), channel_id=1, source_target_pairs={{0,2},{1,3},{2,0},{3,1},{4,6},{5,7},{6,4},{7,5},{8,10},{9,11},{10,... | collective-permute-start | bytes 1228808 | tf_op jit(solution)/shard_map/ppermute | solution.py:512
  69.8 8.3 %filter_grad.1 = (bf16[904,128]{1,0:T(8,128)(2,1)}, bf16[896,128]{1,0:T(8,128)(2,1)}) custom-call(s32[2]{0:T(128)} %pad_add_fusion.id_ref, bf16[2,2,160,256]{3,2,1,0:T(8,128)(2,1)} %copy-done.15, bf16[2,2,160,256]{3,2,1,0:T(8,128)(2,1)} %copy-done.40, bf16[2,2,160,256]{3,2,1,0:T(8,128)(2,1)} %copy-done.16, bf16[2,2,160,256]{3,2,1,0:T(8,128)(2,1)} %copy-done.42, ...), custom_call_target="tpu_custom_call" | custom-call | flops 1887436800 | bytes 2621440 | tf_op jit(solution)/shard_map/filter_grad/pallas_call | solution.py:30
  78.1 2.7 %collective-permute-start.36 = (bf16[896,128]{1,0:T(8,128)(2,1)}, bf16[896,128]{1,0:T(8,128)(2,1)S(1)}, u32[]{:S(2)}, u32[]{:S(2)}) collective-permute-start(bf16[896,128]{1,0:T(8,128)(2,1)} %get-tuple-element.38), channel_id=1, source_target_pairs={{0,16},{4,20},{8,24},{12,28},{16,0},{20,4},{24,8},{28,12},{1,17},{... | collective-permute-start | bytes 688136 | tf_op jit(solution)/shard_map/ppermute | solution.py:512
  82.4 2.4 %finish_hidden.1 = (bf16[256,640]{1,0:T(8,128)(2,1)}, bf16[64,640]{1,0:T(8,128)(2,1)}, bf16[4,160,64]{2,1,0:T(8,128)(2,1)}) custom-call(s32[2]{0:T(128)} %pad_add_fusion.id_ref, bf16[256,640]{1,0:T(8,128)(2,1)} %bitcast.42, f32[1,640,256]{2,1,0:T(8,128)} %slice.119.k_ref, bf16[1,640,256]{2,1,0:T(8,128)(2,1)} %copy-done.20), custom_call_target="tpu_custom_call" | custom-call | flops 20971520 | bytes 1638400 | tf_op jit(solution)/shard_map/finish_hidden/pallas_call | solution.py:30
  90.2 2.2 %collective-permute-done.40 = bf16[1,160,64]{2,1,0:T(8,128)(2,1)S(1)} collective-permute-done((bf16[1,160,64]{2,1,0:T(8,128)(2,1)S(1)}, bf16[1,160,64]{2,1,0:T(8,128)(2,1)S(1)}, u32[]{:S(2)}, u32[]{:S(2)}) %collective-permute-start.40) | collective-permute-done | bytes 20512 | tf_op jit(solution)/shard_map/ppermute | solution.py:512
  94.2 2.7 %skip_grad_term.1 = f32[4,40,1280]{2,1,0:T(8,128)} custom-call(s32[2]{0:T(128)} %pad_add_fusion.id_ref, bf16[160,64]{1,0:T(8,128)(2,1)} %get-tuple-element.62.refs_0_, bf16[160,64]{1,0:T(8,128)(2,1)} %bitcast.57, bf16[160,64]{1,0:T(8,128)(2,1)} %bitcast.58, bf16[160,64]{1,0:T(8,128)(2,1)} %bitcast.59, bf16[64,1280]{1,0:T(8,128)(2,1)} %bitcast.49, ...), custom_call_target="tpu_custom_call" | custom-call | flops 104857600 | bytes 819200 | tf_op jit(solution)/shard_map/skip_grad_term/pallas_call | solution.py:30
  97.9 2.4 %collective-permute-done.33 = bf16[904,128]{1,0:T(8,128)(2,1)S(1)} collective-permute-done((bf16[904,128]{1,0:T(8,128)(2,1)S(1)}, bf16[904,128]{1,0:T(8,128)(2,1)S(1)}, u32[]{:S(2)}, u32[]{:S(2)}) %collective-permute-start.33) | collective-permute-done | bytes 231456 | tf_op jit(solution)/shard_map/ppermute | solution.py:512
  100.3 2.4 %collective-permute-start.42 = (bf16[2,40,1280]{2,1,0:T(8,128)(2,1)S(1)}, bf16[2,40,1280]{2,1,0:T(8,128)(2,1)S(1)}, u32[]{:S(2)}, u32[]{:S(2)}) collective-permute-start(bf16[2,40,1280]{2,1,0:T(8,128)(2,1)S(1)} %slice.147), channel_id=1, source_target_pairs={{0,8},{4,12},{8,0},{12,4},{16,24},{20,28},{24,16},{28,20},{1,9},{5... | collective-permute-start | bytes 614408 | tf_op jit(solution)/shard_map/ppermute | solution.py:512
  104.3 6.6 %image_grad.1 = bf16[4,160,256]{2,1,0:T(8,128)(2,1)} custom-call(s32[2]{0:T(128)} %pad_add_fusion.id_ref, bf16[640,256]{1,0:T(8,128)(2,1)} %get-tuple-element.34.b_ref, bf16[1440,640]{1,0:T(8,128)(2,1)} %get-tuple-element.35.w_ref, bf16[640,256]{1,0:T(8,128)(2,1)} %get-tuple-element.37.refs_0_, bf16[640,256]{1,0:T(8,128)(2,1)} %copy-done.39, ...), custom_call_target="tpu_custom_call" | custom-call | flops 1887436800 | bytes 1310720 | tf_op jit(solution)/shard_map/image_grad/pallas_call | solution.py:30
  112.5 3.2 %collective-permute-done.43 = bf16[40,1280]{1,0:T(8,128)(2,1)S(1)} collective-permute-done((bf16[40,1280]{1,0:T(8,128)(2,1)S(1)}, bf16[40,1280]{1,0:T(8,128)(2,1)S(1)}, u32[]{:S(2)}, u32[]{:S(2)}) %collective-permute-start.43) | collective-permute-done | bytes 102432 | tf_op jit(solution)/shard_map/ppermute | solution.py:512
  115.8 4.3 %collective-permute-start.44 = (bf16[40,1280]{1,0:T(8,128)(2,1)S(1)}, bf16[40,1280]{1,0:T(8,128)(2,1)S(1)}, u32[]{:S(2)}, u32[]{:S(2)}) collective-permute-start(bf16[40,1280]{1,0:T(8,128)(2,1)S(1)} %fusion.1), channel_id=1, source_target_pairs={{0,16},{4,20},{8,24},{12,28},{16,0},{20,4},{24,8},{28,12},{1,17},{... | collective-permute-start | bytes 307208 | tf_op jit(solution)/shard_map/ppermute | solution.py:512
  120.2 5.7 %collective-permute-done.44 = bf16[40,1280]{1,0:T(8,128)(2,1)S(1)} collective-permute-done((bf16[40,1280]{1,0:T(8,128)(2,1)S(1)}, bf16[40,1280]{1,0:T(8,128)(2,1)S(1)}, u32[]{:S(2)}, u32[]{:S(2)}) %collective-permute-start.44) | collective-permute-done | bytes 102432 | tf_op jit(solution)/shard_map/ppermute | solution.py:512
  127.9 2.4 %collective-permute-done.31.refs_2_ = bf16[1,160,256]{2,1,0:T(8,128)(2,1)S(1)} collective-permute-done((bf16[1,160,256]{2,1,0:T(8,128)(2,1)S(1)}, bf16[1,160,256]{2,1,0:T(8,128)(2,1)S(1)}, u32[]{:S(2)}, u32[]{:S(2)}) %collective-permute-start.31) | collective-permute-done | bytes 81952 | tf_op jit(solution)/shard_map/ppermute | solution.py:512
  133.8 2.0 %finish_images.1 = bf16[256,640]{1,0:T(8,128)(2,1)} custom-call(s32[2]{0:T(128)} %pad_add_fusion.id_ref, bf16[1,160,256]{2,1,0:T(8,128)(2,1)} %get-tuple-element.42.refs_0_, bf16[1,160,256]{2,1,0:T(8,128)(2,1)} %copy-done.27, bf16[1,160,256]{2,1,0:T(8,128)(2,1)} %copy-done.29, bf16[1,160,256]{2,1,0:T(8,128)(2,1)} %copy-done.31), custom_call_target="tpu_custom_call" | custom-call | bytes 655360 | tf_op jit(solution)/shard_map/finish_images/pallas_call | solution.py:30
  137.3 2.5 %project.1 = bf16[64,1280]{1,0:T(8,128)(2,1)} custom-call(bf16[4,160,64]{2,1,0:T(8,128)(2,1)} %get-tuple-element.29.s_ref, bf16[160,1280]{1,0:T(8,128)(2,1)} %refs_0_, bf16[160,1280]{1,0:T(8,128)(2,1)} %copy-done.12, bf16[160,1280]{1,0:T(8,128)(2,1)} %copy-done.11, bf16[160,1280]{1,0:T(8,128)(2,1)} %copy-done.13), custom_call_target="tpu_custom_call" | custom-call | flops 104857600 | bytes 1638400 | tf_op jit(solution)/shard_map/project/pallas_call | solution.py:30
  141.5 3.6 %collective-permute-done.35.refs_1_ = bf16[2,904,128]{2,1,0:T(8,128)(2,1)S(1)} collective-permute-done((bf16[2,904,128]{2,1,0:T(8,128)(2,1)S(1)}, bf16[2,904,128]{2,1,0:T(8,128)(2,1)S(1)}, u32[]{:S(2)}, u32[]{:S(2)}) %collective-permute-start.35) | collective-permute-done | bytes 462880 | tf_op jit(solution)/shard_map/ppermute | solution.py:512
  145.9 4.6 %place_grad.1 = f32[1440,640]{1,0:T(8,128)} custom-call(s32[2]{0:T(128)} %pad_add_fusion.id_ref, bf16[2,904,128]{2,1,0:T(8,128)(2,1)} %copy-done.1, bf16[2,904,128]{2,1,0:T(8,128)(2,1)} %copy-done.9, bf16[2,896,128]{2,1,0:T(8,128)(2,1)} %copy-done.2, bf16[2,896,128]{2,1,0:T(8,128)(2,1)} %copy-done.10), custom_call_target="tpu_custom_call" | custom-call | bytes 5529600 | tf_op jit(solution)/shard_map/place_grad/pallas_call | solution.py:30
  (197 shorter events, 44.5 us)
Async XLA Ops:
  17.2 9.4 %collective-permute-start.1 = (bf16[1,160,256]{2,1,0:T(8,128)(2,1)S(1)}, bf16[1,160,256]{2,1,0:T(8,128)(2,1)S(1)}, u32[]{:S(2)}, u32[]{:S(2)}) collective-permute-start(bf16[1,160,256]{2,1,0:T(8,128)(2,1)S(1)} %get-tuple-element.56), channel_id=1, source_target_pairs={{0,2},{1,3},{2,0},{3,1},{4,6},{5,7},{6,4},{7,5},{8,10},{9,11},{10,... | collective-permute-start | bytes 245768 | tf_op jit(solution)/shard_map/ppermute | solution.py:512
  17.5 9.6 %collective-permute-start.2 = (bf16[1,160,256]{2,1,0:T(8,128)(2,1)S(1)}, bf16[1,160,256]{2,1,0:T(8,128)(2,1)S(1)}, u32[]{:S(2)}, u32[]{:S(2)}) collective-permute-start(bf16[1,160,256]{2,1,0:T(8,128)(2,1)S(1)} %get-tuple-element.55), channel_id=1, source_target_pairs={{0,3},{1,2},{2,1},{3,0},{4,7},{5,6},{6,5},{7,4},{8,11},{9,10},{10,... | collective-permute-start | bytes 245768 | tf_op jit(solution)/shard_map/ppermute | solution.py:512
  18.9 10.8 %collective-permute-start.6 = (bf16[160,256]{1,0:T(8,128)(2,1)}, bf16[160,256]{1,0:T(8,128)(2,1)S(1)}, u32[]{:S(2)}, u32[]{:S(2)}) collective-permute-start(bf16[160,256]{1,0:T(8,128)(2,1)} %back_product.1.refs_0_), channel_id=1, source_target_pairs={{0,1},{1,0},{2,3},{3,2},{4,5},{5,4},{6,7},{7,6},{8,9},{9,8},{10,11... | collective-permute-start | bytes 245768 | tf_op jit(solution)/shard_map/ppermute | solution.py:512
  19.7 10.0 %collective-permute-start.8 = (bf16[160,256]{1,0:T(8,128)(2,1)S(1)}, bf16[160,256]{1,0:T(8,128)(2,1)S(1)}, u32[]{:S(2)}, u32[]{:S(2)}) collective-permute-start(bf16[160,256]{1,0:T(8,128)(2,1)S(1)} %collective-permute-done.7.refs_2_), channel_id=1, source_target_pairs={{0,1},{1,0},{2,3},{3,2},{4,5},{5,4},{6,7},{7,6},{8,9},{9,8},{10,11... | collective-permute-start | bytes 245768 | tf_op jit(solution)/shard_map/ppermute | solution.py:512
  23.9 17.8 %collective-permute-start.20 = (bf16[1,160,256]{2,1,0:T(8,128)(2,1)S(1)}, bf16[1,160,256]{2,1,0:T(8,128)(2,1)S(1)}, u32[]{:S(2)}, u32[]{:S(2)}) collective-permute-start(bf16[1,160,256]{2,1,0:T(8,128)(2,1)S(1)} %get-tuple-element.48), channel_id=1, source_target_pairs={{0,12},{4,8},{8,4},{12,0},{16,28},{20,24},{24,20},{28,16},{1,13},{... | collective-permute-start | bytes 245768 | tf_op jit(solution)/shard_map/ppermute | solution.py:512
  26.7 15.0 %collective-permute-start.19 = (bf16[1,160,256]{2,1,0:T(8,128)(2,1)S(1)}, bf16[1,160,256]{2,1,0:T(8,128)(2,1)S(1)}, u32[]{:S(2)}, u32[]{:S(2)}) collective-permute-start(bf16[1,160,256]{2,1,0:T(8,128)(2,1)S(1)} %get-tuple-element.49), channel_id=1, source_target_pairs={{0,8},{4,12},{8,0},{12,4},{16,24},{20,28},{24,16},{28,20},{1,9},{5... | collective-permute-start | bytes 245768 | tf_op jit(solution)/shard_map/ppermute | solution.py:512
  27.1 14.5 %collective-permute-start.18 = (bf16[1,160,256]{2,1,0:T(8,128)(2,1)S(1)}, bf16[1,160,256]{2,1,0:T(8,128)(2,1)S(1)}, u32[]{:S(2)}, u32[]{:S(2)}) collective-permute-start(bf16[1,160,256]{2,1,0:T(8,128)(2,1)S(1)} %get-tuple-element.50), channel_id=1, source_target_pairs={{0,4},{4,0},{8,12},{12,8},{16,20},{20,16},{24,28},{28,24},{1,5},{5... | collective-permute-start | bytes 245768 | tf_op jit(solution)/shard_map/ppermute | solution.py:512
  40.1 12.8 %collective-permute-start.9 = (bf16[2,640,256]{2,1,0:T(8,128)(2,1)}, bf16[2,640,256]{2,1,0:T(8,128)(2,1)S(1)}, u32[]{:S(2)}, u32[]{:S(2)}) collective-permute-start(bf16[2,640,256]{2,1,0:T(8,128)(2,1)} %get-tuple-element.27), channel_id=1, source_target_pairs={{0,1},{1,0},{2,3},{3,2},{4,5},{5,4},{6,7},{7,6},{8,9},{9,8},{10,11... | collective-permute-start | bytes 1966088 | tf_op jit(solution)/shard_map/ppermute | solution.py:512
  41.7 10.0 %collective-permute-start.22 = (bf16[4,160,256]{2,1,0:T(8,128)(2,1)S(1)}, bf16[4,160,256]{2,1,0:T(8,128)(2,1)S(1)}, u32[]{:S(2)}, u32[]{:S(2)}) collective-permute-start(bf16[4,160,256]{2,1,0:T(8,128)(2,1)S(1)} %pad_maximum_fusion.5.refs_4_), channel_id=1, source_target_pairs={{0,2},{1,3},{2,0},{3,1},{4,6},{5,7},{6,4},{7,5},{8,10},{9,11},{10,... | collective-permute-start | bytes 983048 | tf_op jit(solution)/shard_map/ppermute | solution.py:512
  43.6 8.1 %collective-permute-start.21 = (bf16[4,160,256]{2,1,0:T(8,128)(2,1)S(1)}, bf16[4,160,256]{2,1,0:T(8,128)(2,1)S(1)}, u32[]{:S(2)}, u32[]{:S(2)}) collective-permute-start(bf16[4,160,256]{2,1,0:T(8,128)(2,1)S(1)} %pad_maximum_fusion.5.refs_4_), channel_id=1, source_target_pairs={{0,1},{1,0},{2,3},{3,2},{4,5},{5,4},{6,7},{7,6},{8,9},{9,8},{10,11... | collective-permute-start | bytes 983048 | tf_op jit(solution)/shard_map/ppermute | solution.py:512
  46.9 22.0 %collective-permute-start.15 = (bf16[2,2,160,256]{3,2,1,0:T(8,128)(2,1)S(1)}, bf16[2,2,160,256]{3,2,1,0:T(8,128)(2,1)S(1)}, u32[]{:S(2)}, u32[]{:S(2)}) collective-permute-start(bf16[2,2,160,256]{3,2,1,0:T(8,128)(2,1)S(1)} %pad_maximum_fusion.3.refs_0_), channel_id=1, source_target_pairs={{0,8},{4,12},{8,0},{12,4},{16,24},{20,28},{24,16},{28,20},{1,9},{5... | collective-permute-start | bytes 983048 | tf_op jit(solution)/shard_map/ppermute | solution.py:512
  50.7 18.3 %collective-permute-start.17 = (bf16[2,2,160,256]{3,2,1,0:T(8,128)(2,1)S(1)}, bf16[2,2,160,256]{3,2,1,0:T(8,128)(2,1)S(1)}, u32[]{:S(2)}, u32[]{:S(2)}) collective-permute-start(bf16[2,2,160,256]{3,2,1,0:T(8,128)(2,1)S(1)} %pad_maximum_fusion.4.refs_2_), channel_id=1, source_target_pairs={{0,4},{4,0},{8,12},{12,8},{16,20},{20,16},{24,28},{28,24},{1,5},{5... | collective-permute-start | bytes 983048 | tf_op jit(solution)/shard_map/ppermute | solution.py:512
  51.7 17.3 %collective-permute-start.23 = (bf16[4,160,256]{2,1,0:T(8,128)(2,1)S(1)}, bf16[4,160,256]{2,1,0:T(8,128)(2,1)S(1)}, u32[]{:S(2)}, u32[]{:S(2)}) collective-permute-start(bf16[4,160,256]{2,1,0:T(8,128)(2,1)S(1)} %collective-permute-done.22.refs_6_), channel_id=1, source_target_pairs={{0,1},{1,0},{2,3},{3,2},{4,5},{5,4},{6,7},{7,6},{8,9},{9,8},{10,11... | collective-permute-start | bytes 983048 | tf_op jit(solution)/shard_map/ppermute | solution.py:512
  51.8 9.7 %collective-permute-start.24 = (bf16[1,160,256]{2,1,0:T(8,128)(2,1)S(1)}, bf16[1,160,256]{2,1,0:T(8,128)(2,1)S(1)}, u32[]{:S(2)}, u32[]{:S(2)}) collective-permute-start(bf16[1,160,256]{2,1,0:T(8,128)(2,1)S(1)} %get-tuple-element.45), channel_id=1, source_target_pairs={{0,4},{4,0},{8,12},{12,8},{16,20},{20,16},{24,28},{28,24},{1,5},{5... | collective-permute-start | bytes 245768 | tf_op jit(solution)/shard_map/ppermute | solution.py:512
  52.9 8.6 %collective-permute-start.25 = (bf16[1,160,256]{2,1,0:T(8,128)(2,1)S(1)}, bf16[1,160,256]{2,1,0:T(8,128)(2,1)S(1)}, u32[]{:S(2)}, u32[]{:S(2)}) collective-permute-start(bf16[1,160,256]{2,1,0:T(8,128)(2,1)S(1)} %get-tuple-element.44), channel_id=1, source_target_pairs={{0,8},{4,12},{8,0},{12,4},{16,24},{20,28},{24,16},{28,20},{1,9},{5... | collective-permute-start | bytes 245768 | tf_op jit(solution)/shard_map/ppermute | solution.py:512
  61.5 20.2 %collective-permute-start.10 = (bf16[1,640,256]{2,1,0:T(8,128)(2,1)S(1)}, bf16[1,640,256]{2,1,0:T(8,128)(2,1)S(1)}, u32[]{:S(2)}, u32[]{:S(2)}) collective-permute-start(bf16[1,640,256]{2,1,0:T(8,128)(2,1)S(1)} %slice.146), channel_id=1, source_target_pairs={{0,2},{1,3},{2,0},{3,1},{4,6},{5,7},{6,4},{7,5},{8,10},{9,11},{10,... | collective-permute-start | bytes 983048 | tf_op jit(solution)/shard_map/ppermute | solution.py:512
  66.9 21.0 %collective-permute-start.12 = (bf16[160,1280]{1,0:T(8,128)(2,1)S(1)}, bf16[160,1280]{1,0:T(8,128)(2,1)S(1)}, u32[]{:S(2)}, u32[]{:S(2)}) collective-permute-start(bf16[160,1280]{1,0:T(8,128)(2,1)S(1)} %copy-done.3), channel_id=1, source_target_pairs={{0,2},{1,3},{2,0},{3,1},{4,6},{5,7},{6,4},{7,5},{8,10},{9,11},{10,... | collective-permute-start | bytes 1228808 | tf_op jit(solution)/shard_map/ppermute | solution.py:512
  68.9 18.0 %collective-permute-start.28 = (bf16[640,256]{1,0:T(8,128)(2,1)S(1)}, bf16[640,256]{1,0:T(8,128)(2,1)S(1)}, u32[]{:S(2)}, u32[]{:S(2)}) collective-permute-start(bf16[640,256]{1,0:T(8,128)(2,1)S(1)} %copy-done.35), channel_id=1, source_target_pairs={{0,2},{1,3},{2,0},{3,1},{4,6},{5,7},{6,4},{7,5},{8,10},{9,11},{10,... | collective-permute-start | bytes 983048 | tf_op jit(solution)/shard_map/ppermute | solution.py:512
  78.1 10.3 %collective-permute-start.36 = (bf16[896,128]{1,0:T(8,128)(2,1)}, bf16[896,128]{1,0:T(8,128)(2,1)S(1)}, u32[]{:S(2)}, u32[]{:S(2)}) collective-permute-start(bf16[896,128]{1,0:T(8,128)(2,1)} %get-tuple-element.38), channel_id=1, source_target_pairs={{0,16},{4,20},{8,24},{12,28},{16,0},{20,4},{24,8},{28,12},{1,17},{... | collective-permute-start | bytes 688136 | tf_op jit(solution)/shard_map/ppermute | solution.py:512
  86.3 16.5 %collective-permute-start.27 = (bf16[640,256]{1,0:T(8,128)(2,1)S(1)}, bf16[640,256]{1,0:T(8,128)(2,1)S(1)}, u32[]{:S(2)}, u32[]{:S(2)}) collective-permute-start(bf16[640,256]{1,0:T(8,128)(2,1)S(1)} %copy-done.35), channel_id=1, source_target_pairs={{0,1},{1,0},{2,3},{3,2},{4,5},{5,4},{6,7},{7,6},{8,9},{9,8},{10,11... | collective-permute-start | bytes 983048 | tf_op jit(solution)/shard_map/ppermute | solution.py:512
  86.8 13.5 %collective-permute-start.33 = (bf16[904,128]{1,0:T(8,128)(2,1)S(1)}, bf16[904,128]{1,0:T(8,128)(2,1)S(1)}, u32[]{:S(2)}, u32[]{:S(2)}) collective-permute-start(bf16[904,128]{1,0:T(8,128)(2,1)S(1)} %copy-done.21), channel_id=1, source_target_pairs={{0,16},{4,20},{8,24},{12,28},{16,0},{20,4},{24,8},{28,12},{1,17},{... | collective-permute-start | bytes 694280 | tf_op jit(solution)/shard_map/ppermute | solution.py:512
  87.9 15.0 %collective-permute-start.29 = (bf16[640,256]{1,0:T(8,128)(2,1)S(1)}, bf16[640,256]{1,0:T(8,128)(2,1)S(1)}, u32[]{:S(2)}, u32[]{:S(2)}) collective-permute-start(bf16[640,256]{1,0:T(8,128)(2,1)S(1)} %collective-permute-done.28.refs_2_), channel_id=1, source_target_pairs={{0,1},{1,0},{2,3},{3,2},{4,5},{5,4},{6,7},{7,6},{8,9},{9,8},{10,11... | collective-permute-start | bytes 983048 | tf_op jit(solution)/shard_map/ppermute | solution.py:512
  92.4 43.3 %collective-permute-start.11 = (bf16[160,1280]{1,0:T(8,128)(2,1)S(1)}, bf16[160,1280]{1,0:T(8,128)(2,1)S(1)}, u32[]{:S(2)}, u32[]{:S(2)}) collective-permute-start(bf16[160,1280]{1,0:T(8,128)(2,1)S(1)} %copy-done.3), channel_id=1, source_target_pairs={{0,1},{1,0},{2,3},{3,2},{4,5},{5,4},{6,7},{7,6},{8,9},{9,8},{10,11... | collective-permute-start | bytes 1228808 | tf_op jit(solution)/shard_map/ppermute | solution.py:512
  93.5 42.2 %collective-permute-start.13 = (bf16[160,1280]{1,0:T(8,128)(2,1)S(1)}, bf16[160,1280]{1,0:T(8,128)(2,1)S(1)}, u32[]{:S(2)}, u32[]{:S(2)}) collective-permute-start(bf16[160,1280]{1,0:T(8,128)(2,1)S(1)} %collective-permute-done.12.refs_2_), channel_id=1, source_target_pairs={{0,1},{1,0},{2,3},{3,2},{4,5},{5,4},{6,7},{7,6},{8,9},{9,8},{10,11... | collective-permute-start | bytes 1228808 | tf_op jit(solution)/shard_map/ppermute | solution.py:512
  100.3 10.6 %collective-permute-start.42 = (bf16[2,40,1280]{2,1,0:T(8,128)(2,1)S(1)}, bf16[2,40,1280]{2,1,0:T(8,128)(2,1)S(1)}, u32[]{:S(2)}, u32[]{:S(2)}) collective-permute-start(bf16[2,40,1280]{2,1,0:T(8,128)(2,1)S(1)} %slice.147), channel_id=1, source_target_pairs={{0,8},{4,12},{8,0},{12,4},{16,24},{20,28},{24,16},{28,20},{1,9},{5... | collective-permute-start | bytes 614408 | tf_op jit(solution)/shard_map/ppermute | solution.py:512
  102.8 13.0 %collective-permute-start.37 = (bf16[896,128]{1,0:T(8,128)(2,1)S(1)}, bf16[896,128]{1,0:T(8,128)(2,1)S(1)}, u32[]{:S(2)}, u32[]{:S(2)}) collective-permute-start(bf16[896,128]{1,0:T(8,128)(2,1)S(1)} %add_convert_fusion.1), channel_id=1, source_target_pairs={{0,8},{4,12},{8,0},{12,4},{16,24},{20,28},{24,16},{28,20},{1,9},{5... | collective-permute-start | bytes 688136 | tf_op jit(solution)/shard_map/ppermute | solution.py:512
  102.9 24.0 %collective-permute-start.34 = (bf16[904,128]{1,0:T(8,128)(2,1)S(1)}, bf16[904,128]{1,0:T(8,128)(2,1)S(1)}, u32[]{:S(2)}, u32[]{:S(2)}) collective-permute-start(bf16[904,128]{1,0:T(8,128)(2,1)S(1)} %add_convert_fusion), channel_id=1, source_target_pairs={{0,4},{4,0},{8,12},{12,8},{16,20},{20,16},{24,28},{28,24},{1,5},{5... | collective-permute-start | bytes 694280 | tf_op jit(solution)/shard_map/ppermute | solution.py:512
  115.8 12.0 %collective-permute-start.30 = (bf16[1,160,256]{2,1,0:T(8,128)(2,1)S(1)}, bf16[1,160,256]{2,1,0:T(8,128)(2,1)S(1)}, u32[]{:S(2)}, u32[]{:S(2)}) collective-permute-start(bf16[1,160,256]{2,1,0:T(8,128)(2,1)S(1)} %get-tuple-element.41), channel_id=1, source_target_pairs={{0,1},{1,0},{2,3},{3,2},{4,5},{5,4},{6,7},{7,6},{8,9},{9,8},{10,11... | collective-permute-start | bytes 245768 | tf_op jit(solution)/shard_map/ppermute | solution.py:512
  115.8 10.0 %collective-permute-start.44 = (bf16[40,1280]{1,0:T(8,128)(2,1)S(1)}, bf16[40,1280]{1,0:T(8,128)(2,1)S(1)}, u32[]{:S(2)}, u32[]{:S(2)}) collective-permute-start(bf16[40,1280]{1,0:T(8,128)(2,1)S(1)} %fusion.1), channel_id=1, source_target_pairs={{0,16},{4,20},{8,24},{12,28},{16,0},{20,4},{24,8},{28,12},{1,17},{... | collective-permute-start | bytes 307208 | tf_op jit(solution)/shard_map/ppermute | solution.py:512
  130.3 11.2 %collective-permute-start.38 = (bf16[2,896,128]{2,1,0:T(8,128)(2,1)S(1)}, bf16[2,896,128]{2,1,0:T(8,128)(2,1)S(1)}, u32[]{:S(2)}, u32[]{:S(2)}) collective-permute-start(bf16[2,896,128]{2,1,0:T(8,128)(2,1)S(1)} %pad_maximum_fusion.1.refs_2_), channel_id=1, source_target_pairs={{0,4},{4,0},{8,12},{12,8},{16,20},{20,16},{24,28},{28,24},{1,5},{5... | collective-permute-start | bytes 1376264 | tf_op jit(solution)/shard_map/ppermute | solution.py:512
  131.6 13.5 %collective-permute-start.35 = (bf16[2,904,128]{2,1,0:T(8,128)(2,1)S(1)}, bf16[2,904,128]{2,1,0:T(8,128)(2,1)S(1)}, u32[]{:S(2)}, u32[]{:S(2)}) collective-permute-start(bf16[2,904,128]{2,1,0:T(8,128)(2,1)S(1)} %pad_maximum_fusion.refs_0_), channel_id=1, source_target_pairs={{0,8},{4,12},{8,0},{12,4},{16,24},{20,28},{24,16},{28,20},{1,9},{5... | collective-permute-start | bytes 1388552 | tf_op jit(solution)/shard_map/ppermute | solution.py:512
  132.4 18.1 %collective-permute-start.46 = (bf16[2,40,1280]{2,1,0:T(8,128)(2,1)S(1)}, bf16[2,40,1280]{2,1,0:T(8,128)(2,1)S(1)}, u32[]{:S(2)}, u32[]{:S(2)}) collective-permute-start(bf16[2,40,1280]{2,1,0:T(8,128)(2,1)S(1)} %pad_maximum_fusion.6), channel_id=1, source_target_pairs={{0,8},{4,12},{8,0},{12,4},{16,24},{20,28},{24,16},{28,20},{1,9},{5... | collective-permute-start | bytes 614408 | tf_op jit(solution)/shard_map/ppermute | solution.py:512
  (62 other events, 322.6 us)

commit v3 on v2

v3 whole, which is shorter than its diff:
```python
import math

import jax
import jax.numpy as jnp
from jax import lax
from jax.experimental import pallas as pl
from jax.experimental.pallas import tpu as pltpu
from jax.sharding import PartitionSpec as P

BF = jnp.bfloat16
F32 = jnp.float32
VMEM_LIMIT = 56 << 20
LANES = 128
BLOCK = 4


def dot(a, b, dims=((1,), (0,))):
    return lax.dot_general(a, b, (dims, ((), ())), preferred_element_type=F32)


NT = ((1,), (1,))
TN = ((0,), (0,))


def call(name, body, outs, scratch, flops, moved, args, scalars=0):
    specs = [
        pl.BlockSpec(memory_space=pltpu.SMEM if i < scalars else pltpu.VMEM)
        for i in range(len(args))
    ]
    return pl.pallas_call(
        body,
        out_shape=outs,
        in_specs=specs,
        out_specs=jax.tree.map(lambda _: pl.BlockSpec(memory_space=pltpu.VMEM), outs),
        scratch_shapes=scratch,
        compiler_params=pltpu.CompilerParams(vmem_limit_bytes=VMEM_LIMIT),
        cost_estimate=pl.CostEstimate(flops=flops, bytes_accessed=moved, transcendentals=0),
        name=name,
    )(*args)


def shape(dims, kind):
    return jax.ShapeDtypeStruct(dims, kind)


def rows_at(start, size, step):
    return pl.ds(pl.multiple_of(start, step), size)


def round_up(value, step):
    return -(-value // step) * step


def turn_filters(conv_weight):
    rows, chans = conv_weight.shape
    own = rows // 9

    def body(w_ref, o_ref, t_ref, wide):
        for k in range(chans // LANES):
            cols = slice(k * LANES, (k + 1) * LANES)
            wide[k] = w_ref[:, cols].astype(F32)
            for t in range(9):
                piece = wide[k, pl.ds(t, own, stride=9), :]
                o_ref[t * own : (t + 1) * own, cols] = piece.astype(BF)
        t_ref[...] = o_ref[...].T

    return call(
        "turn_filters",
        body,
        [shape((rows, chans), BF), shape((chans, rows), BF)],
        [pltpu.VMEM((chans // LANES, rows, LANES), F32)],
        0,
        6 * rows * chans,
        [conv_weight],
    )


def col_sets(chans):
    rest = (chans - BLOCK * LANES) // BLOCK
    return BLOCK * LANES, rest


def turn_images(ids, source, group, own):
    pixels, chans = source.shape

    def body(id_ref, i_ref, img_ref, wide):
        wide[...] = i_ref[...].astype(F32).T
        for j in range(group):
            img_ref[j] = wide[rows_at((id_ref[0] ^ j) * own, own, 8), :].astype(BF)

    return call(
        "turn_images",
        body,
        shape((group, own, pixels), BF),
        [pltpu.VMEM((chans, pixels), F32)],
        0,
        4 * pixels * chans,
        [ids, source],
        1,
    )


def back_product(ids, cots, skip_weight):
    few, wide_chans = cots[0].shape
    own = skip_weight.shape[0]
    group = len(cots)

    def body(id_ref, s_ref, *refs):
        o_ref, held = refs[group:]
        for j in range(group):
            held[rows_at((id_ref[0] ^ j) * few, few, 16), :] = refs[j][...]
        o_ref[...] = dot(s_ref[...], held[...], NT).astype(BF)

    return call(
        "back_product",
        body,
        [shape((own, group * few), BF), shape((group * few, wide_chans), BF)],
        [],
        2 * own * group * few * wide_chans,
        group * few * wide_chans * 2,
        [ids, skip_weight, *cots],
        1,
    )


def pixel_parts(pixels, width):
    at = lax.broadcasted_iota(jnp.int32, (1, pixels), 1)
    return at // width, at % width


def neighbours(value, pixels, width):
    height = pixels // width
    y, x = pixel_parts(pixels, width)
    for dy in range(3):
        for dx in range(3):
            off = (dy - 1) * width + dx - 1
            if off == 0:
                yield value
                continue
            inside = (y >= 1 - dy) & (y < height + 1 - dy) & (x >= 1 - dx) & (x < width + 1 - dx)
            yield jnp.where(inside, pltpu.roll(value, -off % pixels, 1), 0.0)


def spread_matrix(few_all, few, pixels, width):
    y, x = pixel_parts(pixels, width)
    coarse = (y // 2) * (width // 2) + x // 2
    even = (y % 2 == 0) & (x % 2 == 0)
    row = lax.broadcasted_iota(jnp.int32, (few_all, pixels), 0)
    for d in range(few_all // few):
        yield jnp.where(even & (row == d * few + coarse), 1.0, 0.0).astype(BF)


def spread_rows(few_all, few, pixels, width, d):
    at = lax.broadcasted_iota(jnp.int32, (pixels, 1), 0)
    y, x = at // width, at % width
    coarse = jnp.where((y % 2 == 0) & (x % 2 == 0), (y // 2) * (width // 2) + x // 2, -few_all)
    col = lax.broadcasted_iota(jnp.int32, (pixels, few_all), 1)
    return jnp.where(col == d * few + coarse, 1.0, 0.0).astype(BF)


def forward(ids, own_images, w_turned, width, few):
    group = len(own_images)
    own, pixels = own_images[0].shape[1:]
    chans, rows = w_turned.shape
    few_all = group * few

    def body(id_ref, w_ref, *refs):
        keep_ref, send_ref, patch, sums, moves = refs[group:]
        for m in range(group):
            v = refs[m][0].astype(F32)
            value = (v / (1.0 + jnp.exp(-v))).astype(BF).astype(F32)
            here = slice(m * pixels, (m + 1) * pixels)
            for t, moved in enumerate(neighbours(value, pixels, width)):
                patch[t * own : (t + 1) * own, here] = moved.astype(BF)
            moves[here] = spread_rows(few_all, few, pixels, width, id_ref[0] ^ m)
        out = dot(w_ref[...], patch[...])
        for m in range(group):
            piece = out[:, m * pixels : (m + 1) * pixels]
            if m % 2:
                send_ref[m // 2, :chans] = piece.astype(BF)
            else:
                keep_ref[m // 2, :chans] = piece
        evens = dot(patch[...], moves[...]).astype(BF)
        sums[...] = dot(w_ref[...], evens)
        for j in range(group):
            piece = sums[rows_at((id_ref[0] ^ j) * own, own, 8), :]
            for n in range(few_all // pixels):
                below = slice(chans + n * own, chans + (n + 1) * own)
                cols = piece[:, n * pixels : (n + 1) * pixels]
                if j % 2:
                    send_ref[j // 2, below] = cols.astype(BF)
                else:
                    keep_ref[j // 2, below] = cols

    return call(
        "forward",
        body,
        [
            shape((group // 2, chans + own * few_all // pixels, pixels), F32),
            shape((group // 2, chans + own * few_all // pixels, pixels), BF),
            shape((rows, group * pixels), BF),
        ],
        [pltpu.VMEM((chans, few_all), F32), pltpu.VMEM((group * pixels, few_all), BF)],
        2 * group * pixels * rows * (chans + few_all),
        group * chans * pixels * 3,
        [ids, w_turned, *own_images],
        1,
    )


def filter_grad(ids, patch, hidden_cots, backs, width, few, halves):
    rows = patch.shape[0]
    group = len(hidden_cots)
    pixels, chans = hidden_cots[0].shape
    own, few_all = backs[0].shape
    _, rest = col_sets(chans)
    tiles = chans // LANES
    part = round_up(-(-rows // BLOCK), 8)

    def body(id_ref, p_ref, *refs):
        cot_refs, back_refs = refs[:group], refs[group : 2 * group]
        hid = refs[2 * group]
        outs = refs[2 * group + 1 : -3]
        back, tile, last = refs[-3:]
        for j in range(group):
            back[rows_at((id_ref[0] ^ j) * own, own, 8), :] = back_refs[j][...].astype(F32)
        back_all = back[...].astype(BF)
        for j in range(group):
            d = id_ref[0] ^ j
            spread = dot(spread_rows(few_all, few, pixels, width, d), back_all, NT)
            hid[j * pixels : (j + 1) * pixels] = (cot_refs[j][...].astype(F32) + spread).astype(BF)
        total = dot(p_ref[...], hid[...])
        for n in range(tiles):
            tile[n] = total[:, n * LANES : (n + 1) * LANES]
        lane = lax.broadcasted_iota(jnp.int32, (part, LANES), 1) // rest
        for k in range(BLOCK):
            q = id_ref[1] ^ k
            share = jnp.zeros((part, LANES), F32)
            for i in range(BLOCK):
                size = min(part, rows - i * part)
                piece = tile[tiles - 1, i * part : i * part + size, :]
                if size < part:
                    piece = jnp.concatenate([piece, jnp.zeros((part - size, LANES), F32)])
                turn = ((i - q + BLOCK) % BLOCK) * rest
                share = share + jnp.where(lane == i, pltpu.roll(piece, turn, 1), 0.0)
            last[...] = share
            for h, (low, high) in enumerate(halves):
                ref = outs[2 * h + k % 2]
                main = min(high, rows)
                if low < main:
                    ref[k // 2, : main - low] = tile[q, low:main, :].astype(ref.dtype)
                if high > rows:
                    start = max(low, rows)
                    ref[k // 2, start - low :] = last[start - rows : high - rows].astype(ref.dtype)

    outs = [shape((group * pixels, chans), BF)]
    for low, high in halves:
        outs += [shape((2, high - low, LANES), F32), shape((2, high - low, LANES), BF)]
    return call(
        "filter_grad",
        body,
        outs,
        [
            pltpu.VMEM((chans, few_all), F32),
            pltpu.VMEM((tiles, rows, LANES), F32),
            pltpu.VMEM((part, LANES), F32),
        ],
        2 * group * pixels * rows * chans,
        group * pixels * chans * 4 + rows * chans * 3,
        [ids, patch, *hidden_cots, *backs],
        1,
    )


def place_grad(ids, pieces, own, chans, scale):
    rows = 9 * own
    part = round_up(-(-rows // BLOCK), 8)
    _, rest = col_sets(chans)
    tiles = chans // LANES

    def body(id_ref, *refs):
        o_ref, wide, last, sems = refs[-4:]
        lane = lax.broadcasted_iota(jnp.int32, (part, LANES), 1) // rest

        def store(where, low, piece):
            high = low + piece.shape[0]
            for t in range(9):
                lo, hi = max(low, t * own), min(high, (t + 1) * own)
                if lo < hi:
                    wide[where, pl.ds((lo - t * own) * 9 + t, hi - lo, stride=9), :] = piece[
                        lo - low : hi - low
                    ]

        def copy_out(n, where):
            at = pl.ds(pl.multiple_of(where * LANES, LANES), LANES)
            return pltpu.make_async_copy(wide.at[where], o_ref.at[:, at], sems.at[n])

        last[...] = jnp.zeros_like(last)
        for k in range(BLOCK):
            q = id_ref[1] ^ k
            for n, (low, high, members, _) in enumerate(pieces):
                if k not in members:
                    continue
                at, main = members.index(k), min(high, rows)
                if low < main:
                    store(q, low, refs[n][at, : main - low, :].astype(F32) * scale)
                if high > rows:
                    assert low <= rows and high >= rows + part
                    share = refs[n][at, rows - low : rows - low + part, :].astype(F32) * scale
                    for i in range(BLOCK):
                        turn = ((q - i + BLOCK) % BLOCK) * rest
                        last[i] += jnp.where(lane == q, pltpu.roll(share, turn, 1), 0.0)
            copy_out(k, q).start()
        for i in range(BLOCK):
            store(BLOCK, i * part, last[i, : min(part, rows - i * part), :])
        copy_out(BLOCK, BLOCK).start()
        for k in range(BLOCK):
            copy_out(k, id_ref[1] ^ k).wait()
        copy_out(BLOCK, BLOCK).wait()

    return pl.pallas_call(
        body,
        out_shape=shape((rows, chans), F32),
        in_specs=[pl.BlockSpec(memory_space=pltpu.SMEM)]
        + [pl.BlockSpec(memory_space=pltpu.VMEM)] * len(pieces),
        out_specs=pl.BlockSpec(memory_space=pl.ANY),
        scratch_shapes=[
            pltpu.VMEM((tiles, rows, LANES), F32),
            pltpu.VMEM((BLOCK, part, LANES), F32),
            pltpu.SemaphoreType.DMA((BLOCK + 1,)),
        ],
        compiler_params=pltpu.CompilerParams(vmem_limit_bytes=VMEM_LIMIT),
        cost_estimate=pl.CostEstimate(
            flops=0, bytes_accessed=rows * chans * 6, transcendentals=0
        ),
        name="place_grad",
    )(ids, *[array for *_, array in pieces])


def finish_hidden(source, held, got, width):
    pixels, chans = source.shape
    few = pixels // 4

    def body(s_ref, k_ref, g_ref, o_ref, sub_ref):
        total = (k_ref[0, :chans] + g_ref[0, :chans].astype(F32)).T
        hidden = (s_ref[...].astype(F32) + total).astype(BF)
        o_ref[...] = hidden
        (one_hot,) = spread_matrix(few, few, pixels, width)
        sub_ref[...] = dot(one_hot, hidden).astype(BF)

    return call(
        "finish_hidden",
        body,
        [shape((pixels, chans), BF), shape((few, chans), BF)],
        [],
        2 * few * pixels * chans,
        pixels * chans * 10,
        [source, held, got],
    )


def skip_grad_term(ids, held, got, own_images, cots, width, few):
    group = len(own_images)
    own, pixels = own_images[0].shape[1:]
    few_all, wide_chans = cots.shape
    blocks = few_all // pixels
    low = held.shape[1] - own * blocks
    part, tiles = own // BLOCK, wide_chans // LANES

    def body(id_ref, k_ref, g_ref, c_ref, *refs):
        keep_ref, send_ref, total = refs[-3:]
        sub = k_ref[0, low:] + g_ref[0, low:].astype(F32)
        sub = jnp.concatenate([sub[n * own : (n + 1) * own] for n in range(blocks)], axis=1)
        row = lax.broadcasted_iota(jnp.int32, (few_all, pixels), 0) // few
        every = jnp.zeros((few_all, pixels), F32)
        for matrix in spread_matrix(few_all, few, pixels, width):
            every = every + matrix.astype(F32)
        for j in range(group):
            chosen = jnp.where(row == (id_ref[0] ^ j), every, 0.0).astype(BF)
            sub = sub + dot(refs[j][0], chosen, NT)
        total[...] = dot(sub.astype(BF), c_ref[...])
        for k in range(BLOCK):
            piece = total[rows_at((id_ref[1] ^ k) * part, part, 8), :]
            ref = send_ref if k % 2 else keep_ref
            for n in range(tiles):
                cols = piece[:, n * LANES : (n + 1) * LANES]
                ref[k // 2, n * part : (n + 1) * part] = cols.astype(ref.dtype)

    return call(
        "skip_grad_term",
        body,
        [shape((2, part * tiles, LANES), F32), shape((2, part * tiles, LANES), BF)],
        [pltpu.VMEM((own, wide_chans), F32)],
        2 * own * few_all * wide_chans,
        own * wide_chans * 4,
        [ids, held, got, cots, *own_images],
        1,
    )


def project(ids, sub, skips):
    few, chans = sub.shape
    own, wide_chans = skips[0].shape
    group = len(skips)

    def body(id_ref, s_ref, *refs):
        o_ref, turned = refs[group:]
        turned[...] = s_ref[...].astype(F32).T
        total = jnp.zeros((few, wide_chans), F32)
        for j in range(group):
            rows = turned[rows_at((id_ref[0] ^ j) * own, own, 8), :].astype(BF)
            total = total + dot(rows, refs[j][...], TN)
        o_ref[...] = total.astype(BF)

    return call(
        "project",
        body,
        shape((few, wide_chans), BF),
        [pltpu.VMEM((chans, few), F32)],
        2 * few * chans * wide_chans,
        chans * wide_chans * 2,
        [ids, sub, *skips],
        1,
    )


def image_grad(ids, hidden_grad, own_images, w_tap, width):
    group = len(own_images)
    own, pixels = own_images[0].shape[1:]
    rows, chans = w_tap.shape
    height = pixels // width

    def body(id_ref, h_ref, w_ref, *refs):
        img_refs = refs[:group]
        o_ref, turned, tap = refs[group:]
        y, x = pixel_parts(pixels, width)
        for j in range(group):
            hid = h_ref[j * pixels : (j + 1) * pixels]
            turned[...] = hid.astype(F32).T
            tap[...] = dot(w_ref[...], hid, NT)
            side = tap[4 * own : 5 * own]
            for dy in range(3):
                for dx in range(3):
                    off = (dy - 1) * width + dx - 1
                    if off == 0:
                        continue
                    inside = (y >= dy - 1) & (y < height + dy - 1)
                    inside = inside & (x >= dx - 1) & (x < width + dx - 1)
                    t = 3 * dy + dx
                    moved = pltpu.roll(tap[t * own : (t + 1) * own], off % pixels, 1)
                    side = side + jnp.where(inside, moved, 0.0)
            v = img_refs[j][0].astype(F32)
            sig = 1.0 / (1.0 + jnp.exp(-v))
            slope = sig * (1.0 + v * (1.0 - sig))
            mine = turned[rows_at(id_ref[0] * own, own, 8), :]
            o_ref[j] = (mine + slope * side).astype(BF)

    return call(
        "image_grad",
        body,
        shape((group, own, pixels), BF),
        [pltpu.VMEM((chans, pixels), F32), pltpu.VMEM((rows, pixels), F32)],
        2 * group * pixels * rows * chans,
        group * pixels * chans * 2,
        [ids, hidden_grad, w_tap, *own_images],
        1,
    )


def finish_images(ids, pieces, chans):
    group = len(pieces)
    own, pixels = pieces[0].shape[1:]

    def body(id_ref, *refs):
        o_ref, wide = refs[group:]
        for j in range(group):
            wide[rows_at((id_ref[0] ^ j) * own, own, 8), :] = refs[j][0].astype(F32)
        o_ref[...] = wide[...].T.astype(BF)

    return call(
        "finish_images",
        body,
        shape((pixels, chans), BF),
        [pltpu.VMEM((chans, pixels), F32)],
        0,
        pixels * chans * 4,
        [ids, *pieces],
        1,
    )


def flip(value, axis, bit):
    return lax.ppermute(value, axis, [(i, i ^ bit) for i in range(lax.axis_size(axis))])


def after(value, *others):
    return lax.optimization_barrier((value, *others))[0]


def high_bits(count):
    return [1 << k for k in reversed(range(count.bit_length() - 1))]


def gather(value, axis, *others):
    found = {0: value}
    for n, bit in enumerate(high_bits(lax.axis_size(axis))):
        for j, held in list(found.items()):
            if n == 1 and j and others:
                held = found[j] = after(held, *others)
            found[j ^ bit] = flip(held, axis, bit)
    return [found[j] for j in range(len(found))]


def exchange(blocks, axis, count):
    return [flip(blocks[j : j + 1], axis, j) if j else blocks[:1] for j in range(count)]


def hop(value, bit):
    ranks, group = lax.axis_size("rep"), lax.axis_size("shard")
    pairs = []
    for r in range(ranks):
        for s in range(group):
            other = r ^ (bit if s % 2 == 0 else 3 - bit)
            pairs.append((r * group + s, other * group + s))
    return lax.ppermute(value, ("rep", "shard"), pairs)


def block_gather(value):
    pair = jnp.stack([value, hop(value, 2)])
    return [((0, 2), pair), ((1, 3), hop(pair, 1))]


def add_beyond_block(value):
    for bit in reversed(high_bits(lax.axis_size("rep"))):
        if bit >= BLOCK:
            got = flip(value, "rep", bit)
            value = (value.astype(F32) + got.astype(F32)).astype(BF)
    return value


def sum_scatter(keep, send):
    bits = list(reversed(high_bits(lax.axis_size("shard"))))
    for bit in bits[:-1]:
        total = keep + flip(send, "shard", bit).astype(F32)
        keep, send = total[0::2], total[1::2].astype(BF)
    return keep, flip(send, "shard", bits[-1])


def on_device(images, conv_weight, skip_weight, cotangent, hidden_cot):
    _, height, width, chans = images.shape
    own, wide = skip_weight.shape
    pixels, few = height * width, (height // 2) * (width // 2)
    group, ranks = lax.axis_size("shard"), lax.axis_size("rep")
    shard, rank = lax.axis_index("shard"), lax.axis_index("rep") % BLOCK
    member = jnp.where(shard % 2 == 0, rank, rank // 2 + 2 * (rank % 2))
    ids = jnp.stack([shard, member]).astype(jnp.int32)
    source = images.reshape(pixels, chans)

    img_sets = turn_images(ids, source, group, own)
    cots = gather(cotangent.reshape(few, wide), "shard", img_sets)
    own_images = exchange(img_sets, "shard", group)
    hidden_cots = gather(after(hidden_cot.reshape(pixels, chans), img_sets), "shard")
    back, cots = back_product(ids, cots, skip_weight)
    backs = [back] + [flip(back, "shard", j) for j in range(1, group)]
    w_tap, w_turned = turn_filters(after(conv_weight, back, *own_images))

    keep, send, patch = forward(after(ids, *backs, hidden_cots[2]), own_images, w_turned, width, few)

    rows = 9 * own
    part = round_up(-(-rows // BLOCK), 8)
    cut = min(round_up((rows + part) // 2, 8), rows)
    halves = [(0, cut), (cut, rows + part)]
    hidden_grad, keep_a, send_a, keep_b, send_b = filter_grad(
        ids, patch, hidden_cots, backs, width, few, halves
    )
    got_a, got_b = hop(send_a, 1), hop(send_b, 1)
    keep, got = sum_scatter(keep, send)
    own_input = image_grad(ids, hidden_grad, own_images, w_tap, width)
    got_a, own_input = lax.optimization_barrier((got_a, own_input))
    mid_a = (keep_a[1] + got_a[1].astype(F32)).astype(BF)
    last_a = hop(mid_a, 2)
    got_b = after(got_b, mid_a)
    mid_b = (keep_b[1] + got_b[1].astype(F32)).astype(BF)
    last_b = hop(mid_b, 2)
    sum_a = (keep_a[0] + got_a[0].astype(F32) + last_a.astype(F32)).astype(BF)
    full_a = add_beyond_block(sum_a)
    last_b = after(last_b, sum_a)
    sum_b = (keep_b[0] + got_b[0].astype(F32) + last_b.astype(F32)).astype(BF)
    full_b = add_beyond_block(sum_b)

    skip_keep, skip_send = skip_grad_term(
        after(ids, sum_b), keep, got, own_images, cots, width, few
    )
    got_s = hop(skip_send, 1)
    hidden, sub = finish_hidden(after(source, skip_send), keep, got, width)
    got_s, hidden = lax.optimization_barrier((got_s, hidden))
    mid_s = (skip_keep[1] + got_s[1].astype(F32)).astype(BF)
    last_s = hop(mid_s, 2)
    arrived = exchange(after(own_input, mid_b), "shard", group)
    input_grad = finish_images(after(ids, mid_s), arrived, chans)
    last_s, input_grad = lax.optimization_barrier((last_s, input_grad))
    sum_s = (skip_keep[0] + got_s[0].astype(F32) + last_s.astype(F32)).astype(BF)
    full_s = add_beyond_block(sum_s)
    skips = gather(after(skip_weight, mid_b), "shard")
    projected = project(after(ids, sum_s), sub, skips).reshape(cotangent.shape)
    sum_a, sum_b, sum_s = full_a, full_b, full_s
    sum_a = block_gather(sum_a)
    sum_b = block_gather(jnp.concatenate([sum_b, sum_s]))
    factor = 1.0 / math.sqrt(ranks * group * few)
    pieces = [(*halves[0], *pair) for pair in sum_a] + [(*halves[1], *pair) for pair in sum_b]
    conv_grad = place_grad(ids, pieces, own, chans, factor)
    skip_sum = {}
    for members, array in sum_b:
        for n, k in enumerate(members):
            skip_sum[k] = array[n, -sum_s.shape[0] :]
    skip_sum = jnp.stack([skip_sum[k] for k in range(BLOCK)])
    skip_sum = skip_sum[jnp.arange(BLOCK, dtype=jnp.int32) ^ member].astype(F32) * factor
    skip_sum = skip_sum.reshape(BLOCK, wide // LANES, own // BLOCK, LANES)
    skip_grad = skip_sum.transpose(0, 2, 1, 3).reshape(own, wide)

    return (
        hidden.reshape(images.shape),
        projected,
        input_grad.reshape(images.shape),
        conv_grad,
        skip_grad,
    )


def solution(mesh):
    placed = (
        P(("rep", "shard"), None, None, None),
        P("shard", None),
        P("shard", None),
        P(("rep", "shard"), None, None, None),
        P(("rep", "shard"), None, None, None),
    )
    return jax.shard_map(
        on_device,
        mesh=mesh,
        in_specs=placed,
        out_specs=(
            P(("rep", "shard"), None, None, None),
            P(("rep", "shard"), None, None, None),
            P(("rep", "shard"), None, None, None),
            P("shard", None),
            P("shard", None),
        ),
        check_vma=False,
    )
```

time: 153 us -> 138 us (0.902)
  the two profiles are of different devices: /device:TPU:0 before, /device:TPU:1 now
where the time goes in v3:
time: 138 us; the launch traced here: 135 us
  Pallas kernels  44.9 us (33%)
  starting transfers between devices  41.6 us (30%)
  waiting for transfers between devices  35.7 us (26%)
  local copies, waits for them, and re-layouts  10.3 us (7%)
  other arithmetic  1.63 us (1%)
    pallas_call x10, Pallas kernels, call(): pl.pallas_call(body, out_shape=outs, in_specs=specs, out_specs=jax.tree.m...  40.7 us
    ppermute x23, starting transfers between devices, flip(): lax.ppermute(value, axis, [(i, i ^ bit) for i in range(lax.axis_size(axis...  32.3 us
    ppermute x10, waiting for transfers between devices, hop(): return lax.ppermute(value, ('rep', 'shard'), pairs)  19.6 us
    ppermute x23, waiting for transfers between devices, flip(): lax.ppermute(value, axis, [(i, i ^ bit) for i in range(lax.axis_size(axis...  16.1 us
    ppermute x10, starting transfers between devices, hop(): return lax.ppermute(value, ('rep', 'shard'), pairs)  9.3 us
    unnamed x63, local copies, waits for them, and re-layouts  6.11 us
    pallas_call x1, Pallas kernels, place_grad(): pl.pallas_call(body, out_shape=shape((rows, chans), F32), in_specs=[pl.Bl...  4.15 us
  transfers between devices with their start and end apart: 33, of which 12 were waited for; matrix products, arithmetic and copies ran while one was open for 5% of the time, Pallas kernels for 22%

profile of v3, /device:TPU:1, one launch (start us, length us, event | category | flops | bytes accessed | tf_op | source)
XLA Modules:
  0.0 135.3 jit_solution(14146162740153116489)
XLA Ops:
  0.6 2.1 %collective-permute-start.1 = (bf16[64,1280]{1,0:T(8,128)(2,1)}, bf16[64,1280]{1,0:T(8,128)(2,1)S(1)}, u32[]{:S(2)}, u32[]{:S(2)}) collective-permute-start(bf16[64,1280]{1,0:T(8,128)(2,1)} %bitcast.50), channel_id=1, source_target_pairs={{0,2},{1,3},{2,0},{3,1},{4,6},{5,7},{6,4},{7,5},{8,10},{9,11},{10,... | collective-permute-start | bytes 491528 | tf_op jit(solution)/shard_map/ppermute | solution.py:493
  3.4 1.9 %turn_images.1 = bf16[4,160,256]{2,1,0:T(8,128)(2,1)} custom-call(s32[2]{0:T(128)} %pad_add_fusion.id_ref, bf16[256,640]{1,0:T(8,128)(2,1)} %bitcast.42), custom_call_target="tpu_custom_call" | custom-call | bytes 655360 | tf_op jit(solution)/shard_map/turn_images/pallas_call | solution.py:30
  6.9 1.4 %collective-permute-start.2 = (bf16[64,1280]{1,0:T(8,128)(2,1)S(1)}, bf16[64,1280]{1,0:T(8,128)(2,1)S(1)}, u32[]{:S(2)}, u32[]{:S(2)}) collective-permute-start(bf16[64,1280]{1,0:T(8,128)(2,1)S(1)} %collective-permute-done.1.refs_2_), channel_id=1, source_target_pairs={{0,1},{1,0},{2,3},{3,2},{4,5},{5,4},{6,7},{7,6},{8,9},{9,8},{10,11... | collective-permute-start | bytes 491528 | tf_op jit(solution)/shard_map/ppermute | solution.py:493
  8.3 1.7 %fusion.10 = (bf16[1,160,256]{2,1,0:T(8,128)(2,1)S(1)}, bf16[1,160,256]{2,1,0:T(8,128)(2,1)S(1)}, bf16[1,160,256]{2,1,0:T(8,128)(2,1)S(1)}, bf16[1,160,256]{2,1,0:T(8,128)(2,1)}) fusion(bf16[4,160,256]{2,1,0:T(8,128)(2,1)} %turn_images.1), kind=kLoop, calls=%fused_computation.31 | loop fusion | bytes 655360 | tf_op jit(solution)/shard_map/slice | solution.py:515
  10.1 2.1 %collective-permute-start.8 = (bf16[1,160,256]{2,1,0:T(8,128)(2,1)S(1)}, bf16[1,160,256]{2,1,0:T(8,128)(2,1)S(1)}, u32[]{:S(2)}, u32[]{:S(2)}) collective-permute-start(bf16[1,160,256]{2,1,0:T(8,128)(2,1)S(1)} %get-tuple-element.82), channel_id=1, source_target_pairs={{0,2},{1,3},{2,0},{3,1},{4,6},{5,7},{6,4},{7,5},{8,10},{9,11},{10,... | collective-permute-start | bytes 245768 | tf_op jit(solution)/shard_map/ppermute | solution.py:493
  13.5 2.3 %back_product.1 = (bf16[160,256]{1,0:T(8,128)(2,1)}, bf16[256,1280]{1,0:T(8,128)(2,1)}) custom-call(s32[2]{0:T(128)} %pad_add_fusion.id_ref, bf16[160,1280]{1,0:T(8,128)(2,1)} %refs_0_, bf16[64,1280]{1,0:T(8,128)(2,1)} %bitcast.52, bf16[64,1280]{1,0:T(8,128)(2,1)} %copy-done.15, bf16[64,1280]{1,0:T(8,128)(2,1)} %copy-done.14, bf16[64,1280]{1,0:T(8,128)(2,1)} %copy-done.16), custom_call_target="tpu_custom_call" | custom-call | flops 104857600 | bytes 655360 | tf_op jit(solution)/shard_map/back_product/pallas_call | solution.py:30
  17.3 1.8 %collective-permute-start.5 = (bf16[160,256]{1,0:T(8,128)(2,1)}, bf16[160,256]{1,0:T(8,128)(2,1)S(1)}, u32[]{:S(2)}, u32[]{:S(2)}) collective-permute-start(bf16[160,256]{1,0:T(8,128)(2,1)} %get-tuple-element.40.refs_4_), channel_id=1, source_target_pairs={{0,3},{1,2},{2,1},{3,0},{4,7},{5,6},{6,5},{7,4},{8,11},{9,10},{10,... | collective-permute-start | bytes 245768 | tf_op jit(solution)/shard_map/ppermute | solution.py:493
  19.7 4.1 %turn_filters.1 = (bf16[1440,640]{1,0:T(8,128)(2,1)}, bf16[640,1440]{1,0:T(8,128)(2,1)}) custom-call(bf16[1440,640]{1,0:T(8,128)(2,1)} %w_ref), custom_call_target="tpu_custom_call" | custom-call | bytes 5529600 | tf_op jit(solution)/shard_map/turn_filters/pallas_call | solution.py:30
  23.8 8.6 %forward.1 = (f32[2,800,256]{2,1,0:T(8,128)}, bf16[2,800,256]{2,1,0:T(8,128)(2,1)}, bf16[1440,1024]{1,0:T(8,128)(2,1)}) custom-call(s32[2]{0:T(128)} %pad_add_fusion.id_ref, bf16[640,1440]{1,0:T(8,128)(2,1)} %get-tuple-element.44.w_ref, bf16[1,160,256]{2,1,0:T(8,128)(2,1)} %get-tuple-element.84.refs_0_, bf16[1,160,256]{2,1,0:T(8,128)(2,1)} %copy-done.17, ...), custom_call_target="tpu_custom_call" | custom-call | flops 2642411520 | bytes 1966080 | tf_op jit(solution)/shard_map/forward/pallas_call | solution.py:30
  33.3 7.5 %filter_grad.1 = (bf16[1024,640]{1,0:T(8,128)(2,1)}, f32[2,904,128]{2,1,0:T(8,128)}, bf16[2,904,128]{2,1,0:T(8,128)(2,1)}, f32[2,896,128]{2,1,0:T(8,128)}, bf16[2,896,128]{2,1,0:T(8,128)(2,1)}) custom-call(s32[2]{0:T(128)} %pad_add_fusion.id_ref, bf16[1440,1024]{1,0:T(8,128)(2,1)} %get-tuple-element.45.p_ref, bf16[256,640]{1,0:T(8,128)(2,1)} %bitcast.55, ...), custom_call_target="tpu_custom_call" | custom-call | flops 1887436800 | bytes 5386240 | tf_op jit(solution)/shard_map/filter_grad/pallas_call | solution.py:30
  43.6 6.1 %image_grad.1 = bf16[4,160,256]{2,1,0:T(8,128)(2,1)} custom-call(s32[2]{0:T(128)} %pad_add_fusion.id_ref, bf16[1024,640]{1,0:T(8,128)(2,1)} %get-tuple-element.50.h_ref, bf16[1440,640]{1,0:T(8,128)(2,1)} %get-tuple-element.51.w_ref, bf16[1,160,256]{2,1,0:T(8,128)(2,1)} %get-tuple-element.84.refs_0_, bf16[1,160,256]{2,1,0:T(8,128)(2,1)} %copy-done.17, ...), custom_call_target="tpu_custom_call" | custom-call | flops 1887436800 | bytes 1310720 | tf_op jit(solution)/shard_map/image_grad/pallas_call | solution.py:30
  50.0 3.6 %collective-permute-done.12 = bf16[2,896,128]{2,1,0:T(8,128)(2,1)S(1)} collective-permute-done((bf16[2,896,128]{2,1,0:T(8,128)(2,1)}, bf16[2,896,128]{2,1,0:T(8,128)(2,1)S(1)}, u32[]{:S(2)}, u32[]{:S(2)}) %collective-permute-start.12) | collective-permute-done | bytes 458784 | tf_op jit(solution)/shard_map/ppermute | solution.py:525
  53.7 1.7 %collective-permute-start.14 = (bf16[896,128]{1,0:T(8,128)(2,1)S(1)}, bf16[896,128]{1,0:T(8,128)(2,1)S(1)}, u32[]{:S(2)}, u32[]{:S(2)}) collective-permute-start(bf16[896,128]{1,0:T(8,128)(2,1)S(1)} %fusion.3), channel_id=1, source_target_pairs={{0,8},{1,5},{2,10},{3,7},{4,12},{5,1},{6,14},{7,3},{8,0},{9,13},{1... | collective-permute-start | bytes 688136 | tf_op jit(solution)/shard_map/ppermute | solution.py:525
  57.3 1.5 %collective-permute-done.14 = bf16[896,128]{1,0:T(8,128)(2,1)S(1)} collective-permute-done((bf16[896,128]{1,0:T(8,128)(2,1)S(1)}, bf16[896,128]{1,0:T(8,128)(2,1)S(1)}, u32[]{:S(2)}, u32[]{:S(2)}) %collective-permute-start.14) | collective-permute-done | bytes 229408 | tf_op jit(solution)/shard_map/ppermute | solution.py:525
  58.9 5.4 %collective-permute-done.17.g_ref = bf16[1,800,256]{2,1,0:T(8,128)(2,1)S(1)} collective-permute-done((bf16[1,800,256]{2,1,0:T(8,128)(2,1)S(1)}, bf16[1,800,256]{2,1,0:T(8,128)(2,1)S(1)}, u32[]{:S(2)}, u32[]{:S(2)}) %collective-permute-start.17) | collective-permute-done | bytes 409632 | tf_op jit(solution)/shard_map/ppermute | solution.py:493
  65.0 3.3 %skip_grad_term.1 = (f32[2,400,128]{2,1,0:T(8,128)}, bf16[2,400,128]{2,1,0:T(8,128)(2,1)}) custom-call(s32[2]{0:T(128)} %pad_add_fusion.id_ref, f32[1,800,256]{2,1,0:T(8,128)} %slice.113.k_ref, bf16[1,800,256]{2,1,0:T(8,128)(2,1)} %copy-done.2, bf16[256,1280]{1,0:T(8,128)(2,1)} %get-tuple-element.58.c_ref, bf16[1,160,256]{2,1,0:T(8,128)(2,1)} %get-tuple-element.84.refs_0_, ...), custom_call_target="tpu_custom_call" | custom-call | flops 104857600 | bytes 819200 | tf_op jit(solution)/shard_map/skip_grad_term/pallas_call | solution.py:30
  68.3 2.9 %collective-permute-start.18 = (bf16[2,400,128]{2,1,0:T(8,128)(2,1)}, bf16[2,400,128]{2,1,0:T(8,128)(2,1)S(1)}, u32[]{:S(2)}, u32[]{:S(2)}) collective-permute-start(bf16[2,400,128]{2,1,0:T(8,128)(2,1)} %get-tuple-element.59), channel_id=1, source_target_pairs={{0,4},{1,9},{2,6},{3,11},{4,0},{5,13},{6,2},{7,15},{8,12},{9,1},{1... | collective-permute-start | bytes 614408 | tf_op jit(solution)/shard_map/ppermute | solution.py:525
  71.2 2.4 %finish_hidden.1 = (bf16[256,640]{1,0:T(8,128)(2,1)}, bf16[64,640]{1,0:T(8,128)(2,1)}) custom-call(bf16[256,640]{1,0:T(8,128)(2,1)} %bitcast.43, f32[1,800,256]{2,1,0:T(8,128)} %slice.113.k_ref, bf16[1,800,256]{2,1,0:T(8,128)(2,1)} %copy-done.2), custom_call_target="tpu_custom_call" | custom-call | flops 20971520 | bytes 1638400 | tf_op jit(solution)/shard_map/finish_hidden/pallas_call | solution.py:30
  75.4 5.9 %collective-permute-start.20 = (bf16[1,160,256]{2,1,0:T(8,128)(2,1)S(1)}, bf16[1,160,256]{2,1,0:T(8,128)(2,1)S(1)}, u32[]{:S(2)}, u32[]{:S(2)}) collective-permute-start(bf16[1,160,256]{2,1,0:T(8,128)(2,1)S(1)} %get-tuple-element.79), channel_id=1, source_target_pairs={{0,1},{1,0},{2,3},{3,2},{4,5},{5,4},{6,7},{7,6},{8,9},{9,8},{10,11... | collective-permute-start | bytes 245768 | tf_op jit(solution)/shard_map/ppermute | solution.py:493
  82.9 2.3 %collective-permute-start.29 = (bf16[896,128]{1,0:T(8,128)(2,1)S(1)}, bf16[896,128]{1,0:T(8,128)(2,1)S(1)}, u32[]{:S(2)}, u32[]{:S(2)}) collective-permute-start(bf16[896,128]{1,0:T(8,128)(2,1)S(1)} %fusion.1), channel_id=1, source_target_pairs={{0,16},{4,20},{8,24},{12,28},{16,0},{20,4},{24,8},{28,12},{1,17},{... | collective-permute-start | bytes 688136 | tf_op jit(solution)/shard_map/ppermute | solution.py:493
  85.4 1.8 %collective-permute-done.22.refs_3_ = bf16[1,160,256]{2,1,0:T(8,128)(2,1)S(1)} collective-permute-done((bf16[1,160,256]{2,1,0:T(8,128)(2,1)S(1)}, bf16[1,160,256]{2,1,0:T(8,128)(2,1)S(1)}, u32[]{:S(2)}, u32[]{:S(2)}) %collective-permute-start.22) | collective-permute-done | bytes 81952 | tf_op jit(solution)/shard_map/ppermute | solution.py:493
  87.9 2.0 %finish_images.1 = bf16[256,640]{1,0:T(8,128)(2,1)} custom-call(s32[2]{0:T(128)} %pad_add_fusion.id_ref, bf16[1,160,256]{2,1,0:T(8,128)(2,1)} %get-tuple-element.80.refs_0_, bf16[1,160,256]{2,1,0:T(8,128)(2,1)} %copy-done.20, bf16[1,160,256]{2,1,0:T(8,128)(2,1)} %copy-done.21, bf16[1,160,256]{2,1,0:T(8,128)(2,1)} %copy-done.22), custom_call_target="tpu_custom_call" | custom-call | bytes 655360 | tf_op jit(solution)/shard_map/finish_images/pallas_call | solution.py:30
  89.9 2.7 %collective-permute-start.30 = (bf16[400,128]{1,0:T(8,128)(2,1)S(1)}, bf16[400,128]{1,0:T(8,128)(2,1)S(1)}, u32[]{:S(2)}, u32[]{:S(2)}) collective-permute-start(bf16[400,128]{1,0:T(8,128)(2,1)S(1)} %fusion.4), channel_id=1, source_target_pairs={{0,16},{4,20},{8,24},{12,28},{16,0},{20,4},{24,8},{28,12},{1,17},{... | collective-permute-start | bytes 307208 | tf_op jit(solution)/shard_map/ppermute | solution.py:493
  92.5 5.9 %collective-permute-done.29 = bf16[896,128]{1,0:T(8,128)(2,1)S(1)} collective-permute-done((bf16[896,128]{1,0:T(8,128)(2,1)S(1)}, bf16[896,128]{1,0:T(8,128)(2,1)S(1)}, u32[]{:S(2)}, u32[]{:S(2)}) %collective-permute-start.29) | collective-permute-done | bytes 229408 | tf_op jit(solution)/shard_map/ppermute | solution.py:493
  98.5 2.1 %collective-permute-done.30 = bf16[400,128]{1,0:T(8,128)(2,1)S(1)} collective-permute-done((bf16[400,128]{1,0:T(8,128)(2,1)S(1)}, bf16[400,128]{1,0:T(8,128)(2,1)S(1)}, u32[]{:S(2)}, u32[]{:S(2)}) %collective-permute-start.30) | collective-permute-done | bytes 102432 | tf_op jit(solution)/shard_map/ppermute | solution.py:493
  101.5 5.6 %collective-permute-done.31 = bf16[1296,128]{1,0:T(8,128)(2,1)S(1)} collective-permute-done((bf16[1296,128]{1,0:T(8,128)(2,1)S(1)}, bf16[1296,128]{1,0:T(8,128)(2,1)S(1)}, u32[]{:S(2)}, u32[]{:S(2)}) %collective-permute-start.31) | collective-permute-done | bytes 331808 | tf_op jit(solution)/shard_map/ppermute | solution.py:525
  107.2 7.1 %collective-permute-start.23 = (bf16[160,1280]{1,0:T(8,128)(2,1)S(1)}, bf16[160,1280]{1,0:T(8,128)(2,1)S(1)}, u32[]{:S(2)}, u32[]{:S(2)}) collective-permute-start(bf16[160,1280]{1,0:T(8,128)(2,1)S(1)} %copy-done.3), channel_id=1, source_target_pairs={{0,1},{1,0},{2,3},{3,2},{4,5},{5,4},{6,7},{7,6},{8,9},{9,8},{10,11... | collective-permute-start | bytes 1228808 | tf_op jit(solution)/shard_map/ppermute | solution.py:493
  114.5 1.7 %collective-permute-start.27 = (bf16[904,128]{1,0:T(8,128)(2,1)S(1)}, bf16[904,128]{1,0:T(8,128)(2,1)S(1)}, u32[]{:S(2)}, u32[]{:S(2)}) collective-permute-start(bf16[904,128]{1,0:T(8,128)(2,1)S(1)} %add_convert_fusion), channel_id=1, source_target_pairs={{0,8},{1,5},{2,10},{3,7},{4,12},{5,1},{6,14},{7,3},{8,0},{9,13},{1... | collective-permute-start | bytes 694280 | tf_op jit(solution)/shard_map/ppermute | solution.py:525
  116.2 6.2 %collective-permute-done.27 = bf16[904,128]{1,0:T(8,128)(2,1)S(1)} collective-permute-done((bf16[904,128]{1,0:T(8,128)(2,1)S(1)}, bf16[904,128]{1,0:T(8,128)(2,1)S(1)}, u32[]{:S(2)}, u32[]{:S(2)}) %collective-permute-start.27) | collective-permute-done | bytes 231456 | tf_op jit(solution)/shard_map/ppermute | solution.py:525
  123.5 2.6 %project.1 = bf16[64,1280]{1,0:T(8,128)(2,1)} custom-call(s32[2]{0:T(128)} %pad_add_fusion.id_ref, bf16[64,640]{1,0:T(8,128)(2,1)} %get-tuple-element.70.s_ref, bf16[160,1280]{1,0:T(8,128)(2,1)} %refs_0_, bf16[160,1280]{1,0:T(8,128)(2,1)} %copy-done.11, bf16[160,1280]{1,0:T(8,128)(2,1)} %copy-done.10, bf16[160,1280]{1,0:T(8,128)(2,1)} %copy-done.12), custom_call_target="tpu_custom_call" | custom-call | flops 104857600 | bytes 1638400 | tf_op jit(solution)/shard_map/project/pallas_call | solution.py:30
  128.5 1.7 %collective-permute-done.28.refs_1_ = bf16[2,904,128]{2,1,0:T(8,128)(2,1)S(1)} collective-permute-done((bf16[2,904,128]{2,1,0:T(8,128)(2,1)S(1)}, bf16[2,904,128]{2,1,0:T(8,128)(2,1)S(1)}, u32[]{:S(2)}, u32[]{:S(2)}) %collective-permute-start.28) | collective-permute-done | bytes 462880 | tf_op jit(solution)/shard_map/ppermute | solution.py:525
  131.0 4.2 %place_grad.1 = f32[1440,640]{1,0:T(8,128)} custom-call(s32[2]{0:T(128)} %pad_add_fusion.id_ref, bf16[2,904,128]{2,1,0:T(8,128)(2,1)} %copy-done.1, bf16[2,904,128]{2,1,0:T(8,128)(2,1)} %copy-done.8, bf16[2,1296,128]{2,1,0:T(8,128)(2,1)} %copy-done, bf16[2,1296,128]{2,1,0:T(8,128)(2,1)} %copy-done.5), custom_call_target="tpu_custom_call" | custom-call | bytes 5529600 | tf_op jit(solution)/shard_map/place_grad/pallas_call | solution.py:321
  (135 shorter events, 22.0 us)
Async XLA Ops:
  0.6 6.2 %collective-permute-start.1 = (bf16[64,1280]{1,0:T(8,128)(2,1)}, bf16[64,1280]{1,0:T(8,128)(2,1)S(1)}, u32[]{:S(2)}, u32[]{:S(2)}) collective-permute-start(bf16[64,1280]{1,0:T(8,128)(2,1)} %bitcast.50), channel_id=1, source_target_pairs={{0,2},{1,3},{2,0},{3,1},{4,6},{5,7},{6,4},{7,5},{8,10},{9,11},{10,... | collective-permute-start | bytes 491528 | tf_op jit(solution)/shard_map/ppermute | solution.py:493
  5.3 13.9 %collective-permute-start.6 = (bf16[256,640]{1,0:T(8,128)(2,1)}, bf16[256,640]{1,0:T(8,128)(2,1)S(1)}, u32[]{:S(2)}, u32[]{:S(2)}) collective-permute-start(bf16[256,640]{1,0:T(8,128)(2,1)} %bitcast.54), channel_id=1, source_target_pairs={{0,2},{1,3},{2,0},{3,1},{4,6},{5,7},{6,4},{7,5},{8,10},{9,11},{10,... | collective-permute-start | bytes 983048 | tf_op jit(solution)/shard_map/ppermute | solution.py:493
  5.3 6.8 %collective-permute-start = (bf16[64,1280]{1,0:T(8,128)(2,1)}, bf16[64,1280]{1,0:T(8,128)(2,1)S(1)}, u32[]{:S(2)}, u32[]{:S(2)}) collective-permute-start(bf16[64,1280]{1,0:T(8,128)(2,1)} %bitcast.51), channel_id=1, source_target_pairs={{0,1},{1,0},{2,3},{3,2},{4,5},{5,4},{6,7},{7,6},{8,9},{9,8},{10,11... | collective-permute-start | bytes 491528 | tf_op jit(solution)/shard_map/ppermute | solution.py:493
  6.9 5.7 %collective-permute-start.2 = (bf16[64,1280]{1,0:T(8,128)(2,1)S(1)}, bf16[64,1280]{1,0:T(8,128)(2,1)S(1)}, u32[]{:S(2)}, u32[]{:S(2)}) collective-permute-start(bf16[64,1280]{1,0:T(8,128)(2,1)S(1)} %collective-permute-done.1.refs_2_), channel_id=1, source_target_pairs={{0,1},{1,0},{2,3},{3,2},{4,5},{5,4},{6,7},{7,6},{8,9},{9,8},{10,11... | collective-permute-start | bytes 491528 | tf_op jit(solution)/shard_map/ppermute | solution.py:493
  10.0 6.6 %collective-permute-start.7 = (bf16[1,160,256]{2,1,0:T(8,128)(2,1)S(1)}, bf16[1,160,256]{2,1,0:T(8,128)(2,1)S(1)}, u32[]{:S(2)}, u32[]{:S(2)}) collective-permute-start(bf16[1,160,256]{2,1,0:T(8,128)(2,1)S(1)} %get-tuple-element.83), channel_id=1, source_target_pairs={{0,1},{1,0},{2,3},{3,2},{4,5},{5,4},{6,7},{7,6},{8,9},{9,8},{10,11... | collective-permute-start | bytes 245768 | tf_op jit(solution)/shard_map/ppermute | solution.py:493
  10.1 7.3 %collective-permute-start.8 = (bf16[1,160,256]{2,1,0:T(8,128)(2,1)S(1)}, bf16[1,160,256]{2,1,0:T(8,128)(2,1)S(1)}, u32[]{:S(2)}, u32[]{:S(2)}) collective-permute-start(bf16[1,160,256]{2,1,0:T(8,128)(2,1)S(1)} %get-tuple-element.82), channel_id=1, source_target_pairs={{0,2},{1,3},{2,0},{3,1},{4,6},{5,7},{6,4},{7,5},{8,10},{9,11},{10,... | collective-permute-start | bytes 245768 | tf_op jit(solution)/shard_map/ppermute | solution.py:493
  12.2 6.9 %collective-permute-start.9 = (bf16[1,160,256]{2,1,0:T(8,128)(2,1)S(1)}, bf16[1,160,256]{2,1,0:T(8,128)(2,1)S(1)}, u32[]{:S(2)}, u32[]{:S(2)}) collective-permute-start(bf16[1,160,256]{2,1,0:T(8,128)(2,1)S(1)} %get-tuple-element.81), channel_id=1, source_target_pairs={{0,3},{1,2},{2,1},{3,0},{4,7},{5,6},{6,5},{7,4},{8,11},{9,10},{10,... | collective-permute-start | bytes 245768 | tf_op jit(solution)/shard_map/ppermute | solution.py:493
  15.8 7.9 %collective-permute-start.3 = (bf16[160,256]{1,0:T(8,128)(2,1)}, bf16[160,256]{1,0:T(8,128)(2,1)S(1)}, u32[]{:S(2)}, u32[]{:S(2)}) collective-permute-start(bf16[160,256]{1,0:T(8,128)(2,1)} %get-tuple-element.40.refs_4_), channel_id=1, source_target_pairs={{0,1},{1,0},{2,3},{3,2},{4,5},{5,4},{6,7},{7,6},{8,9},{9,8},{10,11... | collective-permute-start | bytes 245768 | tf_op jit(solution)/shard_map/ppermute | solution.py:493
  16.6 7.2 %collective-permute-start.4 = (bf16[160,256]{1,0:T(8,128)(2,1)}, bf16[160,256]{1,0:T(8,128)(2,1)S(1)}, u32[]{:S(2)}, u32[]{:S(2)}) collective-permute-start(bf16[160,256]{1,0:T(8,128)(2,1)} %get-tuple-element.40.refs_4_), channel_id=1, source_target_pairs={{0,2},{1,3},{2,0},{3,1},{4,6},{5,7},{6,4},{7,5},{8,10},{9,11},{10,... | collective-permute-start | bytes 245768 | tf_op jit(solution)/shard_map/ppermute | solution.py:493
  17.3 6.4 %collective-permute-start.5 = (bf16[160,256]{1,0:T(8,128)(2,1)}, bf16[160,256]{1,0:T(8,128)(2,1)S(1)}, u32[]{:S(2)}, u32[]{:S(2)}) collective-permute-start(bf16[160,256]{1,0:T(8,128)(2,1)} %get-tuple-element.40.refs_4_), channel_id=1, source_target_pairs={{0,3},{1,2},{2,1},{3,0},{4,7},{5,6},{6,5},{7,4},{8,11},{9,10},{10,... | collective-permute-start | bytes 245768 | tf_op jit(solution)/shard_map/ppermute | solution.py:493
  19.1 13.3 %collective-permute-start.10 = (bf16[256,640]{1,0:T(8,128)(2,1)S(1)}, bf16[256,640]{1,0:T(8,128)(2,1)S(1)}, u32[]{:S(2)}, u32[]{:S(2)}) collective-permute-start(bf16[256,640]{1,0:T(8,128)(2,1)S(1)} %bitcast.56), channel_id=1, source_target_pairs={{0,1},{1,0},{2,3},{3,2},{4,5},{5,4},{6,7},{7,6},{8,9},{9,8},{10,11... | collective-permute-start | bytes 983048 | tf_op jit(solution)/shard_map/ppermute | solution.py:493
  19.2 13.2 %collective-permute-start.11 = (bf16[256,640]{1,0:T(8,128)(2,1)S(1)}, bf16[256,640]{1,0:T(8,128)(2,1)S(1)}, u32[]{:S(2)}, u32[]{:S(2)}) collective-permute-start(bf16[256,640]{1,0:T(8,128)(2,1)S(1)} %collective-permute-done.6.refs_2_), channel_id=1, source_target_pairs={{0,1},{1,0},{2,3},{3,2},{4,5},{5,4},{6,7},{7,6},{8,9},{9,8},{10,11... | collective-permute-start | bytes 983048 | tf_op jit(solution)/shard_map/ppermute | solution.py:493
  40.7 8.9 %collective-permute-start.13 = (bf16[2,904,128]{2,1,0:T(8,128)(2,1)}, bf16[2,904,128]{2,1,0:T(8,128)(2,1)S(1)}, u32[]{:S(2)}, u32[]{:S(2)}) collective-permute-start(bf16[2,904,128]{2,1,0:T(8,128)(2,1)} %get-tuple-element.49), channel_id=1, source_target_pairs={{0,4},{1,9},{2,6},{3,11},{4,0},{5,13},{6,2},{7,15},{8,12},{9,1},{1... | collective-permute-start | bytes 1388552 | tf_op jit(solution)/shard_map/ppermute | solution.py:525
  41.9 13.4 %collective-permute-start.16 = (bf16[2,800,256]{2,1,0:T(8,128)(2,1)S(1)}, bf16[2,800,256]{2,1,0:T(8,128)(2,1)S(1)}, u32[]{:S(2)}, u32[]{:S(2)}) collective-permute-start(bf16[2,800,256]{2,1,0:T(8,128)(2,1)S(1)} %copy-done.23), channel_id=1, source_target_pairs={{0,1},{1,0},{2,3},{3,2},{4,5},{5,4},{6,7},{7,6},{8,9},{9,8},{10,11... | collective-permute-start | bytes 2457608 | tf_op jit(solution)/shard_map/ppermute | solution.py:493
  42.3 11.4 %collective-permute-start.12 = (bf16[2,896,128]{2,1,0:T(8,128)(2,1)}, bf16[2,896,128]{2,1,0:T(8,128)(2,1)S(1)}, u32[]{:S(2)}, u32[]{:S(2)}) collective-permute-start(bf16[2,896,128]{2,1,0:T(8,128)(2,1)} %get-tuple-element.47), channel_id=1, source_target_pairs={{0,4},{1,9},{2,6},{3,11},{4,0},{5,13},{6,2},{7,15},{8,12},{9,1},{1... | collective-permute-start | bytes 1376264 | tf_op jit(solution)/shard_map/ppermute | solution.py:525
  49.7 7.4 %collective-permute-start.15 = (bf16[904,128]{1,0:T(8,128)(2,1)S(1)}, bf16[904,128]{1,0:T(8,128)(2,1)S(1)}, u32[]{:S(2)}, u32[]{:S(2)}) collective-permute-start(bf16[904,128]{1,0:T(8,128)(2,1)S(1)} %fusion.2), channel_id=1, source_target_pairs={{0,8},{1,5},{2,10},{3,7},{4,12},{5,1},{6,14},{7,3},{8,0},{9,13},{1... | collective-permute-start | bytes 694280 | tf_op jit(solution)/shard_map/ppermute | solution.py:525
  53.7 5.1 %collective-permute-start.14 = (bf16[896,128]{1,0:T(8,128)(2,1)S(1)}, bf16[896,128]{1,0:T(8,128)(2,1)S(1)}, u32[]{:S(2)}, u32[]{:S(2)}) collective-permute-start(bf16[896,128]{1,0:T(8,128)(2,1)S(1)} %fusion.3), channel_id=1, source_target_pairs={{0,8},{1,5},{2,10},{3,7},{4,12},{5,1},{6,14},{7,3},{8,0},{9,13},{1... | collective-permute-start | bytes 688136 | tf_op jit(solution)/shard_map/ppermute | solution.py:525
  56.5 7.7 %collective-permute-start.17 = (bf16[1,800,256]{2,1,0:T(8,128)(2,1)S(1)}, bf16[1,800,256]{2,1,0:T(8,128)(2,1)S(1)}, u32[]{:S(2)}, u32[]{:S(2)}) collective-permute-start(bf16[1,800,256]{2,1,0:T(8,128)(2,1)S(1)} %slice.138), channel_id=1, source_target_pairs={{0,2},{1,3},{2,0},{3,1},{4,6},{5,7},{6,4},{7,5},{8,10},{9,11},{10,... | collective-permute-start | bytes 1228808 | tf_op jit(solution)/shard_map/ppermute | solution.py:493
  68.3 6.2 %collective-permute-start.18 = (bf16[2,400,128]{2,1,0:T(8,128)(2,1)}, bf16[2,400,128]{2,1,0:T(8,128)(2,1)S(1)}, u32[]{:S(2)}, u32[]{:S(2)}) collective-permute-start(bf16[2,400,128]{2,1,0:T(8,128)(2,1)} %get-tuple-element.59), channel_id=1, source_target_pairs={{0,4},{1,9},{2,6},{3,11},{4,0},{5,13},{6,2},{7,15},{8,12},{9,1},{1... | collective-permute-start | bytes 614408 | tf_op jit(solution)/shard_map/ppermute | solution.py:525
  74.6 15.2 %collective-permute-start.19 = (bf16[400,128]{1,0:T(8,128)(2,1)S(1)}, bf16[400,128]{1,0:T(8,128)(2,1)S(1)}, u32[]{:S(2)}, u32[]{:S(2)}) collective-permute-start(bf16[400,128]{1,0:T(8,128)(2,1)S(1)} %fusion.5), channel_id=1, source_target_pairs={{0,8},{1,5},{2,10},{3,7},{4,12},{5,1},{6,14},{7,3},{8,0},{9,13},{1... | collective-permute-start | bytes 307208 | tf_op jit(solution)/shard_map/ppermute | solution.py:525
  75.4 9.9 %collective-permute-start.20 = (bf16[1,160,256]{2,1,0:T(8,128)(2,1)S(1)}, bf16[1,160,256]{2,1,0:T(8,128)(2,1)S(1)}, u32[]{:S(2)}, u32[]{:S(2)}) collective-permute-start(bf16[1,160,256]{2,1,0:T(8,128)(2,1)S(1)} %get-tuple-element.79), channel_id=1, source_target_pairs={{0,1},{1,0},{2,3},{3,2},{4,5},{5,4},{6,7},{7,6},{8,9},{9,8},{10,11... | collective-permute-start | bytes 245768 | tf_op jit(solution)/shard_map/ppermute | solution.py:493
  81.9 5.3 %collective-permute-start.22 = (bf16[1,160,256]{2,1,0:T(8,128)(2,1)S(1)}, bf16[1,160,256]{2,1,0:T(8,128)(2,1)S(1)}, u32[]{:S(2)}, u32[]{:S(2)}) collective-permute-start(bf16[1,160,256]{2,1,0:T(8,128)(2,1)S(1)} %get-tuple-element.77), channel_id=1, source_target_pairs={{0,3},{1,2},{2,1},{3,0},{4,7},{5,6},{6,5},{7,4},{8,11},{9,10},{10,... | collective-permute-start | bytes 245768 | tf_op jit(solution)/shard_map/ppermute | solution.py:493
  82.9 15.5 %collective-permute-start.29 = (bf16[896,128]{1,0:T(8,128)(2,1)S(1)}, bf16[896,128]{1,0:T(8,128)(2,1)S(1)}, u32[]{:S(2)}, u32[]{:S(2)}) collective-permute-start(bf16[896,128]{1,0:T(8,128)(2,1)S(1)} %fusion.1), channel_id=1, source_target_pairs={{0,16},{4,20},{8,24},{12,28},{16,0},{20,4},{24,8},{28,12},{1,17},{... | collective-permute-start | bytes 688136 | tf_op jit(solution)/shard_map/ppermute | solution.py:493
  89.9 10.8 %collective-permute-start.30 = (bf16[400,128]{1,0:T(8,128)(2,1)S(1)}, bf16[400,128]{1,0:T(8,128)(2,1)S(1)}, u32[]{:S(2)}, u32[]{:S(2)}) collective-permute-start(bf16[400,128]{1,0:T(8,128)(2,1)S(1)} %fusion.4), channel_id=1, source_target_pairs={{0,16},{4,20},{8,24},{12,28},{16,0},{20,4},{24,8},{28,12},{1,17},{... | collective-permute-start | bytes 307208 | tf_op jit(solution)/shard_map/ppermute | solution.py:493
  100.7 6.3 %collective-permute-start.31 = (bf16[1296,128]{1,0:T(8,128)(2,1)S(1)}, bf16[1296,128]{1,0:T(8,128)(2,1)S(1)}, u32[]{:S(2)}, u32[]{:S(2)}) collective-permute-start(bf16[1296,128]{1,0:T(8,128)(2,1)S(1)} %get-tuple-element.76), channel_id=1, source_target_pairs={{0,8},{1,5},{2,10},{3,7},{4,12},{5,1},{6,14},{7,3},{8,0},{9,13},{1... | collective-permute-start | bytes 995336 | tf_op jit(solution)/shard_map/ppermute | solution.py:525
  100.8 13.5 %collective-permute-start.24 = (bf16[160,1280]{1,0:T(8,128)(2,1)S(1)}, bf16[160,1280]{1,0:T(8,128)(2,1)S(1)}, u32[]{:S(2)}, u32[]{:S(2)}) collective-permute-start(bf16[160,1280]{1,0:T(8,128)(2,1)S(1)} %copy-done.3), channel_id=1, source_target_pairs={{0,2},{1,3},{2,0},{3,1},{4,6},{5,7},{6,4},{7,5},{8,10},{9,11},{10,... | collective-permute-start | bytes 1228808 | tf_op jit(solution)/shard_map/ppermute | solution.py:493
  101.5 12.9 %collective-permute-start.26 = (bf16[904,128]{1,0:T(8,128)(2,1)S(1)}, bf16[904,128]{1,0:T(8,128)(2,1)S(1)}, u32[]{:S(2)}, u32[]{:S(2)}) collective-permute-start(bf16[904,128]{1,0:T(8,128)(2,1)S(1)} %fusion), channel_id=1, source_target_pairs={{0,16},{4,20},{8,24},{12,28},{16,0},{20,4},{24,8},{28,12},{1,17},{... | collective-permute-start | bytes 694280 | tf_op jit(solution)/shard_map/ppermute | solution.py:493
  107.1 19.1 %collective-permute-start.32 = (bf16[2,1296,128]{2,1,0:T(8,128)(2,1)S(1)}, bf16[2,1296,128]{2,1,0:T(8,128)(2,1)S(1)}, u32[]{:S(2)}, u32[]{:S(2)}) collective-permute-start(bf16[2,1296,128]{2,1,0:T(8,128)(2,1)S(1)} %pad_maximum_fusion.refs_2_), channel_id=1, source_target_pairs={{0,4},{1,9},{2,6},{3,11},{4,0},{5,13},{6,2},{7,15},{8,12},{9,1},{1... | collective-permute-start | bytes 1990664 | tf_op jit(solution)/shard_map/ppermute | solution.py:525
  107.2 15.3 %collective-permute-start.23 = (bf16[160,1280]{1,0:T(8,128)(2,1)S(1)}, bf16[160,1280]{1,0:T(8,128)(2,1)S(1)}, u32[]{:S(2)}, u32[]{:S(2)}) collective-permute-start(bf16[160,1280]{1,0:T(8,128)(2,1)S(1)} %copy-done.3), channel_id=1, source_target_pairs={{0,1},{1,0},{2,3},{3,2},{4,5},{5,4},{6,7},{7,6},{8,9},{9,8},{10,11... | collective-permute-start | bytes 1228808 | tf_op jit(solution)/shard_map/ppermute | solution.py:493
  114.3 8.2 %collective-permute-start.25 = (bf16[160,1280]{1,0:T(8,128)(2,1)S(1)}, bf16[160,1280]{1,0:T(8,128)(2,1)S(1)}, u32[]{:S(2)}, u32[]{:S(2)}) collective-permute-start(bf16[160,1280]{1,0:T(8,128)(2,1)S(1)} %collective-permute-done.24.refs_2_), channel_id=1, source_target_pairs={{0,1},{1,0},{2,3},{3,2},{4,5},{5,4},{6,7},{7,6},{8,9},{9,8},{10,11... | collective-permute-start | bytes 1228808 | tf_op jit(solution)/shard_map/ppermute | solution.py:493
  114.5 7.9 %collective-permute-start.27 = (bf16[904,128]{1,0:T(8,128)(2,1)S(1)}, bf16[904,128]{1,0:T(8,128)(2,1)S(1)}, u32[]{:S(2)}, u32[]{:S(2)}) collective-permute-start(bf16[904,128]{1,0:T(8,128)(2,1)S(1)} %add_convert_fusion), channel_id=1, source_target_pairs={{0,8},{1,5},{2,10},{3,7},{4,12},{5,1},{6,14},{7,3},{8,0},{9,13},{1... | collective-permute-start | bytes 694280 | tf_op jit(solution)/shard_map/ppermute | solution.py:525
  122.5 7.7 %collective-permute-start.28 = (bf16[2,904,128]{2,1,0:T(8,128)(2,1)S(1)}, bf16[2,904,128]{2,1,0:T(8,128)(2,1)S(1)}, u32[]{:S(2)}, u32[]{:S(2)}) collective-permute-start(bf16[2,904,128]{2,1,0:T(8,128)(2,1)S(1)} %pad_maximum_fusion.1.refs_0_), channel_id=1, source_target_pairs={{0,4},{1,9},{2,6},{3,11},{4,0},{5,13},{6,2},{7,15},{8,12},{9,1},{1... | collective-permute-start | bytes 1388552 | tf_op jit(solution)/shard_map/ppermute | solution.py:525
  (32 other events, 200.3 us)

commit v4 on v3

v4 whole, which is shorter than its diff:
```python
import math

import jax
import jax.numpy as jnp
from jax import lax
from jax.experimental import pallas as pl
from jax.experimental.pallas import tpu as pltpu
from jax.sharding import PartitionSpec as P

BF = jnp.bfloat16
F32 = jnp.float32
VMEM_LIMIT = 56 << 20
LANES = 128
BLOCK = 4


def dot(a, b, dims=((1,), (0,))):
    return lax.dot_general(a, b, (dims, ((), ())), preferred_element_type=F32)


NT = ((1,), (1,))
TN = ((0,), (0,))


def call(name, body, outs, scratch, flops, moved, args, scalars=0):
    specs = [
        pl.BlockSpec(memory_space=pltpu.SMEM if i < scalars else pltpu.VMEM)
        for i in range(len(args))
    ]
    return pl.pallas_call(
        body,
        out_shape=outs,
        in_specs=specs,
        out_specs=jax.tree.map(lambda _: pl.BlockSpec(memory_space=pltpu.VMEM), outs),
        scratch_shapes=scratch,
        compiler_params=pltpu.CompilerParams(vmem_limit_bytes=VMEM_LIMIT),
        cost_estimate=pl.CostEstimate(flops=flops, bytes_accessed=moved, transcendentals=0),
        name=name,
    )(*args)


def shape(dims, kind):
    return jax.ShapeDtypeStruct(dims, kind)


def rows_at(start, size, step):
    return pl.ds(pl.multiple_of(start, step), size)


def round_up(value, step):
    return -(-value // step) * step


def turn_filters(conv_weight):
    rows, chans = conv_weight.shape
    own = rows // 9

    def body(w_ref, o_ref, t_ref, wide):
        for k in range(chans // LANES):
            cols = slice(k * LANES, (k + 1) * LANES)
            wide[k] = w_ref[:, cols].astype(F32)
            for t in range(9):
                piece = wide[k, pl.ds(t, own, stride=9), :]
                o_ref[t * own : (t + 1) * own, cols] = piece.astype(BF)
        t_ref[...] = o_ref[...].T

    return call(
        "turn_filters",
        body,
        [shape((rows, chans), BF), shape((chans, rows), BF)],
        [pltpu.VMEM((chans // LANES, rows, LANES), F32)],
        0,
        6 * rows * chans,
        [conv_weight],
    )


def col_sets(chans):
    rest = (chans - BLOCK * LANES) // BLOCK
    return BLOCK * LANES, rest


def turn_images(ids, source, group, own):
    pixels, chans = source.shape

    def body(id_ref, i_ref, *refs):
        wide = refs[group]
        wide[...] = i_ref[...].astype(F32).T
        for j in range(group):
            refs[j][...] = wide[rows_at((id_ref[0] ^ j) * own, own, 8), :].astype(BF)

    return call(
        "turn_images",
        body,
        [shape((own, pixels), BF)] * group,
        [pltpu.VMEM((chans, pixels), F32)],
        0,
        4 * pixels * chans,
        [ids, source],
        1,
    )


def back_product(ids, cots, skip_weight):
    few, wide_chans = cots[0].shape
    own = skip_weight.shape[0]
    group = len(cots)

    def body(id_ref, s_ref, *refs):
        o_ref, held = refs[group:]
        for j in range(group):
            held[rows_at((id_ref[0] ^ j) * few, few, 16), :] = refs[j][...]
        o_ref[...] = dot(s_ref[...], held[...], NT).astype(BF)

    return call(
        "back_product",
        body,
        [shape((own, group * few), BF), shape((group * few, wide_chans), BF)],
        [],
        2 * own * group * few * wide_chans,
        group * few * wide_chans * 2,
        [ids, skip_weight, *cots],
        1,
    )


def pixel_parts(pixels, width):
    at = lax.broadcasted_iota(jnp.int32, (1, pixels), 1)
    return at // width, at % width


def neighbours(value, pixels, width):
    height = pixels // width
    y, x = pixel_parts(pixels, width)
    for dy in range(3):
        for dx in range(3):
            off = (dy - 1) * width + dx - 1
            if off == 0:
                yield value
                continue
            inside = (y >= 1 - dy) & (y < height + 1 - dy) & (x >= 1 - dx) & (x < width + 1 - dx)
            yield jnp.where(inside, pltpu.roll(value, -off % pixels, 1), 0.0)


def spread_matrix(few_all, few, pixels, width):
    y, x = pixel_parts(pixels, width)
    coarse = (y // 2) * (width // 2) + x // 2
    even = (y % 2 == 0) & (x % 2 == 0)
    row = lax.broadcasted_iota(jnp.int32, (few_all, pixels), 0)
    for d in range(few_all // few):
        yield jnp.where(even & (row == d * few + coarse), 1.0, 0.0).astype(BF)


def spread_rows(few_all, few, pixels, width, d):
    at = lax.broadcasted_iota(jnp.int32, (pixels, 1), 0)
    y, x = at // width, at % width
    coarse = jnp.where((y % 2 == 0) & (x % 2 == 0), (y // 2) * (width // 2) + x // 2, -few_all)
    col = lax.broadcasted_iota(jnp.int32, (pixels, few_all), 1)
    return jnp.where(col == d * few + coarse, 1.0, 0.0).astype(BF)


def make_patches(own_images, width):
    group = len(own_images)
    own, pixels = own_images[0].shape

    def body(*refs):
        patch = refs[group]
        for m in range(group):
            v = refs[m][...].astype(F32)
            value = (v / (1.0 + jnp.exp(-v))).astype(BF).astype(F32)
            here = slice(m * pixels, (m + 1) * pixels)
            for t, moved in enumerate(neighbours(value, pixels, width)):
                patch[t * own : (t + 1) * own, here] = moved.astype(BF)

    return call(
        "make_patches",
        body,
        shape((9 * own, group * pixels), BF),
        [],
        0,
        20 * own * group * pixels,
        own_images,
    )


def forward(ids, patch, w_turned, pixels, width, few):
    chans, rows = w_turned.shape
    group, own = patch.shape[1] // pixels, rows // 9
    few_all = group * few

    def body(id_ref, w_ref, p_ref, *refs):
        keep_refs = refs[: group // 2]
        send_ref, sums, moves = refs[group // 2 :]
        for m in range(group):
            here = slice(m * pixels, (m + 1) * pixels)
            moves[here] = spread_rows(few_all, few, pixels, width, id_ref[0] ^ m)
        out = dot(w_ref[...], p_ref[...])
        for m in range(group):
            piece = out[:, m * pixels : (m + 1) * pixels]
            if m % 2:
                send_ref[m // 2, :chans] = piece.astype(BF)
            else:
                keep_refs[m // 2][:chans] = piece
        evens = dot(p_ref[...], moves[...]).astype(BF)
        sums[...] = dot(w_ref[...], evens)
        for j in range(group):
            piece = sums[rows_at((id_ref[0] ^ j) * own, own, 8), :]
            for n in range(few_all // pixels):
                below = slice(chans + n * own, chans + (n + 1) * own)
                cols = piece[:, n * pixels : (n + 1) * pixels]
                if j % 2:
                    send_ref[j // 2, below] = cols.astype(BF)
                else:
                    keep_refs[j // 2][below] = cols

    return call(
        "forward",
        body,
        [shape((chans + own * few_all // pixels, pixels), F32)] * (group // 2)
        + [shape((group // 2, chans + own * few_all // pixels, pixels), BF)],
        [pltpu.VMEM((chans, few_all), F32), pltpu.VMEM((group * pixels, few_all), BF)],
        2 * group * pixels * rows * (chans + few_all),
        group * chans * pixels * 3,
        [ids, w_turned, patch],
        1,
    )


def filter_grad(ids, patch, hidden_cots, backs, width, few):
    rows = patch.shape[0]
    group = len(hidden_cots)
    pixels, chans = hidden_cots[0].shape
    own, few_all = backs[0].shape
    _, rest = col_sets(chans)
    tiles = chans // LANES
    part = round_up(-(-rows // BLOCK), 8)

    def body(id_ref, p_ref, *refs):
        cot_refs, back_refs = refs[:group], refs[group : 2 * group]
        hid = refs[2 * group]
        keep_refs, send_ref = refs[-5:-3], refs[-3]
        back, tile = refs[-2:]
        for j in range(group):
            back[rows_at((id_ref[0] ^ j) * own, own, 8), :] = back_refs[j][...].astype(F32)
        back_all = back[...].astype(BF)
        for j in range(group):
            d = id_ref[0] ^ j
            spread = dot(spread_rows(few_all, few, pixels, width, d), back_all, NT)
            hid[j * pixels : (j + 1) * pixels] = (cot_refs[j][...].astype(F32) + spread).astype(BF)
        total = dot(p_ref[...], hid[...])
        for n in range(tiles):
            tile[n] = total[:, n * LANES : (n + 1) * LANES]
        lane = lax.broadcasted_iota(jnp.int32, (part, LANES), 1) // rest
        for k in (1, 3, 0, 2):
            q = id_ref[1] ^ k
            share = jnp.zeros((part, LANES), F32)
            for i in range(BLOCK):
                size = min(part, rows - i * part)
                piece = tile[tiles - 1, i * part : i * part + size, :]
                if size < part:
                    piece = jnp.concatenate([piece, jnp.zeros((part - size, LANES), F32)])
                turn = ((i - q + BLOCK) % BLOCK) * rest
                share = share + jnp.where(lane == i, pltpu.roll(piece, turn, 1), 0.0)
            if k % 2:
                send_ref[k // 2, :rows] = tile[q].astype(BF)
                send_ref[k // 2, rows:] = share.astype(BF)
            else:
                keep_refs[k // 2][:rows] = tile[q]
                keep_refs[k // 2][rows:] = share

    return call(
        "filter_grad",
        body,
        [
            shape((group * pixels, chans), BF),
            shape((rows + part, LANES), F32),
            shape((rows + part, LANES), F32),
            shape((2, rows + part, LANES), BF),
        ],
        [
            pltpu.VMEM((chans, few_all), F32),
            pltpu.VMEM((tiles, rows, LANES), F32),
        ],
        2 * group * pixels * rows * chans,
        group * pixels * chans * 4 + rows * chans * 3,
        [ids, patch, *hidden_cots, *backs],
        1,
    )


def place_grad(ids, members, array, own, chans, scale, begun=None):
    rows = 9 * own
    part = round_up(-(-rows // BLOCK), 8)
    _, rest = col_sets(chans)
    tiles = chans // LANES
    final = begun is not None

    def body(id_ref, p_ref, *refs):
        if final:
            _, begun_ref, o_ref, wide, last, sems = refs
            last[...] = begun_ref[...]
        else:
            o_ref, last, wide, sems = refs
            last[...] = jnp.zeros_like(last)
        lane = lax.broadcasted_iota(jnp.int32, (part, LANES), 1) // rest

        def store(where, low, piece):
            high = low + piece.shape[0]
            for t in range(9):
                lo, hi = max(low, t * own), min(high, (t + 1) * own)
                if lo < hi:
                    wide[where, pl.ds((lo - t * own) * 9 + t, hi - lo, stride=9), :] = piece[
                        lo - low : hi - low
                    ]

        def copy_out(slot, where):
            at = pl.ds(pl.multiple_of(where * LANES, LANES), LANES)
            return pltpu.make_async_copy(wide.at[slot], o_ref.at[:, at], sems.at[slot])

        for n, k in enumerate(members):
            q = id_ref[1] ^ k
            store(n, 0, p_ref[n, :rows, :].astype(F32) * scale)
            copy_out(n, q).start()
            share = p_ref[n, rows:, :].astype(F32) * scale
            for i in range(BLOCK):
                turn = ((q - i + BLOCK) % BLOCK) * rest
                last[i] += jnp.where(lane == q, pltpu.roll(share, turn, 1), 0.0)
        if final:
            for i in range(BLOCK):
                store(2, i * part, last[i, : min(part, rows - i * part), :])
            copy_out(2, tiles - 1).start()
        for n, k in enumerate(members):
            copy_out(n, id_ref[1] ^ k).wait()
        if final:
            copy_out(2, tiles - 1).wait()

    vmem, anywhere = pl.BlockSpec(memory_space=pltpu.VMEM), pl.BlockSpec(memory_space=pl.ANY)
    share_shape = (BLOCK, part, LANES)
    scratch = [pltpu.VMEM((3, rows, LANES), F32)]
    if final:
        scratch.append(pltpu.VMEM(share_shape, F32))
    return pl.pallas_call(
        body,
        out_shape=shape((rows, chans), F32)
        if final
        else [shape((rows, chans), F32), shape(share_shape, F32)],
        in_specs=[pl.BlockSpec(memory_space=pltpu.SMEM), vmem] + [anywhere, vmem] * final,
        out_specs=anywhere if final else [anywhere, vmem],
        scratch_shapes=scratch + [pltpu.SemaphoreType.DMA((3,))],
        input_output_aliases={2: 0} if final else {},
        compiler_params=pltpu.CompilerParams(vmem_limit_bytes=VMEM_LIMIT),
        cost_estimate=pl.CostEstimate(
            flops=0, bytes_accessed=rows * chans * 3, transcendentals=0
        ),
        name="place_grad",
    )(ids, array, *(begun or ()))


def place_skip(ids, pieces, own, wide_chans, scale):
    few_rows = own // BLOCK

    def body(id_ref, *refs):
        o_ref, shares = refs[-2:]
        for ref, (members, _) in zip(refs, pieces):
            for n, k in enumerate(members):
                for i in range(wide_chans // LANES):
                    piece = ref[n, i * few_rows : (i + 1) * few_rows, :].astype(F32) * scale
                    shares[id_ref[1] ^ k, :, i * LANES : (i + 1) * LANES] = piece
        for q in range(BLOCK):
            o_ref[q * few_rows : (q + 1) * few_rows] = shares[q]

    return call(
        "place_skip",
        body,
        shape((own, wide_chans), F32),
        [pltpu.VMEM((BLOCK, few_rows, wide_chans), F32)],
        0,
        6 * own * wide_chans,
        [ids, *[array for _, array in pieces]],
        1,
    )


def finish_hidden(source, held, got, width):
    pixels, chans = source.shape
    few = pixels // 4

    def body(s_ref, k_ref, g_ref, o_ref, sub_ref):
        total = (k_ref[:chans] + g_ref[:chans].astype(F32)).T
        hidden = (s_ref[...].astype(F32) + total).astype(BF)
        o_ref[...] = hidden
        (one_hot,) = spread_matrix(few, few, pixels, width)
        sub_ref[...] = dot(one_hot, hidden).astype(BF)

    return call(
        "finish_hidden",
        body,
        [shape((pixels, chans), BF), shape((few, chans), BF)],
        [],
        2 * few * pixels * chans,
        pixels * chans * 10,
        [source, held, got],
    )


def skip_grad_term(ids, held, got, own_images, cots, width, few):
    group = len(own_images)
    own, pixels = own_images[0].shape
    few_all, wide_chans = cots.shape
    blocks = few_all // pixels
    low = held.shape[0] - own * blocks
    part, tiles = own // BLOCK, wide_chans // LANES

    def body(id_ref, k_ref, g_ref, c_ref, *refs):
        keep_refs, send_ref, total = refs[-4:-2], refs[-2], refs[-1]
        sub = k_ref[low:] + g_ref[low:].astype(F32)
        sub = jnp.concatenate([sub[n * own : (n + 1) * own] for n in range(blocks)], axis=1)
        row = lax.broadcasted_iota(jnp.int32, (few_all, pixels), 0) // few
        every = jnp.zeros((few_all, pixels), F32)
        for matrix in spread_matrix(few_all, few, pixels, width):
            every = every + matrix.astype(F32)
        for j in range(group):
            chosen = jnp.where(row == (id_ref[0] ^ j), every, 0.0).astype(BF)
            sub = sub + dot(refs[j][...], chosen, NT)
        term = dot(sub.astype(BF), c_ref[...])
        for q in range(BLOCK):
            total[q] = term[q * part : (q + 1) * part]
        for k in range(BLOCK):
            piece = total[id_ref[1] ^ k]
            ref = send_ref.at[k // 2] if k % 2 else keep_refs[k // 2]
            for n in range(tiles):
                cols = piece[:, n * LANES : (n + 1) * LANES]
                ref[n * part : (n + 1) * part] = cols.astype(ref.dtype)

    return call(
        "skip_grad_term",
        body,
        [shape((part * tiles, LANES), F32)] * 2 + [shape((2, part * tiles, LANES), BF)],
        [pltpu.VMEM((BLOCK, part, wide_chans), F32)],
        2 * own * few_all * wide_chans,
        own * wide_chans * 4,
        [ids, held, got, cots, *own_images],
        1,
    )


def project(ids, sub, skips):
    few, chans = sub.shape
    own, wide_chans = skips[0].shape
    group = len(skips)

    def body(id_ref, s_ref, *refs):
        o_ref, turned = refs[group:]
        turned[...] = s_ref[...].astype(F32).T
        total = jnp.zeros((few, wide_chans), F32)
        for j in range(group):
            rows = turned[rows_at((id_ref[0] ^ j) * own, own, 8), :].astype(BF)
            total = total + dot(rows, refs[j][...], TN)
        o_ref[...] = total.astype(BF)

    return call(
        "project",
        body,
        shape((few, wide_chans), BF),
        [pltpu.VMEM((chans, few), F32)],
        2 * few * chans * wide_chans,
        chans * wide_chans * 2,
        [ids, sub, *skips],
        1,
    )


def image_grad(ids, hidden_grad, own_images, w_tap, width):
    group = len(own_images)
    own, pixels = own_images[0].shape
    rows, chans = w_tap.shape
    height = pixels // width

    def body(id_ref, h_ref, w_ref, *refs):
        img_refs = refs[:group]
        o_refs, turned, tap = refs[group:-2], refs[-2], refs[-1]
        y, x = pixel_parts(pixels, width)
        for j in range(group):
            hid = h_ref[j * pixels : (j + 1) * pixels]
            turned[...] = hid.astype(F32).T
            tap[...] = dot(w_ref[...], hid, NT)
            side = tap[4 * own : 5 * own]
            for dy in range(3):
                for dx in range(3):
                    off = (dy - 1) * width + dx - 1
                    if off == 0:
                        continue
                    inside = (y >= dy - 1) & (y < height + dy - 1)
                    inside = inside & (x >= dx - 1) & (x < width + dx - 1)
                    t = 3 * dy + dx
                    moved = pltpu.roll(tap[t * own : (t + 1) * own], off % pixels, 1)
                    side = side + jnp.where(inside, moved, 0.0)
            v = img_refs[j][...].astype(F32)
            sig = 1.0 / (1.0 + jnp.exp(-v))
            slope = sig * (1.0 + v * (1.0 - sig))
            mine = turned[rows_at(id_ref[0] * own, own, 8), :]
            o_refs[j][...] = (mine + slope * side).astype(BF)

    return call(
        "image_grad",
        body,
        [shape((own, pixels), BF)] * group,
        [pltpu.VMEM((chans, pixels), F32), pltpu.VMEM((rows, pixels), F32)],
        2 * group * pixels * rows * chans,
        group * pixels * chans * 2,
        [ids, hidden_grad, w_tap, *own_images],
        1,
    )


def finish_images(ids, pieces, chans):
    group = len(pieces)
    own, pixels = pieces[0].shape

    def body(id_ref, *refs):
        o_ref, wide = refs[group:]
        for j in range(group):
            wide[rows_at((id_ref[0] ^ j) * own, own, 8), :] = refs[j][...].astype(F32)
        o_ref[...] = wide[...].T.astype(BF)

    return call(
        "finish_images",
        body,
        shape((pixels, chans), BF),
        [pltpu.VMEM((chans, pixels), F32)],
        0,
        pixels * chans * 4,
        [ids, *pieces],
        1,
    )


def flip(value, axis, bit):
    return lax.ppermute(value, axis, [(i, i ^ bit) for i in range(lax.axis_size(axis))])


def after(value, *others):
    return lax.optimization_barrier((value, *others))[0]


def high_bits(count):
    return [1 << k for k in reversed(range(count.bit_length() - 1))]


def gather(value, axis, *others):
    found = {0: value}
    for n, bit in enumerate(high_bits(lax.axis_size(axis))):
        for j, held in list(found.items()):
            if n == 1 and j and others:
                held = found[j] = after(held, *others)
            found[j ^ bit] = flip(held, axis, bit)
    return [found[j] for j in range(len(found))]


def exchange(blocks, axis, count):
    return [flip(blocks[j], axis, j) if j else blocks[0] for j in range(count)]


def hop(value, bit):
    ranks, group = lax.axis_size("rep"), lax.axis_size("shard")
    pairs = []
    for r in range(ranks):
        for s in range(group):
            other = r ^ (bit if s % 2 == 0 else 3 - bit)
            pairs.append((r * group + s, other * group + s))
    return lax.ppermute(value, ("rep", "shard"), pairs)


def sum_beyond_block(value):
    bits = [bit for bit in reversed(high_bits(lax.axis_size("rep"))) if bit >= BLOCK]
    got = jnp.zeros_like(value)
    for n, bit in enumerate(bits):
        if n:
            value = (value.astype(F32) + got.astype(F32)).astype(BF)
        got = flip(value, "rep", bit)
    return value, got


def add_beyond_block(value):
    value, got = sum_beyond_block(value)
    return (value.astype(F32) + got.astype(F32)).astype(BF)


def sum_scatter(keep, send):
    bits = list(reversed(high_bits(lax.axis_size("shard"))))
    for bit in bits[:-1]:
        got = flip(send, "shard", bit)
        total = [held + got[i].astype(F32) for i, held in enumerate(keep)]
        keep, send = total[0::2], jnp.stack(total[1::2]).astype(BF)
    return keep[0], send[0], flip(send[0], "shard", bits[-1])


def on_device(images, conv_weight, skip_weight, cotangent, hidden_cot):
    _, height, width, chans = images.shape
    own, wide = skip_weight.shape
    pixels, few = height * width, (height // 2) * (width // 2)
    group, ranks = lax.axis_size("shard"), lax.axis_size("rep")
    shard, rank = lax.axis_index("shard"), lax.axis_index("rep") % BLOCK
    member = jnp.where(shard % 2 == 0, rank, rank // 2 + 2 * (rank % 2))
    ids = jnp.stack([shard, member]).astype(jnp.int32)
    source = images.reshape(pixels, chans)

    img_sets = turn_images(ids, source, group, own)
    cots = gather(cotangent.reshape(few, wide), "shard", img_sets[0])
    own_images = exchange(img_sets, "shard", group)
    back, cots = back_product(after(ids, *own_images), cots, skip_weight)
    backs = [back] + [flip(back, "shard", j) for j in range(1, group)]
    patch = make_patches([after(piece, back) for piece in own_images], width)
    hidden_cots = hidden_cot.reshape(pixels, chans)
    hidden_cots = gather(after(hidden_cots, *own_images[2:]), "shard", patch, *backs)

    hidden_grad, keep_0, keep_2, send_g = filter_grad(
        after(ids, patch), patch, hidden_cots, backs, width, few
    )
    got_g = hop(send_g, 1)
    w_tap, w_turned = turn_filters(after(conv_weight, send_g))
    *keep, send = forward(ids, patch, w_turned, pixels, width, few)
    skips = gather(after(skip_weight, send_g), "shard")
    got_g = after(got_g, send, skips[2])
    mid_g = (keep_2 + got_g[1].astype(F32)).astype(BF)
    last_g = hop(mid_g, 2)
    keep, last, got = sum_scatter(keep, after(send, mid_g))
    own_input = image_grad(after(ids, last), hidden_grad, own_images, w_tap, width)
    last_g = after(last_g, own_input[0], got, *skips)
    sum_g = (keep_0 + got_g[0].astype(F32) + last_g.astype(F32)).astype(BF)

    beyond = sum_beyond_block(sum_g)
    skip_0, skip_2, send_s = skip_grad_term(
        after(ids, sum_g), keep, got, own_images, cots, width, few
    )
    hidden, sub = finish_hidden(after(source, sum_g), keep, got, width)
    got_s = hop(send_s, 1)
    projected = project(ids, sub, skips).reshape(cotangent.shape)
    got_s, far, projected = lax.optimization_barrier((got_s, beyond[1], projected))
    total = (beyond[0].astype(F32) + far.astype(F32)).astype(BF)
    across = hop(total, 2)
    last_s = hop((skip_2 + got_s[1].astype(F32)).astype(BF), 2)
    arrived = exchange([after(piece, total) for piece in own_input], "shard", group)
    pair = jnp.stack([total, after(across, *arrived)])
    rest = hop(pair, 1)
    last_s = after(last_s, pair)
    sum_s = (skip_0 + got_s[0].astype(F32) + last_s.astype(F32)).astype(BF)
    beyond_s = sum_beyond_block(sum_s)
    input_grad = finish_images(after(ids, sum_s), arrived, chans)
    far_s = after(beyond_s[1], input_grad)
    full_s = (beyond_s[0].astype(F32) + far_s.astype(F32)).astype(BF)
    factor = 1.0 / math.sqrt(ranks * group * few)
    across_s = hop(full_s, 2)
    first = place_grad(after(ids, full_s), (0, 2), pair, own, chans, factor)
    pair_s = jnp.stack([full_s, after(across_s, first[0])])
    rest_s = hop(pair_s, 1)
    skip_grad = place_skip(
        ids, [((0, 2), pair_s), ((1, 3), rest_s)], own, wide, factor
    )
    rest = after(rest, skip_grad)
    conv_grad = place_grad(ids, (1, 3), rest, own, chans, factor, first)

    return (
        hidden.reshape(images.shape),
        projected,
        input_grad.reshape(images.shape),
        conv_grad,
        skip_grad,
    )


def solution(mesh):
    placed = (
        P(("rep", "shard"), None, None, None),
        P("shard", None),
        P("shard", None),
        P(("rep", "shard"), None, None, None),
        P(("rep", "shard"), None, None, None),
    )
    return jax.shard_map(
        on_device,
        mesh=mesh,
        in_specs=placed,
        out_specs=(
            P(("rep", "shard"), None, None, None),
            P(("rep", "shard"), None, None, None),
            P(("rep", "shard"), None, None, None),
            P("shard", None),
            P("shard", None),
        ),
        check_vma=False,
    )
```

time: 138 us -> 129 us (0.935); the launches traced: 135 us -> 129 us
  starting transfers between devices: 41.6 us -> 31.4 us
  Pallas kernels: 44.9 us -> 52.7 us
  local copies, waits for them, and re-layouts: 10.3 us -> 3.84 us
  waiting for transfers between devices: 35.7 us -> 37.6 us
    ppermute x23 -> x22, waiting for transfers between devices: 16.1 us -> 31.4 us  [flip(): lax.ppermute(value, axis, [(i, i ^ bit) for i in range(lax.axis_size(axis...]
    ppermute x10 -> x8, waiting for transfers between devices: 19.6 us -> 6.17 us  [hop(): return lax.ppermute(value, ('rep', 'shard'), pairs)]
    ppermute x23 -> x22, starting transfers between devices: 32.3 us -> 20.8 us  [flip(): lax.ppermute(value, axis, [(i, i ^ bit) for i in range(lax.axis_size(axis...]
    pallas_call x10 -> x12, Pallas kernels: 40.7 us -> 46 us  [call(): pl.pallas_call(body, out_shape=outs, in_specs=specs, out_specs=jax.tree.m...]
    slice x7 -> x0, local copies, waits for them, and re-layouts: 3.34 us -> none  [the longest x2 2.32 us: exchange(): blocks[j:j + 1]]
    pallas_call x1 -> x2, Pallas kernels: 4.15 us -> 6.77 us  [place_grad(): pl.pallas_call(body, out_shape=shape((rows, chans), F32) if final else [s...]
    unnamed x63 -> x66, local copies, waits for them, and re-layouts: 6.11 us -> 3.84 us
    ppermute x10 -> x8, starting transfers between devices: 9.3 us -> 10.5 us  [hop(): return lax.ppermute(value, ('rep', 'shard'), pairs)]
  transfers between devices with their start and end apart: 33 -> 30, of which waited for: 12 -> 13; matrix products, arithmetic and copies ran while one was open for 5% -> 2% of each run, Pallas kernels for 22% -> 33%
where the time goes in v4:
time: 129 us
  Pallas kernels  52.7 us (41%)
  waiting for transfers between devices  37.6 us (29%)
  starting transfers between devices  31.4 us (24%)
  local copies, waits for them, and re-layouts  3.84 us (3%)
  other arithmetic  2.42 us (2%)
    pallas_call x12, Pallas kernels, call(): pl.pallas_call(body, out_shape=outs, in_specs=specs, out_specs=jax.tree.m...  46 us
    ppermute x22, waiting for transfers between devices, flip(): lax.ppermute(value, axis, [(i, i ^ bit) for i in range(lax.axis_size(axis...  31.4 us
    ppermute x22, starting transfers between devices, flip(): lax.ppermute(value, axis, [(i, i ^ bit) for i in range(lax.axis_size(axis...  20.8 us
    ppermute x8, starting transfers between devices, hop(): return lax.ppermute(value, ('rep', 'shard'), pairs)  10.5 us
    pallas_call x2, Pallas kernels, place_grad(): pl.pallas_call(body, out_shape=shape((rows, chans), F32) if final else [s...  6.77 us
    ppermute x8, waiting for transfers between devices, hop(): return lax.ppermute(value, ('rep', 'shard'), pairs)  6.17 us
    unnamed x66, local copies, waits for them, and re-layouts  3.84 us
  transfers between devices with their start and end apart: 30, of which 13 were waited for; matrix products, arithmetic and copies ran while one was open for 2% of the time, Pallas kernels for 33%

profile of v4, /device:TPU:1, one launch (start us, length us, event | category | flops | bytes accessed | tf_op | source)
XLA Modules:
  0.0 129.0 jit_solution(17121045719442655745)
XLA Ops:
  0.6 2.1 %collective-permute-start.4 = (bf16[64,1280]{1,0:T(8,128)(2,1)}, bf16[64,1280]{1,0:T(8,128)(2,1)S(1)}, u32[]{:S(2)}, u32[]{:S(2)}) collective-permute-start(bf16[64,1280]{1,0:T(8,128)(2,1)} %bitcast.40), channel_id=1, source_target_pairs={{0,2},{1,3},{2,0},{3,1},{4,6},{5,7},{6,4},{7,5},{8,10},{9,11},{10,... | collective-permute-start | bytes 491528 | tf_op jit(solution)/shard_map/ppermute | solution.py:539
  3.4 1.9 %turn_images.1 = (bf16[160,256]{1,0:T(8,128)(2,1)}, bf16[160,256]{1,0:T(8,128)(2,1)}, bf16[160,256]{1,0:T(8,128)(2,1)}, bf16[160,256]{1,0:T(8,128)(2,1)}) custom-call(s32[2]{0:T(128)} %pad_add_fusion.id_ref, bf16[256,640]{1,0:T(8,128)(2,1)} %bitcast.35), custom_call_target="tpu_custom_call" | custom-call | bytes 655360 | tf_op jit(solution)/shard_map/turn_images/pallas_call | solution.py:30
  5.3 2.5 %collective-permute-start.2 = (bf16[160,256]{1,0:T(8,128)(2,1)}, bf16[160,256]{1,0:T(8,128)(2,1)S(1)}, u32[]{:S(2)}, u32[]{:S(2)}) collective-permute-start(bf16[160,256]{1,0:T(8,128)(2,1)} %get-tuple-element.65), channel_id=1, source_target_pairs={{0,3},{1,2},{2,1},{3,0},{4,7},{5,6},{6,5},{7,4},{8,11},{9,10},{10,... | collective-permute-start | bytes 245768 | tf_op jit(solution)/shard_map/ppermute | solution.py:539
  8.8 2.7 %collective-permute-done.2.refs_3_ = bf16[160,256]{1,0:T(8,128)(2,1)S(1)} collective-permute-done((bf16[160,256]{1,0:T(8,128)(2,1)}, bf16[160,256]{1,0:T(8,128)(2,1)S(1)}, u32[]{:S(2)}, u32[]{:S(2)}) %collective-permute-start.2) | collective-permute-done | bytes 81952 | tf_op jit(solution)/shard_map/ppermute | solution.py:539
  16.4 2.3 %back_product.1 = (bf16[160,256]{1,0:T(8,128)(2,1)}, bf16[256,1280]{1,0:T(8,128)(2,1)}) custom-call(s32[2]{0:T(128)} %pad_add_fusion.id_ref, bf16[160,1280]{1,0:T(8,128)(2,1)} %refs_0_, bf16[64,1280]{1,0:T(8,128)(2,1)} %bitcast.42, bf16[64,1280]{1,0:T(8,128)(2,1)} %copy-done.19, bf16[64,1280]{1,0:T(8,128)(2,1)} %copy-done.18, bf16[64,1280]{1,0:T(8,128)(2,1)} %copy-done.20), custom_call_target="tpu_custom_call" | custom-call | flops 104857600 | bytes 655360 | tf_op jit(solution)/shard_map/back_product/pallas_call | solution.py:30
  19.0 1.5 %collective-permute-start.9 = (bf16[160,256]{1,0:T(8,128)(2,1)}, bf16[160,256]{1,0:T(8,128)(2,1)S(1)}, u32[]{:S(2)}, u32[]{:S(2)}) collective-permute-start(bf16[160,256]{1,0:T(8,128)(2,1)} %get-tuple-element.68.refs_4_), channel_id=1, source_target_pairs={{0,2},{1,3},{2,0},{3,1},{4,6},{5,7},{6,4},{7,5},{8,10},{9,11},{10,... | collective-permute-start | bytes 245768 | tf_op jit(solution)/shard_map/ppermute | solution.py:539
  21.1 3.6 %make_patches.1.p_ref = bf16[1440,1024]{1,0:T(8,128)(2,1)} custom-call(bf16[160,256]{1,0:T(8,128)(2,1)} %get-tuple-element.69.refs_0_, bf16[160,256]{1,0:T(8,128)(2,1)} %copy-done.14, bf16[160,256]{1,0:T(8,128)(2,1)} %copy-done.12, bf16[160,256]{1,0:T(8,128)(2,1)} %copy-done.13), custom_call_target="tpu_custom_call" | custom-call | bytes 3276800 | tf_op jit(solution)/shard_map/make_patches/pallas_call | solution.py:30
  27.7 7.4 %filter_grad.1 = (bf16[1024,640]{1,0:T(8,128)(2,1)}, f32[1800,128]{1,0:T(8,128)}, f32[1800,128]{1,0:T(8,128)}, bf16[2,1800,128]{2,1,0:T(8,128)(2,1)}) custom-call(s32[2]{0:T(128)} %pad_add_fusion.id_ref, bf16[1440,1024]{1,0:T(8,128)(2,1)} %make_patches.1.p_ref, bf16[256,640]{1,0:T(8,128)(2,1)} %bitcast.47, bf16[256,640]{1,0:T(8,128)(2,1)} %copy-done.25, ...), custom_call_target="tpu_custom_call" | custom-call | flops 1887436800 | bytes 5386240 | tf_op jit(solution)/shard_map/filter_grad/pallas_call | solution.py:30
  35.2 1.4 %collective-permute-start.12 = (bf16[2,1800,128]{2,1,0:T(8,128)(2,1)}, bf16[2,1800,128]{2,1,0:T(8,128)(2,1)S(1)}, u32[]{:S(2)}, u32[]{:S(2)}) collective-permute-start(bf16[2,1800,128]{2,1,0:T(8,128)(2,1)} %get-tuple-element.77), channel_id=1, source_target_pairs={{0,4},{1,9},{2,6},{3,11},{4,0},{5,13},{6,2},{7,15},{8,12},{9,1},{1... | collective-permute-start | bytes 2764808 | tf_op jit(solution)/shard_map/ppermute | solution.py:571
  37.2 4.1 %turn_filters.1 = (bf16[1440,640]{1,0:T(8,128)(2,1)}, bf16[640,1440]{1,0:T(8,128)(2,1)}) custom-call(bf16[1440,640]{1,0:T(8,128)(2,1)} %w_ref), custom_call_target="tpu_custom_call" | custom-call | bytes 5529600 | tf_op jit(solution)/shard_map/turn_filters/pallas_call | solution.py:30
  41.3 8.3 %forward.1 = (f32[800,256]{1,0:T(8,128)}, f32[800,256]{1,0:T(8,128)}, bf16[2,800,256]{2,1,0:T(8,128)(2,1)}) custom-call(s32[2]{0:T(128)} %pad_add_fusion.id_ref, bf16[640,1440]{1,0:T(8,128)(2,1)} %get-tuple-element.79.w_ref, bf16[1440,1024]{1,0:T(8,128)(2,1)} %make_patches.1.p_ref), custom_call_target="tpu_custom_call" | custom-call | flops 2642411520 | bytes 1966080 | tf_op jit(solution)/shard_map/forward/pallas_call | solution.py:30
  51.6 1.6 %collective-permute-done.15 = bf16[2,800,256]{2,1,0:T(8,128)(2,1)S(1)} collective-permute-done((bf16[2,800,256]{2,1,0:T(8,128)(2,1)}, bf16[2,800,256]{2,1,0:T(8,128)(2,1)S(1)}, u32[]{:S(2)}, u32[]{:S(2)}) %collective-permute-start.15) | collective-permute-done | bytes 819232 | tf_op jit(solution)/shard_map/ppermute | solution.py:539
  55.2 6.0 %image_grad.1 = (bf16[160,256]{1,0:T(8,128)(2,1)}, bf16[160,256]{1,0:T(8,128)(2,1)}, bf16[160,256]{1,0:T(8,128)(2,1)}, bf16[160,256]{1,0:T(8,128)(2,1)}) custom-call(s32[2]{0:T(128)} %pad_add_fusion.id_ref, bf16[1024,640]{1,0:T(8,128)(2,1)} %get-tuple-element.87.h_ref, bf16[1440,640]{1,0:T(8,128)(2,1)} %get-tuple-element.88.w_ref, ...), custom_call_target="tpu_custom_call" | custom-call | flops 1887436800 | bytes 1310720 | tf_op jit(solution)/shard_map/image_grad/pallas_call | solution.py:30
  61.3 3.8 %collective-permute-done.16.g_ref = bf16[800,256]{1,0:T(8,128)(2,1)S(1)} collective-permute-done((bf16[800,256]{1,0:T(8,128)(2,1)S(1)}, bf16[800,256]{1,0:T(8,128)(2,1)S(1)}, u32[]{:S(2)}, u32[]{:S(2)}) %collective-permute-start.16) | collective-permute-done | bytes 409632 | tf_op jit(solution)/shard_map/ppermute | solution.py:539
  65.2 2.4 %collective-permute-start.20 = (bf16[1800,128]{1,0:T(8,128)(2,1)S(1)}, bf16[1800,128]{1,0:T(8,128)(2,1)S(1)}, u32[]{:S(2)}, u32[]{:S(2)}) collective-permute-start(bf16[1800,128]{1,0:T(8,128)(2,1)S(1)} %fusion.2), channel_id=1, source_target_pairs={{0,16},{4,20},{8,24},{12,28},{16,0},{20,4},{24,8},{28,12},{1,17},{... | collective-permute-start | bytes 1382408 | tf_op jit(solution)/shard_map/ppermute | solution.py:539
  67.6 3.3 %skip_grad_term.1 = (f32[400,128]{1,0:T(8,128)}, f32[400,128]{1,0:T(8,128)}, bf16[2,400,128]{2,1,0:T(8,128)(2,1)}) custom-call(s32[2]{0:T(128)} %pad_add_fusion.id_ref, f32[800,256]{1,0:T(8,128)} %get-tuple-element.119.k_ref, bf16[800,256]{1,0:T(8,128)(2,1)} %copy-done.1, bf16[256,1280]{1,0:T(8,128)(2,1)} %get-tuple-element.95.c_ref, ...), custom_call_target="tpu_custom_call" | custom-call | flops 104857600 | bytes 819200 | tf_op jit(solution)/shard_map/skip_grad_term/pallas_call | solution.py:30
  70.9 1.4 %collective-permute-start.19 = (bf16[2,400,128]{2,1,0:T(8,128)(2,1)}, bf16[2,400,128]{2,1,0:T(8,128)(2,1)S(1)}, u32[]{:S(2)}, u32[]{:S(2)}) collective-permute-start(bf16[2,400,128]{2,1,0:T(8,128)(2,1)} %get-tuple-element.96), channel_id=1, source_target_pairs={{0,4},{1,9},{2,6},{3,11},{4,0},{5,13},{6,2},{7,15},{8,12},{9,1},{1... | collective-permute-start | bytes 614408 | tf_op jit(solution)/shard_map/ppermute | solution.py:571
  72.3 2.3 %finish_hidden.1 = (bf16[256,640]{1,0:T(8,128)(2,1)}, bf16[64,640]{1,0:T(8,128)(2,1)}) custom-call(bf16[256,640]{1,0:T(8,128)(2,1)} %bitcast.36, f32[800,256]{1,0:T(8,128)} %get-tuple-element.119.k_ref, bf16[800,256]{1,0:T(8,128)(2,1)} %copy-done.1), custom_call_target="tpu_custom_call" | custom-call | flops 20971520 | bytes 1638400 | tf_op jit(solution)/shard_map/finish_hidden/pallas_call | solution.py:30
  74.6 2.7 %project.1 = bf16[64,1280]{1,0:T(8,128)(2,1)} custom-call(s32[2]{0:T(128)} %pad_add_fusion.id_ref, bf16[64,640]{1,0:T(8,128)(2,1)} %get-tuple-element.97.s_ref, bf16[160,1280]{1,0:T(8,128)(2,1)} %refs_0_, bf16[160,1280]{1,0:T(8,128)(2,1)} %copy-done.10, bf16[160,1280]{1,0:T(8,128)(2,1)} %copy-done.9, bf16[160,1280]{1,0:T(8,128)(2,1)} %copy-done.11), custom_call_target="tpu_custom_call" | custom-call | flops 104857600 | bytes 1638400 | tf_op jit(solution)/shard_map/project/pallas_call | solution.py:30
  77.3 3.0 %collective-permute-done.19 = bf16[2,400,128]{2,1,0:T(8,128)(2,1)S(1)} collective-permute-done((bf16[2,400,128]{2,1,0:T(8,128)(2,1)}, bf16[2,400,128]{2,1,0:T(8,128)(2,1)S(1)}, u32[]{:S(2)}, u32[]{:S(2)}) %collective-permute-start.19) | collective-permute-done | bytes 204832 | tf_op jit(solution)/shard_map/ppermute | solution.py:571
  80.3 7.2 %collective-permute-done.20 = bf16[1800,128]{1,0:T(8,128)(2,1)S(1)} collective-permute-done((bf16[1800,128]{1,0:T(8,128)(2,1)S(1)}, bf16[1800,128]{1,0:T(8,128)(2,1)S(1)}, u32[]{:S(2)}, u32[]{:S(2)}) %collective-permute-start.20) | collective-permute-done | bytes 460832 | tf_op jit(solution)/shard_map/ppermute | solution.py:539
  87.6 1.8 %collective-permute-start.22 = (bf16[1800,128]{1,0:T(8,128)(2,1)S(1)}, bf16[1800,128]{1,0:T(8,128)(2,1)S(1)}, u32[]{:S(2)}, u32[]{:S(2)}) collective-permute-start(bf16[1800,128]{1,0:T(8,128)(2,1)S(1)} %add_convert_fusion), channel_id=1, source_target_pairs={{0,8},{1,5},{2,10},{3,7},{4,12},{5,1},{6,14},{7,3},{8,0},{9,13},{1... | collective-permute-start | bytes 1382408 | tf_op jit(solution)/shard_map/ppermute | solution.py:571
  91.8 2.7 %collective-permute-done.25.refs_3_ = bf16[160,256]{1,0:T(8,128)(2,1)S(1)} collective-permute-done((bf16[160,256]{1,0:T(8,128)(2,1)S(1)}, bf16[160,256]{1,0:T(8,128)(2,1)S(1)}, u32[]{:S(2)}, u32[]{:S(2)}) %collective-permute-start.25) | collective-permute-done | bytes 81952 | tf_op jit(solution)/shard_map/ppermute | solution.py:539
  94.4 1.4 %collective-permute-done.24.refs_2_ = bf16[160,256]{1,0:T(8,128)(2,1)S(1)} collective-permute-done((bf16[160,256]{1,0:T(8,128)(2,1)S(1)}, bf16[160,256]{1,0:T(8,128)(2,1)S(1)}, u32[]{:S(2)}, u32[]{:S(2)}) %collective-permute-start.24) | collective-permute-done | bytes 81952 | tf_op jit(solution)/shard_map/ppermute | solution.py:539
  97.0 3.1 %collective-permute-start.27 = (bf16[400,128]{1,0:T(8,128)(2,1)S(1)}, bf16[400,128]{1,0:T(8,128)(2,1)S(1)}, u32[]{:S(2)}, u32[]{:S(2)}) collective-permute-start(bf16[400,128]{1,0:T(8,128)(2,1)S(1)} %fusion.6), channel_id=1, source_target_pairs={{0,16},{4,20},{8,24},{12,28},{16,0},{20,4},{24,8},{28,12},{1,17},{... | collective-permute-start | bytes 307208 | tf_op jit(solution)/shard_map/ppermute | solution.py:539
  100.2 2.0 %finish_images.1 = bf16[256,640]{1,0:T(8,128)(2,1)} custom-call(s32[2]{0:T(128)} %pad_add_fusion.id_ref, bf16[160,256]{1,0:T(8,128)(2,1)} %get-tuple-element.103.refs_0_, bf16[160,256]{1,0:T(8,128)(2,1)} %copy-done.23, bf16[160,256]{1,0:T(8,128)(2,1)} %copy-done.22, bf16[160,256]{1,0:T(8,128)(2,1)} %copy-done.21), custom_call_target="tpu_custom_call" | custom-call | bytes 655360 | tf_op jit(solution)/shard_map/finish_images/pallas_call | solution.py:30
  102.1 8.5 %collective-permute-done.27 = bf16[400,128]{1,0:T(8,128)(2,1)S(1)} collective-permute-done((bf16[400,128]{1,0:T(8,128)(2,1)S(1)}, bf16[400,128]{1,0:T(8,128)(2,1)S(1)}, u32[]{:S(2)}, u32[]{:S(2)}) %collective-permute-start.27) | collective-permute-done | bytes 102432 | tf_op jit(solution)/shard_map/ppermute | solution.py:539
  111.7 3.7 %place_grad.2 = (f32[1440,640]{1,0:T(8,128)}, f32[4,360,128]{2,1,0:T(8,128)}) custom-call(s32[2]{0:T(128)} %pad_add_fusion.id_ref, bf16[2,1800,128]{2,1,0:T(8,128)(2,1)} %copy-done), custom_call_target="tpu_custom_call" | custom-call | bytes 2764800 | tf_op jit(solution)/shard_map/place_grad/pallas_call | solution.py:342
  115.5 3.4 %collective-permute-start.29 = (bf16[2,400,128]{2,1,0:T(8,128)(2,1)S(1)}, bf16[2,400,128]{2,1,0:T(8,128)(2,1)S(1)}, u32[]{:S(2)}, u32[]{:S(2)}) collective-permute-start(bf16[2,400,128]{2,1,0:T(8,128)(2,1)S(1)} %pad_maximum_fusion.1.refs_0_), channel_id=1, source_target_pairs={{0,4},{1,9},{2,6},{3,11},{4,0},{5,13},{6,2},{7,15},{8,12},{9,1},{1... | collective-permute-start | bytes 614408 | tf_op jit(solution)/shard_map/ppermute | solution.py:571
  118.8 3.1 %collective-permute-done.29.refs_1_ = bf16[2,400,128]{2,1,0:T(8,128)(2,1)S(1)} collective-permute-done((bf16[2,400,128]{2,1,0:T(8,128)(2,1)S(1)}, bf16[2,400,128]{2,1,0:T(8,128)(2,1)S(1)}, u32[]{:S(2)}, u32[]{:S(2)}) %collective-permute-start.29) | collective-permute-done | bytes 204832 | tf_op jit(solution)/shard_map/ppermute | solution.py:571
  122.7 2.0 %place_skip.1 = f32[160,1280]{1,0:T(8,128)} custom-call(s32[2]{0:T(128)} %pad_add_fusion.id_ref, bf16[2,400,128]{2,1,0:T(8,128)(2,1)} %copy-done.8, bf16[2,400,128]{2,1,0:T(8,128)(2,1)} %copy-done.17), custom_call_target="tpu_custom_call" | custom-call | bytes 1228800 | tf_op jit(solution)/shard_map/place_skip/pallas_call | solution.py:30
  125.7 3.1 %place_grad.3 = f32[1440,640]{1,0:T(8,128)} custom-call(s32[2]{0:T(128)} %pad_add_fusion.id_ref, bf16[2,1800,128]{2,1,0:T(8,128)(2,1)} %copy-done.5, f32[1440,640]{1,0:T(8,128)} %get-tuple-element.115.refs_0_, f32[4,360,128]{2,1,0:T(8,128)} %get-tuple-element.118.refs_1_), custom_call_target="tpu_custom_call", output_to_operand_aliasing={{}: (2, {})} | custom-call | bytes 2764800 | tf_op jit(solution)/shard_map/place_grad/pallas_call | solution.py:342
  (118 shorter events, 21.7 us)
Async XLA Ops:
  0.6 12.6 %collective-permute-start.4 = (bf16[64,1280]{1,0:T(8,128)(2,1)}, bf16[64,1280]{1,0:T(8,128)(2,1)S(1)}, u32[]{:S(2)}, u32[]{:S(2)}) collective-permute-start(bf16[64,1280]{1,0:T(8,128)(2,1)} %bitcast.40), channel_id=1, source_target_pairs={{0,2},{1,3},{2,0},{3,1},{4,6},{5,7},{6,4},{7,5},{8,10},{9,11},{10,... | collective-permute-start | bytes 491528 | tf_op jit(solution)/shard_map/ppermute | solution.py:539
  5.3 3.5 %collective-permute-start.1 = (bf16[160,256]{1,0:T(8,128)(2,1)}, bf16[160,256]{1,0:T(8,128)(2,1)S(1)}, u32[]{:S(2)}, u32[]{:S(2)}) collective-permute-start(bf16[160,256]{1,0:T(8,128)(2,1)} %get-tuple-element.64), channel_id=1, source_target_pairs={{0,2},{1,3},{2,0},{3,1},{4,6},{5,7},{6,4},{7,5},{8,10},{9,11},{10,... | collective-permute-start | bytes 245768 | tf_op jit(solution)/shard_map/ppermute | solution.py:539
  5.3 6.1 %collective-permute-start.2 = (bf16[160,256]{1,0:T(8,128)(2,1)}, bf16[160,256]{1,0:T(8,128)(2,1)S(1)}, u32[]{:S(2)}, u32[]{:S(2)}) collective-permute-start(bf16[160,256]{1,0:T(8,128)(2,1)} %get-tuple-element.65), channel_id=1, source_target_pairs={{0,3},{1,2},{2,1},{3,0},{4,7},{5,6},{6,5},{7,4},{8,11},{9,10},{10,... | collective-permute-start | bytes 245768 | tf_op jit(solution)/shard_map/ppermute | solution.py:539
  11.4 13.5 %collective-permute-start.7 = (bf16[256,640]{1,0:T(8,128)(2,1)}, bf16[256,640]{1,0:T(8,128)(2,1)S(1)}, u32[]{:S(2)}, u32[]{:S(2)}) collective-permute-start(bf16[256,640]{1,0:T(8,128)(2,1)} %bitcast.45), channel_id=1, source_target_pairs={{0,2},{1,3},{2,0},{3,1},{4,6},{5,7},{6,4},{7,5},{8,10},{9,11},{10,... | collective-permute-start | bytes 983048 | tf_op jit(solution)/shard_map/ppermute | solution.py:539
  12.6 2.4 %collective-permute-start.3 = (bf16[64,1280]{1,0:T(8,128)(2,1)}, bf16[64,1280]{1,0:T(8,128)(2,1)S(1)}, u32[]{:S(2)}, u32[]{:S(2)}) collective-permute-start(bf16[64,1280]{1,0:T(8,128)(2,1)} %bitcast.41), channel_id=1, source_target_pairs={{0,1},{1,0},{2,3},{3,2},{4,5},{5,4},{6,7},{7,6},{8,9},{9,8},{10,11... | collective-permute-start | bytes 491528 | tf_op jit(solution)/shard_map/ppermute | solution.py:539
  13.3 1.7 %collective-permute-start.5 = (bf16[64,1280]{1,0:T(8,128)(2,1)S(1)}, bf16[64,1280]{1,0:T(8,128)(2,1)S(1)}, u32[]{:S(2)}, u32[]{:S(2)}) collective-permute-start(bf16[64,1280]{1,0:T(8,128)(2,1)S(1)} %collective-permute-done.4.refs_2_), channel_id=1, source_target_pairs={{0,1},{1,0},{2,3},{3,2},{4,5},{5,4},{6,7},{7,6},{8,9},{9,8},{10,11... | collective-permute-start | bytes 491528 | tf_op jit(solution)/shard_map/ppermute | solution.py:539
  13.3 1.7 %collective-permute-start = (bf16[160,256]{1,0:T(8,128)(2,1)}, bf16[160,256]{1,0:T(8,128)(2,1)S(1)}, u32[]{:S(2)}, u32[]{:S(2)}) collective-permute-start(bf16[160,256]{1,0:T(8,128)(2,1)} %get-tuple-element.63), channel_id=1, source_target_pairs={{0,1},{1,0},{2,3},{3,2},{4,5},{5,4},{6,7},{7,6},{8,9},{9,8},{10,11... | collective-permute-start | bytes 245768 | tf_op jit(solution)/shard_map/ppermute | solution.py:539
  18.7 6.1 %collective-permute-start.10 = (bf16[160,256]{1,0:T(8,128)(2,1)}, bf16[160,256]{1,0:T(8,128)(2,1)S(1)}, u32[]{:S(2)}, u32[]{:S(2)}) collective-permute-start(bf16[160,256]{1,0:T(8,128)(2,1)} %get-tuple-element.68.refs_4_), channel_id=1, source_target_pairs={{0,3},{1,2},{2,1},{3,0},{4,7},{5,6},{6,5},{7,4},{8,11},{9,10},{10,... | collective-permute-start | bytes 245768 | tf_op jit(solution)/shard_map/ppermute | solution.py:539
  18.7 6.0 %collective-permute-start.8 = (bf16[160,256]{1,0:T(8,128)(2,1)}, bf16[160,256]{1,0:T(8,128)(2,1)S(1)}, u32[]{:S(2)}, u32[]{:S(2)}) collective-permute-start(bf16[160,256]{1,0:T(8,128)(2,1)} %get-tuple-element.68.refs_4_), channel_id=1, source_target_pairs={{0,1},{1,0},{2,3},{3,2},{4,5},{5,4},{6,7},{7,6},{8,9},{9,8},{10,11... | collective-permute-start | bytes 245768 | tf_op jit(solution)/shard_map/ppermute | solution.py:539
  19.0 5.9 %collective-permute-start.9 = (bf16[160,256]{1,0:T(8,128)(2,1)}, bf16[160,256]{1,0:T(8,128)(2,1)S(1)}, u32[]{:S(2)}, u32[]{:S(2)}) collective-permute-start(bf16[160,256]{1,0:T(8,128)(2,1)} %get-tuple-element.68.refs_4_), channel_id=1, source_target_pairs={{0,2},{1,3},{2,0},{3,1},{4,6},{5,7},{6,4},{7,5},{8,10},{9,11},{10,... | collective-permute-start | bytes 245768 | tf_op jit(solution)/shard_map/ppermute | solution.py:539
  20.5 5.2 %collective-permute-start.6 = (bf16[256,640]{1,0:T(8,128)(2,1)}, bf16[256,640]{1,0:T(8,128)(2,1)S(1)}, u32[]{:S(2)}, u32[]{:S(2)}) collective-permute-start(bf16[256,640]{1,0:T(8,128)(2,1)} %bitcast.46), channel_id=1, source_target_pairs={{0,1},{1,0},{2,3},{3,2},{4,5},{5,4},{6,7},{7,6},{8,9},{9,8},{10,11... | collective-permute-start | bytes 983048 | tf_op jit(solution)/shard_map/ppermute | solution.py:539
  24.9 2.0 %collective-permute-start.11 = (bf16[256,640]{1,0:T(8,128)(2,1)S(1)}, bf16[256,640]{1,0:T(8,128)(2,1)S(1)}, u32[]{:S(2)}, u32[]{:S(2)}) collective-permute-start(bf16[256,640]{1,0:T(8,128)(2,1)S(1)} %collective-permute-done.7.refs_2_), channel_id=1, source_target_pairs={{0,1},{1,0},{2,3},{3,2},{4,5},{5,4},{6,7},{7,6},{8,9},{9,8},{10,11... | collective-permute-start | bytes 983048 | tf_op jit(solution)/shard_map/ppermute | solution.py:539
  35.2 14.4 %collective-permute-start.12 = (bf16[2,1800,128]{2,1,0:T(8,128)(2,1)}, bf16[2,1800,128]{2,1,0:T(8,128)(2,1)S(1)}, u32[]{:S(2)}, u32[]{:S(2)}) collective-permute-start(bf16[2,1800,128]{2,1,0:T(8,128)(2,1)} %get-tuple-element.77), channel_id=1, source_target_pairs={{0,4},{1,9},{2,6},{3,11},{4,0},{5,13},{6,2},{7,15},{8,12},{9,1},{1... | collective-permute-start | bytes 2764808 | tf_op jit(solution)/shard_map/ppermute | solution.py:571
  36.6 13.0 %collective-permute-start.13 = (bf16[160,1280]{1,0:T(8,128)(2,1)S(1)}, bf16[160,1280]{1,0:T(8,128)(2,1)S(1)}, u32[]{:S(2)}, u32[]{:S(2)}) collective-permute-start(bf16[160,1280]{1,0:T(8,128)(2,1)S(1)} %copy-done.2), channel_id=1, source_target_pairs={{0,2},{1,3},{2,0},{3,1},{4,6},{5,7},{6,4},{7,5},{8,10},{9,11},{10,... | collective-permute-start | bytes 1228808 | tf_op jit(solution)/shard_map/ppermute | solution.py:539
  49.7 3.5 %collective-permute-start.15 = (bf16[2,800,256]{2,1,0:T(8,128)(2,1)}, bf16[2,800,256]{2,1,0:T(8,128)(2,1)S(1)}, u32[]{:S(2)}, u32[]{:S(2)}) collective-permute-start(bf16[2,800,256]{2,1,0:T(8,128)(2,1)} %get-tuple-element.85), channel_id=1, source_target_pairs={{0,1},{1,0},{2,3},{3,2},{4,5},{5,4},{6,7},{7,6},{8,9},{9,8},{10,11... | collective-permute-start | bytes 2457608 | tf_op jit(solution)/shard_map/ppermute | solution.py:539
  50.7 10.6 %collective-permute-start.17 = (bf16[160,1280]{1,0:T(8,128)(2,1)S(1)}, bf16[160,1280]{1,0:T(8,128)(2,1)S(1)}, u32[]{:S(2)}, u32[]{:S(2)}) collective-permute-start(bf16[160,1280]{1,0:T(8,128)(2,1)S(1)} %copy-done.2), channel_id=1, source_target_pairs={{0,1},{1,0},{2,3},{3,2},{4,5},{5,4},{6,7},{7,6},{8,9},{9,8},{10,11... | collective-permute-start | bytes 1228808 | tf_op jit(solution)/shard_map/ppermute | solution.py:539
  50.7 10.5 %collective-permute-start.18 = (bf16[160,1280]{1,0:T(8,128)(2,1)S(1)}, bf16[160,1280]{1,0:T(8,128)(2,1)S(1)}, u32[]{:S(2)}, u32[]{:S(2)}) collective-permute-start(bf16[160,1280]{1,0:T(8,128)(2,1)S(1)} %collective-permute-done.13.refs_2_), channel_id=1, source_target_pairs={{0,1},{1,0},{2,3},{3,2},{4,5},{5,4},{6,7},{7,6},{8,9},{9,8},{10,11... | collective-permute-start | bytes 1228808 | tf_op jit(solution)/shard_map/ppermute | solution.py:539
  51.2 10.1 %collective-permute-start.14 = (bf16[1800,128]{1,0:T(8,128)(2,1)S(1)}, bf16[1800,128]{1,0:T(8,128)(2,1)S(1)}, u32[]{:S(2)}, u32[]{:S(2)}) collective-permute-start(bf16[1800,128]{1,0:T(8,128)(2,1)S(1)} %fusion), channel_id=1, source_target_pairs={{0,8},{1,5},{2,10},{3,7},{4,12},{5,1},{6,14},{7,3},{8,0},{9,13},{1... | collective-permute-start | bytes 1382408 | tf_op jit(solution)/shard_map/ppermute | solution.py:571
  54.4 10.7 %collective-permute-start.16 = (bf16[800,256]{1,0:T(8,128)(2,1)S(1)}, bf16[800,256]{1,0:T(8,128)(2,1)S(1)}, u32[]{:S(2)}, u32[]{:S(2)}) collective-permute-start(bf16[800,256]{1,0:T(8,128)(2,1)S(1)} %get-tuple-element.120), channel_id=1, source_target_pairs={{0,2},{1,3},{2,0},{3,1},{4,6},{5,7},{6,4},{7,5},{8,10},{9,11},{10,... | collective-permute-start | bytes 1228808 | tf_op jit(solution)/shard_map/ppermute | solution.py:539
  65.2 22.3 %collective-permute-start.20 = (bf16[1800,128]{1,0:T(8,128)(2,1)S(1)}, bf16[1800,128]{1,0:T(8,128)(2,1)S(1)}, u32[]{:S(2)}, u32[]{:S(2)}) collective-permute-start(bf16[1800,128]{1,0:T(8,128)(2,1)S(1)} %fusion.2), channel_id=1, source_target_pairs={{0,16},{4,20},{8,24},{12,28},{16,0},{20,4},{24,8},{28,12},{1,17},{... | collective-permute-start | bytes 1382408 | tf_op jit(solution)/shard_map/ppermute | solution.py:539
  70.9 9.4 %collective-permute-start.19 = (bf16[2,400,128]{2,1,0:T(8,128)(2,1)}, bf16[2,400,128]{2,1,0:T(8,128)(2,1)S(1)}, u32[]{:S(2)}, u32[]{:S(2)}) collective-permute-start(bf16[2,400,128]{2,1,0:T(8,128)(2,1)} %get-tuple-element.96), channel_id=1, source_target_pairs={{0,4},{1,9},{2,6},{3,11},{4,0},{5,13},{6,2},{7,15},{8,12},{9,1},{1... | collective-permute-start | bytes 614408 | tf_op jit(solution)/shard_map/ppermute | solution.py:571
  74.6 16.9 %copy-start.15 = (f32[400,128]{1,0:T(8,128)S(1)}, f32[400,128]{1,0:T(8,128)}, u32[]{:S(2)}) copy-start(f32[400,128]{1,0:T(8,128)} %get-tuple-element.101) | copy-start | bytes 614404
  77.3 19.7 %copy-start.16 = (f32[400,128]{1,0:T(8,128)S(1)}, f32[400,128]{1,0:T(8,128)}, u32[]{:S(2)}) copy-start(f32[400,128]{1,0:T(8,128)} %get-tuple-element.99) | copy-start | bytes 614404
  87.6 8.2 %collective-permute-start.22 = (bf16[1800,128]{1,0:T(8,128)(2,1)S(1)}, bf16[1800,128]{1,0:T(8,128)(2,1)S(1)}, u32[]{:S(2)}, u32[]{:S(2)}) collective-permute-start(bf16[1800,128]{1,0:T(8,128)(2,1)S(1)} %add_convert_fusion), channel_id=1, source_target_pairs={{0,8},{1,5},{2,10},{3,7},{4,12},{5,1},{6,14},{7,3},{8,0},{9,13},{1... | collective-permute-start | bytes 1382408 | tf_op jit(solution)/shard_map/ppermute | solution.py:571
  89.4 5.0 %collective-permute-start.25 = (bf16[160,256]{1,0:T(8,128)(2,1)S(1)}, bf16[160,256]{1,0:T(8,128)(2,1)S(1)}, u32[]{:S(2)}, u32[]{:S(2)}) collective-permute-start(bf16[160,256]{1,0:T(8,128)(2,1)S(1)} %copy-done.29), channel_id=1, source_target_pairs={{0,3},{1,2},{2,1},{3,0},{4,7},{5,6},{6,5},{7,4},{8,11},{9,10},{10,... | collective-permute-start | bytes 245768 | tf_op jit(solution)/shard_map/ppermute | solution.py:539
  90.7 5.2 %collective-permute-start.24 = (bf16[160,256]{1,0:T(8,128)(2,1)S(1)}, bf16[160,256]{1,0:T(8,128)(2,1)S(1)}, u32[]{:S(2)}, u32[]{:S(2)}) collective-permute-start(bf16[160,256]{1,0:T(8,128)(2,1)S(1)} %copy-done.28), channel_id=1, source_target_pairs={{0,2},{1,3},{2,0},{3,1},{4,6},{5,7},{6,4},{7,5},{8,10},{9,11},{10,... | collective-permute-start | bytes 245768 | tf_op jit(solution)/shard_map/ppermute | solution.py:539
  91.3 4.6 %collective-permute-start.23 = (bf16[160,256]{1,0:T(8,128)(2,1)S(1)}, bf16[160,256]{1,0:T(8,128)(2,1)S(1)}, u32[]{:S(2)}, u32[]{:S(2)}) collective-permute-start(bf16[160,256]{1,0:T(8,128)(2,1)S(1)} %copy-done.27), channel_id=1, source_target_pairs={{0,1},{1,0},{2,3},{3,2},{4,5},{5,4},{6,7},{7,6},{8,9},{9,8},{10,11... | collective-permute-start | bytes 245768 | tf_op jit(solution)/shard_map/ppermute | solution.py:539
  91.6 5.4 %collective-permute-start.21 = (bf16[400,128]{1,0:T(8,128)(2,1)S(1)}, bf16[400,128]{1,0:T(8,128)(2,1)S(1)}, u32[]{:S(2)}, u32[]{:S(2)}) collective-permute-start(bf16[400,128]{1,0:T(8,128)(2,1)S(1)} %fusion.4), channel_id=1, source_target_pairs={{0,8},{1,5},{2,10},{3,7},{4,12},{5,1},{6,14},{7,3},{8,0},{9,13},{1... | collective-permute-start | bytes 307208 | tf_op jit(solution)/shard_map/ppermute | solution.py:571
  96.0 28.8 %collective-permute-start.26 = (bf16[2,1800,128]{2,1,0:T(8,128)(2,1)S(1)}, bf16[2,1800,128]{2,1,0:T(8,128)(2,1)S(1)}, u32[]{:S(2)}, u32[]{:S(2)}) collective-permute-start(bf16[2,1800,128]{2,1,0:T(8,128)(2,1)S(1)} %pad_maximum_fusion.p_ref), channel_id=1, source_target_pairs={{0,4},{1,9},{2,6},{3,11},{4,0},{5,13},{6,2},{7,15},{8,12},{9,1},{1... | collective-permute-start | bytes 2764808 | tf_op jit(solution)/shard_map/ppermute | solution.py:571
  97.0 13.6 %collective-permute-start.27 = (bf16[400,128]{1,0:T(8,128)(2,1)S(1)}, bf16[400,128]{1,0:T(8,128)(2,1)S(1)}, u32[]{:S(2)}, u32[]{:S(2)}) collective-permute-start(bf16[400,128]{1,0:T(8,128)(2,1)S(1)} %fusion.6), channel_id=1, source_target_pairs={{0,16},{4,20},{8,24},{12,28},{16,0},{20,4},{24,8},{28,12},{1,17},{... | collective-permute-start | bytes 307208 | tf_op jit(solution)/shard_map/ppermute | solution.py:539
  110.7 4.7 %collective-permute-start.28 = (bf16[400,128]{1,0:T(8,128)(2,1)S(1)}, bf16[400,128]{1,0:T(8,128)(2,1)S(1)}, u32[]{:S(2)}, u32[]{:S(2)}) collective-permute-start(bf16[400,128]{1,0:T(8,128)(2,1)S(1)} %add_convert_fusion.1), channel_id=1, source_target_pairs={{0,8},{1,5},{2,10},{3,7},{4,12},{5,1},{6,14},{7,3},{8,0},{9,13},{1... | collective-permute-start | bytes 307208 | tf_op jit(solution)/shard_map/ppermute | solution.py:571
  115.5 6.5 %collective-permute-start.29 = (bf16[2,400,128]{2,1,0:T(8,128)(2,1)S(1)}, bf16[2,400,128]{2,1,0:T(8,128)(2,1)S(1)}, u32[]{:S(2)}, u32[]{:S(2)}) collective-permute-start(bf16[2,400,128]{2,1,0:T(8,128)(2,1)S(1)} %pad_maximum_fusion.1.refs_0_), channel_id=1, source_target_pairs={{0,4},{1,9},{2,6},{3,11},{4,0},{5,13},{6,2},{7,15},{8,12},{9,1},{1... | collective-permute-start | bytes 614408 | tf_op jit(solution)/shard_map/ppermute | solution.py:571
  (31 other events, 191.6 us)

commit v5 on v4

--- a/solution.py
+++ b/solution.py
@@ -608,23 +608,23 @@
     img_sets = turn_images(ids, source, group, own)
     cots = gather(cotangent.reshape(few, wide), "shard", img_sets[0])
     own_images = exchange(img_sets, "shard", group)
+    w_tap, w_turned = turn_filters(after(conv_weight, img_sets[0]))
     back, cots = back_product(after(ids, *own_images), cots, skip_weight)
     backs = [back] + [flip(back, "shard", j) for j in range(1, group)]
     patch = make_patches([after(piece, back) for piece in own_images], width)
     hidden_cots = hidden_cot.reshape(pixels, chans)
-    hidden_cots = gather(after(hidden_cots, *own_images[2:]), "shard", patch, *backs)
+    hidden_cots = gather(after(hidden_cots, *own_images[2:], w_tap), "shard", patch, *backs)
 
     hidden_grad, keep_0, keep_2, send_g = filter_grad(
         after(ids, patch), patch, hidden_cots, backs, width, few
     )
     got_g = hop(send_g, 1)
-    w_tap, w_turned = turn_filters(after(conv_weight, send_g))
-    *keep, send = forward(ids, patch, w_turned, pixels, width, few)
+    *keep, send = forward(after(ids, send_g), patch, w_turned, pixels, width, few)
     skips = gather(after(skip_weight, send_g), "shard")
     got_g = after(got_g, send, skips[2])
     mid_g = (keep_2 + got_g[1].astype(F32)).astype(BF)
     last_g = hop(mid_g, 2)
-    keep, last, got = sum_scatter(keep, after(send, mid_g))
+    keep, last, got = sum_scatter(keep, send)
     own_input = image_grad(after(ids, last), hidden_grad, own_images, w_tap, width)
     last_g = after(last_g, own_input[0], got, *skips)
     sum_g = (keep_0 + got_g[0].astype(F32) + last_g.astype(F32)).astype(BF)
@@ -654,11 +654,9 @@
     first = place_grad(after(ids, full_s), (0, 2), pair, own, chans, factor)
     pair_s = jnp.stack([full_s, after(across_s, first[0])])
     rest_s = hop(pair_s, 1)
-    skip_grad = place_skip(
-        ids, [((0, 2), pair_s), ((1, 3), rest_s)], own, wide, factor
-    )
-    rest = after(rest, skip_grad)
     conv_grad = place_grad(ids, (1, 3), rest, own, chans, factor, first)
+    rest_s = after(rest_s, conv_grad)
+    skip_grad = place_skip(ids, [((0, 2), pair_s), ((1, 3), rest_s)], own, wide, factor)
 
     return (
         hidden.reshape(images.shape),

time: 129 us -> 122 us (0.946)
  waiting for transfers between devices: 37.6 us -> 30.5 us
    ppermute x22, waiting for transfers between devices: 31.4 us -> 27.3 us  [flip(): lax.ppermute(value, axis, [(i, i ^ bit) for i in range(lax.axis_size(axis...]
    ppermute x8, waiting for transfers between devices: 6.17 us -> 3.13 us  [hop(): return lax.ppermute(value, ('rep', 'shard'), pairs)]
    ppermute x8, starting transfers between devices: 10.5 us -> 8.9 us  [hop(): return lax.ppermute(value, ('rep', 'shard'), pairs)]
    ppermute x22, starting transfers between devices: 20.8 us -> 22.2 us  [flip(): lax.ppermute(value, axis, [(i, i ^ bit) for i in range(lax.axis_size(axis...]
    unnamed x66 -> x70, local copies, waits for them, and re-layouts: 3.84 us -> 3.84 us
  transfers between devices with their start and end apart: 30 -> 30, of which waited for: 13 -> 11; matrix products, arithmetic and copies ran while one was open for 2% -> 2% of each run, Pallas kernels for 33% -> 36%
where the time goes in v5:
time: 122 us; the launch traced here: 121 us
  Pallas kernels  52.7 us (43%)
  starting transfers between devices  31.1 us (25%)
  waiting for transfers between devices  30.5 us (25%)
  local copies, waits for them, and re-layouts  3.84 us (3%)
  other arithmetic  2.34 us (2%)
    pallas_call x12, Pallas kernels, call(): pl.pallas_call(body, out_shape=outs, in_specs=specs, out_specs=jax.tree.m...  46 us
    ppermute x22, waiting for transfers between devices, flip(): lax.ppermute(value, axis, [(i, i ^ bit) for i in range(lax.axis_size(axis...  27.3 us
    ppermute x22, starting transfers between devices, flip(): lax.ppermute(value, axis, [(i, i ^ bit) for i in range(lax.axis_size(axis...  22.2 us
    ppermute x8, starting transfers between devices, hop(): return lax.ppermute(value, ('rep', 'shard'), pairs)  8.9 us
    pallas_call x2, Pallas kernels, place_grad(): pl.pallas_call(body, out_shape=shape((rows, chans), F32) if final else [s...  6.76 us
    unnamed x70, local copies, waits for them, and re-layouts  3.84 us
    ppermute x8, waiting for transfers between devices, hop(): return lax.ppermute(value, ('rep', 'shard'), pairs)  3.13 us
  transfers between devices with their start and end apart: 30, of which 11 were waited for; matrix products, arithmetic and copies ran while one was open for 2% of the time, Pallas kernels for 36%

profile of v5, /device:TPU:1, one launch (start us, length us, event | category | flops | bytes accessed | tf_op | source)
XLA Modules:
  0.0 121.5 jit_solution(8086620015394019540)
XLA Ops:
  0.7 2.1 %collective-permute-start.4 = (bf16[64,1280]{1,0:T(8,128)(2,1)}, bf16[64,1280]{1,0:T(8,128)(2,1)S(1)}, u32[]{:S(2)}, u32[]{:S(2)}) collective-permute-start(bf16[64,1280]{1,0:T(8,128)(2,1)} %bitcast.40), channel_id=1, source_target_pairs={{0,2},{1,3},{2,0},{3,1},{4,6},{5,7},{6,4},{7,5},{8,10},{9,11},{10,... | collective-permute-start | bytes 491528 | tf_op jit(solution)/shard_map/ppermute | solution.py:539
  3.4 1.9 %turn_images.1 = (bf16[160,256]{1,0:T(8,128)(2,1)}, bf16[160,256]{1,0:T(8,128)(2,1)}, bf16[160,256]{1,0:T(8,128)(2,1)}, bf16[160,256]{1,0:T(8,128)(2,1)}) custom-call(s32[2]{0:T(128)} %pad_add_fusion.id_ref, bf16[256,640]{1,0:T(8,128)(2,1)} %bitcast.35), custom_call_target="tpu_custom_call" | custom-call | bytes 655360 | tf_op jit(solution)/shard_map/turn_images/pallas_call | solution.py:30
  5.4 2.5 %collective-permute-start.2 = (bf16[160,256]{1,0:T(8,128)(2,1)}, bf16[160,256]{1,0:T(8,128)(2,1)S(1)}, u32[]{:S(2)}, u32[]{:S(2)}) collective-permute-start(bf16[160,256]{1,0:T(8,128)(2,1)} %get-tuple-element.65), channel_id=1, source_target_pairs={{0,3},{1,2},{2,1},{3,0},{4,7},{5,6},{6,5},{7,4},{8,11},{9,10},{10,... | collective-permute-start | bytes 245768 | tf_op jit(solution)/shard_map/ppermute | solution.py:539
  7.9 4.1 %turn_filters.1 = (bf16[1440,640]{1,0:T(8,128)(2,1)}, bf16[640,1440]{1,0:T(8,128)(2,1)}) custom-call(bf16[1440,640]{1,0:T(8,128)(2,1)} %w_ref), custom_call_target="tpu_custom_call" | custom-call | bytes 5529600 | tf_op jit(solution)/shard_map/turn_filters/pallas_call | solution.py:30
  16.4 2.3 %back_product.1 = (bf16[160,256]{1,0:T(8,128)(2,1)}, bf16[256,1280]{1,0:T(8,128)(2,1)}) custom-call(s32[2]{0:T(128)} %pad_add_fusion.id_ref, bf16[160,1280]{1,0:T(8,128)(2,1)} %refs_0_, bf16[64,1280]{1,0:T(8,128)(2,1)} %bitcast.41, bf16[64,1280]{1,0:T(8,128)(2,1)} %copy-done.20, bf16[64,1280]{1,0:T(8,128)(2,1)} %copy-done.19, bf16[64,1280]{1,0:T(8,128)(2,1)} %copy-done.21), custom_call_target="tpu_custom_call" | custom-call | flops 104857600 | bytes 655360 | tf_op jit(solution)/shard_map/back_product/pallas_call | solution.py:30
  20.9 3.6 %make_patches.1.p_ref = bf16[1440,1024]{1,0:T(8,128)(2,1)} custom-call(bf16[160,256]{1,0:T(8,128)(2,1)} %get-tuple-element.69.refs_0_, bf16[160,256]{1,0:T(8,128)(2,1)} %copy-done.14, bf16[160,256]{1,0:T(8,128)(2,1)} %copy-done.12, bf16[160,256]{1,0:T(8,128)(2,1)} %copy-done.13), custom_call_target="tpu_custom_call" | custom-call | bytes 3276800 | tf_op jit(solution)/shard_map/make_patches/pallas_call | solution.py:30
  25.8 1.3 %collective-permute-done.11.refs_3_ = bf16[256,640]{1,0:T(8,128)(2,1)S(1)} collective-permute-done((bf16[256,640]{1,0:T(8,128)(2,1)S(1)}, bf16[256,640]{1,0:T(8,128)(2,1)S(1)}, u32[]{:S(2)}, u32[]{:S(2)}) %collective-permute-start.11) | collective-permute-done | bytes 327712 | tf_op jit(solution)/shard_map/ppermute | solution.py:539
  27.8 7.4 %filter_grad.1 = (bf16[1024,640]{1,0:T(8,128)(2,1)}, f32[1800,128]{1,0:T(8,128)}, f32[1800,128]{1,0:T(8,128)}, bf16[2,1800,128]{2,1,0:T(8,128)(2,1)}) custom-call(s32[2]{0:T(128)} %pad_add_fusion.id_ref, bf16[1440,1024]{1,0:T(8,128)(2,1)} %make_patches.1.p_ref, bf16[256,640]{1,0:T(8,128)(2,1)} %bitcast.45, bf16[256,640]{1,0:T(8,128)(2,1)} %copy-done.27, ...), custom_call_target="tpu_custom_call" | custom-call | flops 1887436800 | bytes 5386240 | tf_op jit(solution)/shard_map/filter_grad/pallas_call | solution.py:30
  35.2 1.4 %collective-permute-start.12 = (bf16[2,1800,128]{2,1,0:T(8,128)(2,1)}, bf16[2,1800,128]{2,1,0:T(8,128)(2,1)S(1)}, u32[]{:S(2)}, u32[]{:S(2)}) collective-permute-start(bf16[2,1800,128]{2,1,0:T(8,128)(2,1)} %get-tuple-element.79), channel_id=1, source_target_pairs={{0,4},{1,9},{2,6},{3,11},{4,0},{5,13},{6,2},{7,15},{8,12},{9,1},{1... | collective-permute-start | bytes 2764808 | tf_op jit(solution)/shard_map/ppermute | solution.py:571
  37.1 8.3 %forward.1 = (f32[800,256]{1,0:T(8,128)}, f32[800,256]{1,0:T(8,128)}, bf16[2,800,256]{2,1,0:T(8,128)(2,1)}) custom-call(s32[2]{0:T(128)} %pad_add_fusion.id_ref, bf16[640,1440]{1,0:T(8,128)(2,1)} %get-tuple-element.81.w_ref, bf16[1440,1024]{1,0:T(8,128)(2,1)} %make_patches.1.p_ref), custom_call_target="tpu_custom_call" | custom-call | flops 2642411520 | bytes 1966080 | tf_op jit(solution)/shard_map/forward/pallas_call | solution.py:30
  47.0 1.5 %collective-permute-start.18 = (bf16[160,1280]{1,0:T(8,128)(2,1)S(1)}, bf16[160,1280]{1,0:T(8,128)(2,1)S(1)}, u32[]{:S(2)}, u32[]{:S(2)}) collective-permute-start(bf16[160,1280]{1,0:T(8,128)(2,1)S(1)} %collective-permute-done.13.refs_2_), channel_id=1, source_target_pairs={{0,1},{1,0},{2,3},{3,2},{4,5},{5,4},{6,7},{7,6},{8,9},{9,8},{10,11... | collective-permute-start | bytes 1228808 | tf_op jit(solution)/shard_map/ppermute | solution.py:539
  48.6 1.3 %collective-permute-start.14 = (bf16[1800,128]{1,0:T(8,128)(2,1)S(1)}, bf16[1800,128]{1,0:T(8,128)(2,1)S(1)}, u32[]{:S(2)}, u32[]{:S(2)}) collective-permute-start(bf16[1800,128]{1,0:T(8,128)(2,1)S(1)} %fusion), channel_id=1, source_target_pairs={{0,8},{1,5},{2,10},{3,7},{4,12},{5,1},{6,14},{7,3},{8,0},{9,13},{1... | collective-permute-start | bytes 1382408 | tf_op jit(solution)/shard_map/ppermute | solution.py:571
  51.5 6.0 %image_grad.1 = (bf16[160,256]{1,0:T(8,128)(2,1)}, bf16[160,256]{1,0:T(8,128)(2,1)}, bf16[160,256]{1,0:T(8,128)(2,1)}, bf16[160,256]{1,0:T(8,128)(2,1)}) custom-call(s32[2]{0:T(128)} %pad_add_fusion.id_ref, bf16[1024,640]{1,0:T(8,128)(2,1)} %get-tuple-element.88.h_ref, bf16[1440,640]{1,0:T(8,128)(2,1)} %get-tuple-element.75.w_ref, ...), custom_call_target="tpu_custom_call" | custom-call | flops 1887436800 | bytes 1310720 | tf_op jit(solution)/shard_map/image_grad/pallas_call | solution.py:30
  57.5 3.3 %collective-permute-done.16.g_ref = bf16[800,256]{1,0:T(8,128)(2,1)S(1)} collective-permute-done((bf16[800,256]{1,0:T(8,128)(2,1)S(1)}, bf16[800,256]{1,0:T(8,128)(2,1)S(1)}, u32[]{:S(2)}, u32[]{:S(2)}) %collective-permute-start.16) | collective-permute-done | bytes 409632 | tf_op jit(solution)/shard_map/ppermute | solution.py:539
  60.9 2.4 %collective-permute-start.20 = (bf16[1800,128]{1,0:T(8,128)(2,1)S(1)}, bf16[1800,128]{1,0:T(8,128)(2,1)S(1)}, u32[]{:S(2)}, u32[]{:S(2)}) collective-permute-start(bf16[1800,128]{1,0:T(8,128)(2,1)S(1)} %fusion.2), channel_id=1, source_target_pairs={{0,16},{4,20},{8,24},{12,28},{16,0},{20,4},{24,8},{28,12},{1,17},{... | collective-permute-start | bytes 1382408 | tf_op jit(solution)/shard_map/ppermute | solution.py:539
  63.3 3.3 %skip_grad_term.1 = (f32[400,128]{1,0:T(8,128)}, f32[400,128]{1,0:T(8,128)}, bf16[2,400,128]{2,1,0:T(8,128)(2,1)}) custom-call(s32[2]{0:T(128)} %pad_add_fusion.id_ref, f32[800,256]{1,0:T(8,128)} %get-tuple-element.119.k_ref, bf16[800,256]{1,0:T(8,128)(2,1)} %copy-done.1, bf16[256,1280]{1,0:T(8,128)(2,1)} %get-tuple-element.95.c_ref, ...), custom_call_target="tpu_custom_call" | custom-call | flops 104857600 | bytes 819200 | tf_op jit(solution)/shard_map/skip_grad_term/pallas_call | solution.py:30
  66.6 1.8 %collective-permute-start.19 = (bf16[2,400,128]{2,1,0:T(8,128)(2,1)}, bf16[2,400,128]{2,1,0:T(8,128)(2,1)S(1)}, u32[]{:S(2)}, u32[]{:S(2)}) collective-permute-start(bf16[2,400,128]{2,1,0:T(8,128)(2,1)} %get-tuple-element.96), channel_id=1, source_target_pairs={{0,4},{1,9},{2,6},{3,11},{4,0},{5,13},{6,2},{7,15},{8,12},{9,1},{1... | collective-permute-start | bytes 614408 | tf_op jit(solution)/shard_map/ppermute | solution.py:571
  68.4 2.3 %finish_hidden.1 = (bf16[256,640]{1,0:T(8,128)(2,1)}, bf16[64,640]{1,0:T(8,128)(2,1)}) custom-call(bf16[256,640]{1,0:T(8,128)(2,1)} %bitcast.36, f32[800,256]{1,0:T(8,128)} %get-tuple-element.119.k_ref, bf16[800,256]{1,0:T(8,128)(2,1)} %copy-done.1), custom_call_target="tpu_custom_call" | custom-call | flops 20971520 | bytes 1638400 | tf_op jit(solution)/shard_map/finish_hidden/pallas_call | solution.py:30
  70.7 2.7 %project.1 = bf16[64,1280]{1,0:T(8,128)(2,1)} custom-call(s32[2]{0:T(128)} %pad_add_fusion.id_ref, bf16[64,640]{1,0:T(8,128)(2,1)} %get-tuple-element.97.s_ref, bf16[160,1280]{1,0:T(8,128)(2,1)} %refs_0_, bf16[160,1280]{1,0:T(8,128)(2,1)} %copy-done.10, bf16[160,1280]{1,0:T(8,128)(2,1)} %copy-done.9, bf16[160,1280]{1,0:T(8,128)(2,1)} %copy-done.11), custom_call_target="tpu_custom_call" | custom-call | flops 104857600 | bytes 1638400 | tf_op jit(solution)/shard_map/project/pallas_call | solution.py:30
  73.4 2.2 %collective-permute-done.19 = bf16[2,400,128]{2,1,0:T(8,128)(2,1)S(1)} collective-permute-done((bf16[2,400,128]{2,1,0:T(8,128)(2,1)}, bf16[2,400,128]{2,1,0:T(8,128)(2,1)S(1)}, u32[]{:S(2)}, u32[]{:S(2)}) %collective-permute-start.19) | collective-permute-done | bytes 204832 | tf_op jit(solution)/shard_map/ppermute | solution.py:571
  75.7 7.1 %collective-permute-done.20 = bf16[1800,128]{1,0:T(8,128)(2,1)S(1)} collective-permute-done((bf16[1800,128]{1,0:T(8,128)(2,1)S(1)}, bf16[1800,128]{1,0:T(8,128)(2,1)S(1)}, u32[]{:S(2)}, u32[]{:S(2)}) %collective-permute-start.20) | collective-permute-done | bytes 460832 | tf_op jit(solution)/shard_map/ppermute | solution.py:539
  82.9 2.7 %collective-permute-start.23 = (bf16[160,256]{1,0:T(8,128)(2,1)S(1)}, bf16[160,256]{1,0:T(8,128)(2,1)S(1)}, u32[]{:S(2)}, u32[]{:S(2)}) collective-permute-start(bf16[160,256]{1,0:T(8,128)(2,1)S(1)} %copy-done.31), channel_id=1, source_target_pairs={{0,1},{1,0},{2,3},{3,2},{4,5},{5,4},{6,7},{7,6},{8,9},{9,8},{10,11... | collective-permute-start | bytes 245768 | tf_op jit(solution)/shard_map/ppermute | solution.py:539
  86.1 1.2 %collective-permute-start.25 = (bf16[160,256]{1,0:T(8,128)(2,1)S(1)}, bf16[160,256]{1,0:T(8,128)(2,1)S(1)}, u32[]{:S(2)}, u32[]{:S(2)}) collective-permute-start(bf16[160,256]{1,0:T(8,128)(2,1)S(1)} %copy-done.29), channel_id=1, source_target_pairs={{0,3},{1,2},{2,1},{3,0},{4,7},{5,6},{6,5},{7,4},{8,11},{9,10},{10,... | collective-permute-start | bytes 245768 | tf_op jit(solution)/shard_map/ppermute | solution.py:539
  87.5 2.2 %collective-permute-done.24.refs_2_ = bf16[160,256]{1,0:T(8,128)(2,1)S(1)} collective-permute-done((bf16[160,256]{1,0:T(8,128)(2,1)S(1)}, bf16[160,256]{1,0:T(8,128)(2,1)S(1)}, u32[]{:S(2)}, u32[]{:S(2)}) %collective-permute-start.24) | collective-permute-done | bytes 81952 | tf_op jit(solution)/shard_map/ppermute | solution.py:539
  89.6 2.2 %collective-permute-done.25.refs_3_ = bf16[160,256]{1,0:T(8,128)(2,1)S(1)} collective-permute-done((bf16[160,256]{1,0:T(8,128)(2,1)S(1)}, bf16[160,256]{1,0:T(8,128)(2,1)S(1)}, u32[]{:S(2)}, u32[]{:S(2)}) %collective-permute-start.25) | collective-permute-done | bytes 81952 | tf_op jit(solution)/shard_map/ppermute | solution.py:539
  93.2 2.7 %collective-permute-start.27 = (bf16[400,128]{1,0:T(8,128)(2,1)S(1)}, bf16[400,128]{1,0:T(8,128)(2,1)S(1)}, u32[]{:S(2)}, u32[]{:S(2)}) collective-permute-start(bf16[400,128]{1,0:T(8,128)(2,1)S(1)} %fusion.6), channel_id=1, source_target_pairs={{0,16},{4,20},{8,24},{12,28},{16,0},{20,4},{24,8},{28,12},{1,17},{... | collective-permute-start | bytes 307208 | tf_op jit(solution)/shard_map/ppermute | solution.py:539
  95.9 2.0 %finish_images.1 = bf16[256,640]{1,0:T(8,128)(2,1)} custom-call(s32[2]{0:T(128)} %pad_add_fusion.id_ref, bf16[160,256]{1,0:T(8,128)(2,1)} %get-tuple-element.103.refs_0_, bf16[160,256]{1,0:T(8,128)(2,1)} %copy-done.22, bf16[160,256]{1,0:T(8,128)(2,1)} %copy-done.23, bf16[160,256]{1,0:T(8,128)(2,1)} %copy-done.24), custom_call_target="tpu_custom_call" | custom-call | bytes 655360 | tf_op jit(solution)/shard_map/finish_images/pallas_call | solution.py:30
  97.9 8.9 %collective-permute-done.27 = bf16[400,128]{1,0:T(8,128)(2,1)S(1)} collective-permute-done((bf16[400,128]{1,0:T(8,128)(2,1)S(1)}, bf16[400,128]{1,0:T(8,128)(2,1)S(1)}, u32[]{:S(2)}, u32[]{:S(2)}) %collective-permute-start.27) | collective-permute-done | bytes 102432 | tf_op jit(solution)/shard_map/ppermute | solution.py:539
  106.9 3.7 %place_grad.2 = (f32[1440,640]{1,0:T(8,128)}, f32[4,360,128]{2,1,0:T(8,128)}) custom-call(s32[2]{0:T(128)} %pad_add_fusion.id_ref, bf16[2,1800,128]{2,1,0:T(8,128)(2,1)} %copy-done), custom_call_target="tpu_custom_call" | custom-call | bytes 2764800 | tf_op jit(solution)/shard_map/place_grad/pallas_call | solution.py:342
  111.5 3.1 %collective-permute-start.29 = (bf16[2,400,128]{2,1,0:T(8,128)(2,1)S(1)}, bf16[2,400,128]{2,1,0:T(8,128)(2,1)S(1)}, u32[]{:S(2)}, u32[]{:S(2)}) collective-permute-start(bf16[2,400,128]{2,1,0:T(8,128)(2,1)S(1)} %pad_maximum_fusion.1.refs_0_), channel_id=1, source_target_pairs={{0,4},{1,9},{2,6},{3,11},{4,0},{5,13},{6,2},{7,15},{8,12},{9,1},{1... | collective-permute-start | bytes 614408 | tf_op jit(solution)/shard_map/ppermute | solution.py:571
  115.6 3.1 %place_grad.3 = f32[1440,640]{1,0:T(8,128)} custom-call(s32[2]{0:T(128)} %pad_add_fusion.id_ref, bf16[2,1800,128]{2,1,0:T(8,128)(2,1)} %copy-done.5, f32[1440,640]{1,0:T(8,128)} %get-tuple-element.115.refs_0_, f32[4,360,128]{2,1,0:T(8,128)} %get-tuple-element.116.refs_1_), custom_call_target="tpu_custom_call", output_to_operand_aliasing={{}: (2, {})} | custom-call | bytes 2764800 | tf_op jit(solution)/shard_map/place_grad/pallas_call | solution.py:342
  119.4 2.0 %place_skip.1 = f32[160,1280]{1,0:T(8,128)} custom-call(s32[2]{0:T(128)} %pad_add_fusion.id_ref, bf16[2,400,128]{2,1,0:T(8,128)(2,1)} %copy-done.8, bf16[2,400,128]{2,1,0:T(8,128)(2,1)} %copy-done.17), custom_call_target="tpu_custom_call" | custom-call | bytes 1228800 | tf_op jit(solution)/shard_map/place_skip/pallas_call | solution.py:30
  (122 shorter events, 18.0 us)
Async XLA Ops:
  0.7 12.7 %collective-permute-start.4 = (bf16[64,1280]{1,0:T(8,128)(2,1)}, bf16[64,1280]{1,0:T(8,128)(2,1)S(1)}, u32[]{:S(2)}, u32[]{:S(2)}) collective-permute-start(bf16[64,1280]{1,0:T(8,128)(2,1)} %bitcast.40), channel_id=1, source_target_pairs={{0,2},{1,3},{2,0},{3,1},{4,6},{5,7},{6,4},{7,5},{8,10},{9,11},{10,... | collective-permute-start | bytes 491528 | tf_op jit(solution)/shard_map/ppermute | solution.py:539
  5.3 6.7 %collective-permute-start.1 = (bf16[160,256]{1,0:T(8,128)(2,1)}, bf16[160,256]{1,0:T(8,128)(2,1)S(1)}, u32[]{:S(2)}, u32[]{:S(2)}) collective-permute-start(bf16[160,256]{1,0:T(8,128)(2,1)} %get-tuple-element.64), channel_id=1, source_target_pairs={{0,2},{1,3},{2,0},{3,1},{4,6},{5,7},{6,4},{7,5},{8,10},{9,11},{10,... | collective-permute-start | bytes 245768 | tf_op jit(solution)/shard_map/ppermute | solution.py:539
  5.4 6.7 %collective-permute-start.2 = (bf16[160,256]{1,0:T(8,128)(2,1)}, bf16[160,256]{1,0:T(8,128)(2,1)S(1)}, u32[]{:S(2)}, u32[]{:S(2)}) collective-permute-start(bf16[160,256]{1,0:T(8,128)(2,1)} %get-tuple-element.65), channel_id=1, source_target_pairs={{0,3},{1,2},{2,1},{3,0},{4,7},{5,6},{6,5},{7,4},{8,11},{9,10},{10,... | collective-permute-start | bytes 245768 | tf_op jit(solution)/shard_map/ppermute | solution.py:539
  12.1 12.9 %collective-permute-start.7 = (bf16[256,640]{1,0:T(8,128)(2,1)S(1)}, bf16[256,640]{1,0:T(8,128)(2,1)S(1)}, u32[]{:S(2)}, u32[]{:S(2)}) collective-permute-start(bf16[256,640]{1,0:T(8,128)(2,1)S(1)} %bitcast.46), channel_id=1, source_target_pairs={{0,2},{1,3},{2,0},{3,1},{4,6},{5,7},{6,4},{7,5},{8,10},{9,11},{10,... | collective-permute-start | bytes 983048 | tf_op jit(solution)/shard_map/ppermute | solution.py:539
  12.6 2.4 %collective-permute-start.3 = (bf16[64,1280]{1,0:T(8,128)(2,1)S(1)}, bf16[64,1280]{1,0:T(8,128)(2,1)S(1)}, u32[]{:S(2)}, u32[]{:S(2)}) collective-permute-start(bf16[64,1280]{1,0:T(8,128)(2,1)S(1)} %bitcast.42), channel_id=1, source_target_pairs={{0,1},{1,0},{2,3},{3,2},{4,5},{5,4},{6,7},{7,6},{8,9},{9,8},{10,11... | collective-permute-start | bytes 491528 | tf_op jit(solution)/shard_map/ppermute | solution.py:539
  13.3 1.7 %collective-permute-start.5 = (bf16[64,1280]{1,0:T(8,128)(2,1)S(1)}, bf16[64,1280]{1,0:T(8,128)(2,1)S(1)}, u32[]{:S(2)}, u32[]{:S(2)}) collective-permute-start(bf16[64,1280]{1,0:T(8,128)(2,1)S(1)} %collective-permute-done.4.refs_2_), channel_id=1, source_target_pairs={{0,1},{1,0},{2,3},{3,2},{4,5},{5,4},{6,7},{7,6},{8,9},{9,8},{10,11... | collective-permute-start | bytes 491528 | tf_op jit(solution)/shard_map/ppermute | solution.py:539
  13.4 1.6 %collective-permute-start = (bf16[160,256]{1,0:T(8,128)(2,1)}, bf16[160,256]{1,0:T(8,128)(2,1)S(1)}, u32[]{:S(2)}, u32[]{:S(2)}) collective-permute-start(bf16[160,256]{1,0:T(8,128)(2,1)} %get-tuple-element.63), channel_id=1, source_target_pairs={{0,1},{1,0},{2,3},{3,2},{4,5},{5,4},{6,7},{7,6},{8,9},{9,8},{10,11... | collective-permute-start | bytes 245768 | tf_op jit(solution)/shard_map/ppermute | solution.py:539
  18.7 5.8 %collective-permute-start.10 = (bf16[160,256]{1,0:T(8,128)(2,1)}, bf16[160,256]{1,0:T(8,128)(2,1)S(1)}, u32[]{:S(2)}, u32[]{:S(2)}) collective-permute-start(bf16[160,256]{1,0:T(8,128)(2,1)} %get-tuple-element.68.refs_4_), channel_id=1, source_target_pairs={{0,3},{1,2},{2,1},{3,0},{4,7},{5,6},{6,5},{7,4},{8,11},{9,10},{10,... | collective-permute-start | bytes 245768 | tf_op jit(solution)/shard_map/ppermute | solution.py:539
  19.4 5.6 %collective-permute-start.9 = (bf16[160,256]{1,0:T(8,128)(2,1)}, bf16[160,256]{1,0:T(8,128)(2,1)S(1)}, u32[]{:S(2)}, u32[]{:S(2)}) collective-permute-start(bf16[160,256]{1,0:T(8,128)(2,1)} %get-tuple-element.68.refs_4_), channel_id=1, source_target_pairs={{0,2},{1,3},{2,0},{3,1},{4,6},{5,7},{6,4},{7,5},{8,10},{9,11},{10,... | collective-permute-start | bytes 245768 | tf_op jit(solution)/shard_map/ppermute | solution.py:539
  20.4 4.6 %collective-permute-start.8 = (bf16[160,256]{1,0:T(8,128)(2,1)}, bf16[160,256]{1,0:T(8,128)(2,1)S(1)}, u32[]{:S(2)}, u32[]{:S(2)}) collective-permute-start(bf16[160,256]{1,0:T(8,128)(2,1)} %get-tuple-element.68.refs_4_), channel_id=1, source_target_pairs={{0,1},{1,0},{2,3},{3,2},{4,5},{5,4},{6,7},{7,6},{8,9},{9,8},{10,11... | collective-permute-start | bytes 245768 | tf_op jit(solution)/shard_map/ppermute | solution.py:539
  20.9 4.9 %collective-permute-start.6 = (bf16[256,640]{1,0:T(8,128)(2,1)S(1)}, bf16[256,640]{1,0:T(8,128)(2,1)S(1)}, u32[]{:S(2)}, u32[]{:S(2)}) collective-permute-start(bf16[256,640]{1,0:T(8,128)(2,1)S(1)} %bitcast.47), channel_id=1, source_target_pairs={{0,1},{1,0},{2,3},{3,2},{4,5},{5,4},{6,7},{7,6},{8,9},{9,8},{10,11... | collective-permute-start | bytes 983048 | tf_op jit(solution)/shard_map/ppermute | solution.py:539
  25.0 2.0 %collective-permute-start.11 = (bf16[256,640]{1,0:T(8,128)(2,1)S(1)}, bf16[256,640]{1,0:T(8,128)(2,1)S(1)}, u32[]{:S(2)}, u32[]{:S(2)}) collective-permute-start(bf16[256,640]{1,0:T(8,128)(2,1)S(1)} %collective-permute-done.7.refs_2_), channel_id=1, source_target_pairs={{0,1},{1,0},{2,3},{3,2},{4,5},{5,4},{6,7},{7,6},{8,9},{9,8},{10,11... | collective-permute-start | bytes 983048 | tf_op jit(solution)/shard_map/ppermute | solution.py:539
  35.2 13.2 %collective-permute-start.12 = (bf16[2,1800,128]{2,1,0:T(8,128)(2,1)}, bf16[2,1800,128]{2,1,0:T(8,128)(2,1)S(1)}, u32[]{:S(2)}, u32[]{:S(2)}) collective-permute-start(bf16[2,1800,128]{2,1,0:T(8,128)(2,1)} %get-tuple-element.79), channel_id=1, source_target_pairs={{0,4},{1,9},{2,6},{3,11},{4,0},{5,13},{6,2},{7,15},{8,12},{9,1},{1... | collective-permute-start | bytes 2764808 | tf_op jit(solution)/shard_map/ppermute | solution.py:571
  36.6 10.4 %collective-permute-start.13 = (bf16[160,1280]{1,0:T(8,128)(2,1)S(1)}, bf16[160,1280]{1,0:T(8,128)(2,1)S(1)}, u32[]{:S(2)}, u32[]{:S(2)}) collective-permute-start(bf16[160,1280]{1,0:T(8,128)(2,1)S(1)} %copy-done.2), channel_id=1, source_target_pairs={{0,2},{1,3},{2,0},{3,1},{4,6},{5,7},{6,4},{7,5},{8,10},{9,11},{10,... | collective-permute-start | bytes 1228808 | tf_op jit(solution)/shard_map/ppermute | solution.py:539
  45.3 4.6 %collective-permute-start.15 = (bf16[2,800,256]{2,1,0:T(8,128)(2,1)}, bf16[2,800,256]{2,1,0:T(8,128)(2,1)S(1)}, u32[]{:S(2)}, u32[]{:S(2)}) collective-permute-start(bf16[2,800,256]{2,1,0:T(8,128)(2,1)} %get-tuple-element.82), channel_id=1, source_target_pairs={{0,1},{1,0},{2,3},{3,2},{4,5},{5,4},{6,7},{7,6},{8,9},{9,8},{10,11... | collective-permute-start | bytes 2457608 | tf_op jit(solution)/shard_map/ppermute | solution.py:539
  46.2 11.2 %collective-permute-start.17 = (bf16[160,1280]{1,0:T(8,128)(2,1)S(1)}, bf16[160,1280]{1,0:T(8,128)(2,1)S(1)}, u32[]{:S(2)}, u32[]{:S(2)}) collective-permute-start(bf16[160,1280]{1,0:T(8,128)(2,1)S(1)} %copy-done.2), channel_id=1, source_target_pairs={{0,1},{1,0},{2,3},{3,2},{4,5},{5,4},{6,7},{7,6},{8,9},{9,8},{10,11... | collective-permute-start | bytes 1228808 | tf_op jit(solution)/shard_map/ppermute | solution.py:539
  47.0 10.4 %collective-permute-start.18 = (bf16[160,1280]{1,0:T(8,128)(2,1)S(1)}, bf16[160,1280]{1,0:T(8,128)(2,1)S(1)}, u32[]{:S(2)}, u32[]{:S(2)}) collective-permute-start(bf16[160,1280]{1,0:T(8,128)(2,1)S(1)} %collective-permute-done.13.refs_2_), channel_id=1, source_target_pairs={{0,1},{1,0},{2,3},{3,2},{4,5},{5,4},{6,7},{7,6},{8,9},{9,8},{10,11... | collective-permute-start | bytes 1228808 | tf_op jit(solution)/shard_map/ppermute | solution.py:539
  48.6 12.2 %collective-permute-start.14 = (bf16[1800,128]{1,0:T(8,128)(2,1)S(1)}, bf16[1800,128]{1,0:T(8,128)(2,1)S(1)}, u32[]{:S(2)}, u32[]{:S(2)}) collective-permute-start(bf16[1800,128]{1,0:T(8,128)(2,1)S(1)} %fusion), channel_id=1, source_target_pairs={{0,8},{1,5},{2,10},{3,7},{4,12},{5,1},{6,14},{7,3},{8,0},{9,13},{1... | collective-permute-start | bytes 1382408 | tf_op jit(solution)/shard_map/ppermute | solution.py:571
  51.0 9.8 %collective-permute-start.16 = (bf16[800,256]{1,0:T(8,128)(2,1)S(1)}, bf16[800,256]{1,0:T(8,128)(2,1)S(1)}, u32[]{:S(2)}, u32[]{:S(2)}) collective-permute-start(bf16[800,256]{1,0:T(8,128)(2,1)S(1)} %get-tuple-element.120), channel_id=1, source_target_pairs={{0,2},{1,3},{2,0},{3,1},{4,6},{5,7},{6,4},{7,5},{8,10},{9,11},{10,... | collective-permute-start | bytes 1228808 | tf_op jit(solution)/shard_map/ppermute | solution.py:539
  60.9 21.8 %collective-permute-start.20 = (bf16[1800,128]{1,0:T(8,128)(2,1)S(1)}, bf16[1800,128]{1,0:T(8,128)(2,1)S(1)}, u32[]{:S(2)}, u32[]{:S(2)}) collective-permute-start(bf16[1800,128]{1,0:T(8,128)(2,1)S(1)} %fusion.2), channel_id=1, source_target_pairs={{0,16},{4,20},{8,24},{12,28},{16,0},{20,4},{24,8},{28,12},{1,17},{... | collective-permute-start | bytes 1382408 | tf_op jit(solution)/shard_map/ppermute | solution.py:539
  66.6 9.1 %collective-permute-start.19 = (bf16[2,400,128]{2,1,0:T(8,128)(2,1)}, bf16[2,400,128]{2,1,0:T(8,128)(2,1)S(1)}, u32[]{:S(2)}, u32[]{:S(2)}) collective-permute-start(bf16[2,400,128]{2,1,0:T(8,128)(2,1)} %get-tuple-element.96), channel_id=1, source_target_pairs={{0,4},{1,9},{2,6},{3,11},{4,0},{5,13},{6,2},{7,15},{8,12},{9,1},{1... | collective-permute-start | bytes 614408 | tf_op jit(solution)/shard_map/ppermute | solution.py:571
  70.7 16.6 %copy-start.15 = (f32[400,128]{1,0:T(8,128)S(1)}, f32[400,128]{1,0:T(8,128)}, u32[]{:S(2)}) copy-start(f32[400,128]{1,0:T(8,128)} %get-tuple-element.101) | copy-start | bytes 614404
  73.4 19.7 %copy-start.16 = (f32[400,128]{1,0:T(8,128)S(1)}, f32[400,128]{1,0:T(8,128)}, u32[]{:S(2)}) copy-start(f32[400,128]{1,0:T(8,128)} %get-tuple-element.99) | copy-start | bytes 614404
  82.8 9.0 %collective-permute-start.22 = (bf16[1800,128]{1,0:T(8,128)(2,1)S(1)}, bf16[1800,128]{1,0:T(8,128)(2,1)S(1)}, u32[]{:S(2)}, u32[]{:S(2)}) collective-permute-start(bf16[1800,128]{1,0:T(8,128)(2,1)S(1)} %add_convert_fusion), channel_id=1, source_target_pairs={{0,8},{1,5},{2,10},{3,7},{4,12},{5,1},{6,14},{7,3},{8,0},{9,13},{1... | collective-permute-start | bytes 1382408 | tf_op jit(solution)/shard_map/ppermute | solution.py:571
  82.9 4.5 %collective-permute-start.23 = (bf16[160,256]{1,0:T(8,128)(2,1)S(1)}, bf16[160,256]{1,0:T(8,128)(2,1)S(1)}, u32[]{:S(2)}, u32[]{:S(2)}) collective-permute-start(bf16[160,256]{1,0:T(8,128)(2,1)S(1)} %copy-done.31), channel_id=1, source_target_pairs={{0,1},{1,0},{2,3},{3,2},{4,5},{5,4},{6,7},{7,6},{8,9},{9,8},{10,11... | collective-permute-start | bytes 245768 | tf_op jit(solution)/shard_map/ppermute | solution.py:539
  85.6 4.0 %collective-permute-start.24 = (bf16[160,256]{1,0:T(8,128)(2,1)S(1)}, bf16[160,256]{1,0:T(8,128)(2,1)S(1)}, u32[]{:S(2)}, u32[]{:S(2)}) collective-permute-start(bf16[160,256]{1,0:T(8,128)(2,1)S(1)} %copy-done.30), channel_id=1, source_target_pairs={{0,2},{1,3},{2,0},{3,1},{4,6},{5,7},{6,4},{7,5},{8,10},{9,11},{10,... | collective-permute-start | bytes 245768 | tf_op jit(solution)/shard_map/ppermute | solution.py:539
  86.1 5.7 %collective-permute-start.25 = (bf16[160,256]{1,0:T(8,128)(2,1)S(1)}, bf16[160,256]{1,0:T(8,128)(2,1)S(1)}, u32[]{:S(2)}, u32[]{:S(2)}) collective-permute-start(bf16[160,256]{1,0:T(8,128)(2,1)S(1)} %copy-done.29), channel_id=1, source_target_pairs={{0,3},{1,2},{2,1},{3,0},{4,7},{5,6},{6,5},{7,4},{8,11},{9,10},{10,... | collective-permute-start | bytes 245768 | tf_op jit(solution)/shard_map/ppermute | solution.py:539
  87.4 5.7 %collective-permute-start.21 = (bf16[400,128]{1,0:T(8,128)(2,1)S(1)}, bf16[400,128]{1,0:T(8,128)(2,1)S(1)}, u32[]{:S(2)}, u32[]{:S(2)}) collective-permute-start(bf16[400,128]{1,0:T(8,128)(2,1)S(1)} %fusion.4), channel_id=1, source_target_pairs={{0,8},{1,5},{2,10},{3,7},{4,12},{5,1},{6,14},{7,3},{8,0},{9,13},{1... | collective-permute-start | bytes 307208 | tf_op jit(solution)/shard_map/ppermute | solution.py:571
  92.0 22.7 %collective-permute-start.26 = (bf16[2,1800,128]{2,1,0:T(8,128)(2,1)S(1)}, bf16[2,1800,128]{2,1,0:T(8,128)(2,1)S(1)}, u32[]{:S(2)}, u32[]{:S(2)}) collective-permute-start(bf16[2,1800,128]{2,1,0:T(8,128)(2,1)S(1)} %pad_maximum_fusion.p_ref), channel_id=1, source_target_pairs={{0,4},{1,9},{2,6},{3,11},{4,0},{5,13},{6,2},{7,15},{8,12},{9,1},{1... | collective-permute-start | bytes 2764808 | tf_op jit(solution)/shard_map/ppermute | solution.py:571
  93.2 13.6 %collective-permute-start.27 = (bf16[400,128]{1,0:T(8,128)(2,1)S(1)}, bf16[400,128]{1,0:T(8,128)(2,1)S(1)}, u32[]{:S(2)}, u32[]{:S(2)}) collective-permute-start(bf16[400,128]{1,0:T(8,128)(2,1)S(1)} %fusion.6), channel_id=1, source_target_pairs={{0,16},{4,20},{8,24},{12,28},{16,0},{20,4},{24,8},{28,12},{1,17},{... | collective-permute-start | bytes 307208 | tf_op jit(solution)/shard_map/ppermute | solution.py:539
  106.8 4.7 %collective-permute-start.28 = (bf16[400,128]{1,0:T(8,128)(2,1)S(1)}, bf16[400,128]{1,0:T(8,128)(2,1)S(1)}, u32[]{:S(2)}, u32[]{:S(2)}) collective-permute-start(bf16[400,128]{1,0:T(8,128)(2,1)S(1)} %add_convert_fusion.1), channel_id=1, source_target_pairs={{0,8},{1,5},{2,10},{3,7},{4,12},{5,1},{6,14},{7,3},{8,0},{9,13},{1... | collective-permute-start | bytes 307208 | tf_op jit(solution)/shard_map/ppermute | solution.py:571
  111.5 7.2 %collective-permute-start.29 = (bf16[2,400,128]{2,1,0:T(8,128)(2,1)S(1)}, bf16[2,400,128]{2,1,0:T(8,128)(2,1)S(1)}, u32[]{:S(2)}, u32[]{:S(2)}) collective-permute-start(bf16[2,400,128]{2,1,0:T(8,128)(2,1)S(1)} %pad_maximum_fusion.1.refs_0_), channel_id=1, source_target_pairs={{0,4},{1,9},{2,6},{3,11},{4,0},{5,13},{6,2},{7,15},{8,12},{9,1},{1... | collective-permute-start | bytes 614408 | tf_op jit(solution)/shard_map/ppermute | solution.py:571
  (33 other events, 212.5 us)

commit v6 on v5

--- a/solution.py
+++ b/solution.py
@@ -615,13 +615,14 @@
     hidden_cots = hidden_cot.reshape(pixels, chans)
     hidden_cots = gather(after(hidden_cots, *own_images[2:], w_tap), "shard", patch, *backs)
 
+    skips = gather(after(skip_weight, patch), "shard")
+
     hidden_grad, keep_0, keep_2, send_g = filter_grad(
         after(ids, patch), patch, hidden_cots, backs, width, few
     )
     got_g = hop(send_g, 1)
-    *keep, send = forward(after(ids, send_g), patch, w_turned, pixels, width, few)
-    skips = gather(after(skip_weight, send_g), "shard")
-    got_g = after(got_g, send, skips[2])
+    *keep, send = forward(after(ids, send_g, skips[2]), patch, w_turned, pixels, width, few)
+    got_g = after(got_g, send)
     mid_g = (keep_2 + got_g[1].astype(F32)).astype(BF)
     last_g = hop(mid_g, 2)
     keep, last, got = sum_scatter(keep, send)

time: 122 us -> 121 us (level)
  waiting for transfers between devices: 30.5 us -> 27.5 us
  starting transfers between devices: 31.1 us -> 33 us
    ppermute x22, waiting for transfers between devices: 27.3 us -> 24.4 us  [flip(): lax.ppermute(value, axis, [(i, i ^ bit) for i in range(lax.axis_size(axis...]
    ppermute x8, starting transfers between devices: 8.9 us -> 10.2 us  [hop(): return lax.ppermute(value, ('rep', 'shard'), pairs)]
  transfers between devices with their start and end apart: 30 -> 30, of which waited for: 11 -> 12; matrix products, arithmetic and copies ran while one was open for 2% -> 2% of each run, Pallas kernels for 36% -> 42%
where the time goes in v6:
time: 121 us; the launch traced here: 120 us
  Pallas kernels  52.8 us (44%)
  starting transfers between devices  33 us (27%)
  waiting for transfers between devices  27.5 us (23%)
  local copies, waits for them, and re-layouts  3.87 us (3%)
  other arithmetic  2.28 us (2%)
    pallas_call x12, Pallas kernels, call(): pl.pallas_call(body, out_shape=outs, in_specs=specs, out_specs=jax.tree.m...  46.1 us
    ppermute x22, waiting for transfers between devices, flip(): lax.ppermute(value, axis, [(i, i ^ bit) for i in range(lax.axis_size(axis...  24.4 us
    ppermute x22, starting transfers between devices, flip(): lax.ppermute(value, axis, [(i, i ^ bit) for i in range(lax.axis_size(axis...  22.8 us
    ppermute x8, starting transfers between devices, hop(): return lax.ppermute(value, ('rep', 'shard'), pairs)  10.2 us
    pallas_call x2, Pallas kernels, place_grad(): pl.pallas_call(body, out_shape=shape((rows, chans), F32) if final else [s...  6.76 us
    unnamed x70, local copies, waits for them, and re-layouts  3.87 us
    ppermute x8, waiting for transfers between devices, hop(): return lax.ppermute(value, ('rep', 'shard'), pairs)  3.12 us
  transfers between devices with their start and end apart: 30, of which 12 were waited for; matrix products, arithmetic and copies ran while one was open for 2% of the time, Pallas kernels for 42%

profile of v6, /device:TPU:1, one launch (start us, length us, event | category | flops | bytes accessed | tf_op | source)
XLA Modules:
  0.0 120.4 jit_solution(3596421551352186932)
XLA Ops:
  0.7 2.1 %collective-permute-start.4 = (bf16[64,1280]{1,0:T(8,128)(2,1)}, bf16[64,1280]{1,0:T(8,128)(2,1)S(1)}, u32[]{:S(2)}, u32[]{:S(2)}) collective-permute-start(bf16[64,1280]{1,0:T(8,128)(2,1)} %bitcast.40), channel_id=1, source_target_pairs={{0,2},{1,3},{2,0},{3,1},{4,6},{5,7},{6,4},{7,5},{8,10},{9,11},{10,... | collective-permute-start | bytes 491528 | tf_op jit(solution)/shard_map/ppermute | solution.py:539
  3.4 1.9 %turn_images.1 = (bf16[160,256]{1,0:T(8,128)(2,1)}, bf16[160,256]{1,0:T(8,128)(2,1)}, bf16[160,256]{1,0:T(8,128)(2,1)}, bf16[160,256]{1,0:T(8,128)(2,1)}) custom-call(s32[2]{0:T(128)} %pad_add_fusion.id_ref, bf16[256,640]{1,0:T(8,128)(2,1)} %bitcast.35), custom_call_target="tpu_custom_call" | custom-call | bytes 655360 | tf_op jit(solution)/shard_map/turn_images/pallas_call | solution.py:30
  5.3 2.5 %collective-permute-start.2 = (bf16[160,256]{1,0:T(8,128)(2,1)}, bf16[160,256]{1,0:T(8,128)(2,1)S(1)}, u32[]{:S(2)}, u32[]{:S(2)}) collective-permute-start(bf16[160,256]{1,0:T(8,128)(2,1)} %get-tuple-element.65), channel_id=1, source_target_pairs={{0,3},{1,2},{2,1},{3,0},{4,7},{5,6},{6,5},{7,4},{8,11},{9,10},{10,... | collective-permute-start | bytes 245768 | tf_op jit(solution)/shard_map/ppermute | solution.py:539
  7.8 4.1 %turn_filters.1 = (bf16[1440,640]{1,0:T(8,128)(2,1)}, bf16[640,1440]{1,0:T(8,128)(2,1)}) custom-call(bf16[1440,640]{1,0:T(8,128)(2,1)} %w_ref), custom_call_target="tpu_custom_call" | custom-call | bytes 5529600 | tf_op jit(solution)/shard_map/turn_filters/pallas_call | solution.py:30
  13.8 1.2 %collective-permute-done.refs_1_ = bf16[160,256]{1,0:T(8,128)(2,1)S(1)} collective-permute-done((bf16[160,256]{1,0:T(8,128)(2,1)}, bf16[160,256]{1,0:T(8,128)(2,1)S(1)}, u32[]{:S(2)}, u32[]{:S(2)}) %collective-permute-start) | collective-permute-done | bytes 81952 | tf_op jit(solution)/shard_map/ppermute | solution.py:539
  16.3 2.3 %back_product.1 = (bf16[160,256]{1,0:T(8,128)(2,1)}, bf16[256,1280]{1,0:T(8,128)(2,1)}) custom-call(s32[2]{0:T(128)} %pad_add_fusion.id_ref, bf16[160,1280]{1,0:T(8,128)(2,1)} %refs_0_, bf16[64,1280]{1,0:T(8,128)(2,1)} %bitcast.41, bf16[64,1280]{1,0:T(8,128)(2,1)} %copy-done.20, bf16[64,1280]{1,0:T(8,128)(2,1)} %copy-done.19, bf16[64,1280]{1,0:T(8,128)(2,1)} %copy-done.21), custom_call_target="tpu_custom_call" | custom-call | flops 104857600 | bytes 655360 | tf_op jit(solution)/shard_map/back_product/pallas_call | solution.py:30
  21.1 3.6 %make_patches.1.p_ref = bf16[1440,1024]{1,0:T(8,128)(2,1)} custom-call(bf16[160,256]{1,0:T(8,128)(2,1)} %get-tuple-element.69.refs_0_, bf16[160,256]{1,0:T(8,128)(2,1)} %copy-done.14, bf16[160,256]{1,0:T(8,128)(2,1)} %copy-done.12, bf16[160,256]{1,0:T(8,128)(2,1)} %copy-done.13), custom_call_target="tpu_custom_call" | custom-call | bytes 3276800 | tf_op jit(solution)/shard_map/make_patches/pallas_call | solution.py:30
  27.7 7.4 %filter_grad.1 = (bf16[1024,640]{1,0:T(8,128)(2,1)}, f32[1800,128]{1,0:T(8,128)}, f32[1800,128]{1,0:T(8,128)}, bf16[2,1800,128]{2,1,0:T(8,128)(2,1)}) custom-call(s32[2]{0:T(128)} %pad_add_fusion.id_ref, bf16[1440,1024]{1,0:T(8,128)(2,1)} %make_patches.1.p_ref, bf16[256,640]{1,0:T(8,128)(2,1)} %bitcast.45, bf16[256,640]{1,0:T(8,128)(2,1)} %copy-done.27, ...), custom_call_target="tpu_custom_call" | custom-call | flops 1887436800 | bytes 5386240 | tf_op jit(solution)/shard_map/filter_grad/pallas_call | solution.py:30
  35.1 1.3 %collective-permute-start.12 = (bf16[2,1800,128]{2,1,0:T(8,128)(2,1)}, bf16[2,1800,128]{2,1,0:T(8,128)(2,1)S(1)}, u32[]{:S(2)}, u32[]{:S(2)}) collective-permute-start(bf16[2,1800,128]{2,1,0:T(8,128)(2,1)} %get-tuple-element.79), channel_id=1, source_target_pairs={{0,4},{1,9},{2,6},{3,11},{4,0},{5,13},{6,2},{7,15},{8,12},{9,1},{1... | collective-permute-start | bytes 2764808 | tf_op jit(solution)/shard_map/ppermute | solution.py:571
  36.7 8.4 %forward.1 = (f32[800,256]{1,0:T(8,128)}, f32[800,256]{1,0:T(8,128)}, bf16[2,800,256]{2,1,0:T(8,128)(2,1)}) custom-call(s32[2]{0:T(128)} %pad_add_fusion.id_ref, bf16[640,1440]{1,0:T(8,128)(2,1)} %get-tuple-element.82.w_ref, bf16[1440,1024]{1,0:T(8,128)(2,1)} %make_patches.1.p_ref), custom_call_target="tpu_custom_call" | custom-call | flops 2642411520 | bytes 1966080 | tf_op jit(solution)/shard_map/forward/pallas_call | solution.py:30
  46.4 1.5 %collective-permute-done.12 = bf16[2,1800,128]{2,1,0:T(8,128)(2,1)S(1)} collective-permute-done((bf16[2,1800,128]{2,1,0:T(8,128)(2,1)}, bf16[2,1800,128]{2,1,0:T(8,128)(2,1)S(1)}, u32[]{:S(2)}, u32[]{:S(2)}) %collective-permute-start.12) | collective-permute-done | bytes 921632 | tf_op jit(solution)/shard_map/ppermute | solution.py:571
  48.0 1.4 %collective-permute-start.14 = (bf16[1800,128]{1,0:T(8,128)(2,1)S(1)}, bf16[1800,128]{1,0:T(8,128)(2,1)S(1)}, u32[]{:S(2)}, u32[]{:S(2)}) collective-permute-start(bf16[1800,128]{1,0:T(8,128)(2,1)S(1)} %fusion), channel_id=1, source_target_pairs={{0,8},{1,5},{2,10},{3,7},{4,12},{5,1},{6,14},{7,3},{8,0},{9,13},{1... | collective-permute-start | bytes 1382408 | tf_op jit(solution)/shard_map/ppermute | solution.py:571
  49.4 1.1 convert_add_fusion.2
  51.3 6.0 %image_grad.1 = (bf16[160,256]{1,0:T(8,128)(2,1)}, bf16[160,256]{1,0:T(8,128)(2,1)}, bf16[160,256]{1,0:T(8,128)(2,1)}, bf16[160,256]{1,0:T(8,128)(2,1)}) custom-call(s32[2]{0:T(128)} %pad_add_fusion.id_ref, bf16[1024,640]{1,0:T(8,128)(2,1)} %get-tuple-element.88.h_ref, bf16[1440,640]{1,0:T(8,128)(2,1)} %get-tuple-element.75.w_ref, ...), custom_call_target="tpu_custom_call" | custom-call | flops 1887436800 | bytes 1310720 | tf_op jit(solution)/shard_map/image_grad/pallas_call | solution.py:30
  57.4 2.4 %collective-permute-done.16.g_ref = bf16[800,256]{1,0:T(8,128)(2,1)S(1)} collective-permute-done((bf16[800,256]{1,0:T(8,128)(2,1)S(1)}, bf16[800,256]{1,0:T(8,128)(2,1)S(1)}, u32[]{:S(2)}, u32[]{:S(2)}) %collective-permute-start.16) | collective-permute-done | bytes 409632 | tf_op jit(solution)/shard_map/ppermute | solution.py:539
  60.0 2.4 %collective-permute-start.20 = (bf16[1800,128]{1,0:T(8,128)(2,1)S(1)}, bf16[1800,128]{1,0:T(8,128)(2,1)S(1)}, u32[]{:S(2)}, u32[]{:S(2)}) collective-permute-start(bf16[1800,128]{1,0:T(8,128)(2,1)S(1)} %fusion.2), channel_id=1, source_target_pairs={{0,16},{4,20},{8,24},{12,28},{16,0},{20,4},{24,8},{28,12},{1,17},{... | collective-permute-start | bytes 1382408 | tf_op jit(solution)/shard_map/ppermute | solution.py:539
  62.4 3.3 %skip_grad_term.1 = (f32[400,128]{1,0:T(8,128)}, f32[400,128]{1,0:T(8,128)}, bf16[2,400,128]{2,1,0:T(8,128)(2,1)}) custom-call(s32[2]{0:T(128)} %pad_add_fusion.id_ref, f32[800,256]{1,0:T(8,128)} %get-tuple-element.119.k_ref, bf16[800,256]{1,0:T(8,128)(2,1)} %copy-done.1, bf16[256,1280]{1,0:T(8,128)(2,1)} %get-tuple-element.95.c_ref, ...), custom_call_target="tpu_custom_call" | custom-call | flops 104857600 | bytes 819200 | tf_op jit(solution)/shard_map/skip_grad_term/pallas_call | solution.py:30
  65.6 2.6 %collective-permute-start.19 = (bf16[2,400,128]{2,1,0:T(8,128)(2,1)}, bf16[2,400,128]{2,1,0:T(8,128)(2,1)S(1)}, u32[]{:S(2)}, u32[]{:S(2)}) collective-permute-start(bf16[2,400,128]{2,1,0:T(8,128)(2,1)} %get-tuple-element.96), channel_id=1, source_target_pairs={{0,4},{1,9},{2,6},{3,11},{4,0},{5,13},{6,2},{7,15},{8,12},{9,1},{1... | collective-permute-start | bytes 614408 | tf_op jit(solution)/shard_map/ppermute | solution.py:571
  68.2 2.4 %finish_hidden.1 = (bf16[256,640]{1,0:T(8,128)(2,1)}, bf16[64,640]{1,0:T(8,128)(2,1)}) custom-call(bf16[256,640]{1,0:T(8,128)(2,1)} %bitcast.36, f32[800,256]{1,0:T(8,128)} %get-tuple-element.119.k_ref, bf16[800,256]{1,0:T(8,128)(2,1)} %copy-done.1), custom_call_target="tpu_custom_call" | custom-call | flops 20971520 | bytes 1638400 | tf_op jit(solution)/shard_map/finish_hidden/pallas_call | solution.py:30
  70.6 2.7 %project.1 = bf16[64,1280]{1,0:T(8,128)(2,1)} custom-call(s32[2]{0:T(128)} %pad_add_fusion.id_ref, bf16[64,640]{1,0:T(8,128)(2,1)} %get-tuple-element.97.s_ref, bf16[160,1280]{1,0:T(8,128)(2,1)} %refs_0_, bf16[160,1280]{1,0:T(8,128)(2,1)} %copy-done.10, bf16[160,1280]{1,0:T(8,128)(2,1)} %copy-done.9, bf16[160,1280]{1,0:T(8,128)(2,1)} %copy-done.11), custom_call_target="tpu_custom_call" | custom-call | flops 104857600 | bytes 1638400 | tf_op jit(solution)/shard_map/project/pallas_call | solution.py:30
  74.3 6.6 %collective-permute-done.20 = bf16[1800,128]{1,0:T(8,128)(2,1)S(1)} collective-permute-done((bf16[1800,128]{1,0:T(8,128)(2,1)S(1)}, bf16[1800,128]{1,0:T(8,128)(2,1)S(1)}, u32[]{:S(2)}, u32[]{:S(2)}) %collective-permute-start.20) | collective-permute-done | bytes 460832 | tf_op jit(solution)/shard_map/ppermute | solution.py:539
  81.1 4.4 %collective-permute-start.25 = (bf16[160,256]{1,0:T(8,128)(2,1)S(1)}, bf16[160,256]{1,0:T(8,128)(2,1)S(1)}, u32[]{:S(2)}, u32[]{:S(2)}) collective-permute-start(bf16[160,256]{1,0:T(8,128)(2,1)S(1)} %copy-done.31), channel_id=1, source_target_pairs={{0,3},{1,2},{2,1},{3,0},{4,7},{5,6},{6,5},{7,4},{8,11},{9,10},{10,... | collective-permute-start | bytes 245768 | tf_op jit(solution)/shard_map/ppermute | solution.py:539
  86.2 2.5 %collective-permute-done.25.refs_3_ = bf16[160,256]{1,0:T(8,128)(2,1)S(1)} collective-permute-done((bf16[160,256]{1,0:T(8,128)(2,1)S(1)}, bf16[160,256]{1,0:T(8,128)(2,1)S(1)}, u32[]{:S(2)}, u32[]{:S(2)}) %collective-permute-start.25) | collective-permute-done | bytes 81952 | tf_op jit(solution)/shard_map/ppermute | solution.py:539
  88.6 2.0 %collective-permute-done.24.refs_2_ = bf16[160,256]{1,0:T(8,128)(2,1)S(1)} collective-permute-done((bf16[160,256]{1,0:T(8,128)(2,1)S(1)}, bf16[160,256]{1,0:T(8,128)(2,1)S(1)}, u32[]{:S(2)}, u32[]{:S(2)}) %collective-permute-start.24) | collective-permute-done | bytes 81952 | tf_op jit(solution)/shard_map/ppermute | solution.py:539
  90.7 1.1 collective-permute-start.26
  91.9 3.1 %collective-permute-start.27 = (bf16[400,128]{1,0:T(8,128)(2,1)S(1)}, bf16[400,128]{1,0:T(8,128)(2,1)S(1)}, u32[]{:S(2)}, u32[]{:S(2)}) collective-permute-start(bf16[400,128]{1,0:T(8,128)(2,1)S(1)} %fusion.6), channel_id=1, source_target_pairs={{0,16},{4,20},{8,24},{12,28},{16,0},{20,4},{24,8},{28,12},{1,17},{... | collective-permute-start | bytes 307208 | tf_op jit(solution)/shard_map/ppermute | solution.py:539
  94.9 2.0 %finish_images.1 = bf16[256,640]{1,0:T(8,128)(2,1)} custom-call(s32[2]{0:T(128)} %pad_add_fusion.id_ref, bf16[160,256]{1,0:T(8,128)(2,1)} %get-tuple-element.103.refs_0_, bf16[160,256]{1,0:T(8,128)(2,1)} %copy-done.24, bf16[160,256]{1,0:T(8,128)(2,1)} %copy-done.23, bf16[160,256]{1,0:T(8,128)(2,1)} %copy-done.22), custom_call_target="tpu_custom_call" | custom-call | bytes 655360 | tf_op jit(solution)/shard_map/finish_images/pallas_call | solution.py:30
  96.9 8.6 %collective-permute-done.27 = bf16[400,128]{1,0:T(8,128)(2,1)S(1)} collective-permute-done((bf16[400,128]{1,0:T(8,128)(2,1)S(1)}, bf16[400,128]{1,0:T(8,128)(2,1)S(1)}, u32[]{:S(2)}, u32[]{:S(2)}) %collective-permute-start.27) | collective-permute-done | bytes 102432 | tf_op jit(solution)/shard_map/ppermute | solution.py:539
  105.6 3.7 %place_grad.2 = (f32[1440,640]{1,0:T(8,128)}, f32[4,360,128]{2,1,0:T(8,128)}) custom-call(s32[2]{0:T(128)} %pad_add_fusion.id_ref, bf16[2,1800,128]{2,1,0:T(8,128)(2,1)} %copy-done), custom_call_target="tpu_custom_call" | custom-call | bytes 2764800 | tf_op jit(solution)/shard_map/place_grad/pallas_call | solution.py:342
  110.0 3.6 %collective-permute-start.29 = (bf16[2,400,128]{2,1,0:T(8,128)(2,1)S(1)}, bf16[2,400,128]{2,1,0:T(8,128)(2,1)S(1)}, u32[]{:S(2)}, u32[]{:S(2)}) collective-permute-start(bf16[2,400,128]{2,1,0:T(8,128)(2,1)S(1)} %pad_maximum_fusion.1.refs_0_), channel_id=1, source_target_pairs={{0,4},{1,9},{2,6},{3,11},{4,0},{5,13},{6,2},{7,15},{8,12},{9,1},{1... | collective-permute-start | bytes 614408 | tf_op jit(solution)/shard_map/ppermute | solution.py:571
  114.6 3.1 %place_grad.3 = f32[1440,640]{1,0:T(8,128)} custom-call(s32[2]{0:T(128)} %pad_add_fusion.id_ref, bf16[2,1800,128]{2,1,0:T(8,128)(2,1)} %copy-done.5, f32[1440,640]{1,0:T(8,128)} %get-tuple-element.115.refs_0_, f32[4,360,128]{2,1,0:T(8,128)} %get-tuple-element.116.refs_1_), custom_call_target="tpu_custom_call", output_to_operand_aliasing={{}: (2, {})} | custom-call | bytes 2764800 | tf_op jit(solution)/shard_map/place_grad/pallas_call | solution.py:342
  118.4 2.0 %place_skip.1 = f32[160,1280]{1,0:T(8,128)} custom-call(s32[2]{0:T(128)} %pad_add_fusion.id_ref, bf16[2,400,128]{2,1,0:T(8,128)(2,1)} %copy-done.8, bf16[2,400,128]{2,1,0:T(8,128)(2,1)} %copy-done.17), custom_call_target="tpu_custom_call" | custom-call | bytes 1228800 | tf_op jit(solution)/shard_map/place_skip/pallas_call | solution.py:30
  (122 shorter events, 16.4 us)
Async XLA Ops:
  0.7 12.6 %collective-permute-start.4 = (bf16[64,1280]{1,0:T(8,128)(2,1)}, bf16[64,1280]{1,0:T(8,128)(2,1)S(1)}, u32[]{:S(2)}, u32[]{:S(2)}) collective-permute-start(bf16[64,1280]{1,0:T(8,128)(2,1)} %bitcast.40), channel_id=1, source_target_pairs={{0,2},{1,3},{2,0},{3,1},{4,6},{5,7},{6,4},{7,5},{8,10},{9,11},{10,... | collective-permute-start | bytes 491528 | tf_op jit(solution)/shard_map/ppermute | solution.py:539
  5.2 6.7 %collective-permute-start.1 = (bf16[160,256]{1,0:T(8,128)(2,1)}, bf16[160,256]{1,0:T(8,128)(2,1)S(1)}, u32[]{:S(2)}, u32[]{:S(2)}) collective-permute-start(bf16[160,256]{1,0:T(8,128)(2,1)} %get-tuple-element.64), channel_id=1, source_target_pairs={{0,2},{1,3},{2,0},{3,1},{4,6},{5,7},{6,4},{7,5},{8,10},{9,11},{10,... | collective-permute-start | bytes 245768 | tf_op jit(solution)/shard_map/ppermute | solution.py:539
  5.3 6.7 %collective-permute-start.2 = (bf16[160,256]{1,0:T(8,128)(2,1)}, bf16[160,256]{1,0:T(8,128)(2,1)S(1)}, u32[]{:S(2)}, u32[]{:S(2)}) collective-permute-start(bf16[160,256]{1,0:T(8,128)(2,1)} %get-tuple-element.65), channel_id=1, source_target_pairs={{0,3},{1,2},{2,1},{3,0},{4,7},{5,6},{6,5},{7,4},{8,11},{9,10},{10,... | collective-permute-start | bytes 245768 | tf_op jit(solution)/shard_map/ppermute | solution.py:539
  12.0 12.7 %collective-permute-start.7 = (bf16[256,640]{1,0:T(8,128)(2,1)S(1)}, bf16[256,640]{1,0:T(8,128)(2,1)S(1)}, u32[]{:S(2)}, u32[]{:S(2)}) collective-permute-start(bf16[256,640]{1,0:T(8,128)(2,1)S(1)} %bitcast.46), channel_id=1, source_target_pairs={{0,2},{1,3},{2,0},{3,1},{4,6},{5,7},{6,4},{7,5},{8,10},{9,11},{10,... | collective-permute-start | bytes 983048 | tf_op jit(solution)/shard_map/ppermute | solution.py:539
  12.6 2.4 %collective-permute-start.3 = (bf16[64,1280]{1,0:T(8,128)(2,1)S(1)}, bf16[64,1280]{1,0:T(8,128)(2,1)S(1)}, u32[]{:S(2)}, u32[]{:S(2)}) collective-permute-start(bf16[64,1280]{1,0:T(8,128)(2,1)S(1)} %bitcast.42), channel_id=1, source_target_pairs={{0,1},{1,0},{2,3},{3,2},{4,5},{5,4},{6,7},{7,6},{8,9},{9,8},{10,11... | collective-permute-start | bytes 491528 | tf_op jit(solution)/shard_map/ppermute | solution.py:539
  13.2 1.7 %collective-permute-start.5 = (bf16[64,1280]{1,0:T(8,128)(2,1)S(1)}, bf16[64,1280]{1,0:T(8,128)(2,1)S(1)}, u32[]{:S(2)}, u32[]{:S(2)}) collective-permute-start(bf16[64,1280]{1,0:T(8,128)(2,1)S(1)} %collective-permute-done.4.refs_2_), channel_id=1, source_target_pairs={{0,1},{1,0},{2,3},{3,2},{4,5},{5,4},{6,7},{7,6},{8,9},{9,8},{10,11... | collective-permute-start | bytes 491528 | tf_op jit(solution)/shard_map/ppermute | solution.py:539
  13.3 1.6 %collective-permute-start = (bf16[160,256]{1,0:T(8,128)(2,1)}, bf16[160,256]{1,0:T(8,128)(2,1)S(1)}, u32[]{:S(2)}, u32[]{:S(2)}) collective-permute-start(bf16[160,256]{1,0:T(8,128)(2,1)} %get-tuple-element.63), channel_id=1, source_target_pairs={{0,1},{1,0},{2,3},{3,2},{4,5},{5,4},{6,7},{7,6},{8,9},{9,8},{10,11... | collective-permute-start | bytes 245768 | tf_op jit(solution)/shard_map/ppermute | solution.py:539
  18.6 6.1 %collective-permute-start.10 = (bf16[160,256]{1,0:T(8,128)(2,1)}, bf16[160,256]{1,0:T(8,128)(2,1)S(1)}, u32[]{:S(2)}, u32[]{:S(2)}) collective-permute-start(bf16[160,256]{1,0:T(8,128)(2,1)} %get-tuple-element.68.refs_4_), channel_id=1, source_target_pairs={{0,3},{1,2},{2,1},{3,0},{4,7},{5,6},{6,5},{7,4},{8,11},{9,10},{10,... | collective-permute-start | bytes 245768 | tf_op jit(solution)/shard_map/ppermute | solution.py:539
  19.3 5.4 %collective-permute-start.8 = (bf16[160,256]{1,0:T(8,128)(2,1)}, bf16[160,256]{1,0:T(8,128)(2,1)S(1)}, u32[]{:S(2)}, u32[]{:S(2)}) collective-permute-start(bf16[160,256]{1,0:T(8,128)(2,1)} %get-tuple-element.68.refs_4_), channel_id=1, source_target_pairs={{0,1},{1,0},{2,3},{3,2},{4,5},{5,4},{6,7},{7,6},{8,9},{9,8},{10,11... | collective-permute-start | bytes 245768 | tf_op jit(solution)/shard_map/ppermute | solution.py:539
  19.6 5.3 %collective-permute-start.9 = (bf16[160,256]{1,0:T(8,128)(2,1)}, bf16[160,256]{1,0:T(8,128)(2,1)S(1)}, u32[]{:S(2)}, u32[]{:S(2)}) collective-permute-start(bf16[160,256]{1,0:T(8,128)(2,1)} %get-tuple-element.68.refs_4_), channel_id=1, source_target_pairs={{0,2},{1,3},{2,0},{3,1},{4,6},{5,7},{6,4},{7,5},{8,10},{9,11},{10,... | collective-permute-start | bytes 245768 | tf_op jit(solution)/shard_map/ppermute | solution.py:539
  20.5 5.7 %collective-permute-start.6 = (bf16[256,640]{1,0:T(8,128)(2,1)S(1)}, bf16[256,640]{1,0:T(8,128)(2,1)S(1)}, u32[]{:S(2)}, u32[]{:S(2)}) collective-permute-start(bf16[256,640]{1,0:T(8,128)(2,1)S(1)} %bitcast.47), channel_id=1, source_target_pairs={{0,1},{1,0},{2,3},{3,2},{4,5},{5,4},{6,7},{7,6},{8,9},{9,8},{10,11... | collective-permute-start | bytes 983048 | tf_op jit(solution)/shard_map/ppermute | solution.py:539
  24.9 2.0 %collective-permute-start.11 = (bf16[256,640]{1,0:T(8,128)(2,1)S(1)}, bf16[256,640]{1,0:T(8,128)(2,1)S(1)}, u32[]{:S(2)}, u32[]{:S(2)}) collective-permute-start(bf16[256,640]{1,0:T(8,128)(2,1)S(1)} %collective-permute-done.7.refs_2_), channel_id=1, source_target_pairs={{0,1},{1,0},{2,3},{3,2},{4,5},{5,4},{6,7},{7,6},{8,9},{9,8},{10,11... | collective-permute-start | bytes 983048 | tf_op jit(solution)/shard_map/ppermute | solution.py:539
  25.6 11.0 %collective-permute-start.13 = (bf16[160,1280]{1,0:T(8,128)(2,1)S(1)}, bf16[160,1280]{1,0:T(8,128)(2,1)S(1)}, u32[]{:S(2)}, u32[]{:S(2)}) collective-permute-start(bf16[160,1280]{1,0:T(8,128)(2,1)S(1)} %copy-done.2), channel_id=1, source_target_pairs={{0,2},{1,3},{2,0},{3,1},{4,6},{5,7},{6,4},{7,5},{8,10},{9,11},{10,... | collective-permute-start | bytes 1228808 | tf_op jit(solution)/shard_map/ppermute | solution.py:539
  35.1 12.8 %collective-permute-start.12 = (bf16[2,1800,128]{2,1,0:T(8,128)(2,1)}, bf16[2,1800,128]{2,1,0:T(8,128)(2,1)S(1)}, u32[]{:S(2)}, u32[]{:S(2)}) collective-permute-start(bf16[2,1800,128]{2,1,0:T(8,128)(2,1)} %get-tuple-element.79), channel_id=1, source_target_pairs={{0,4},{1,9},{2,6},{3,11},{4,0},{5,13},{6,2},{7,15},{8,12},{9,1},{1... | collective-permute-start | bytes 2764808 | tf_op jit(solution)/shard_map/ppermute | solution.py:571
  45.0 4.3 %collective-permute-start.15 = (bf16[2,800,256]{2,1,0:T(8,128)(2,1)}, bf16[2,800,256]{2,1,0:T(8,128)(2,1)S(1)}, u32[]{:S(2)}, u32[]{:S(2)}) collective-permute-start(bf16[2,800,256]{2,1,0:T(8,128)(2,1)} %get-tuple-element.83), channel_id=1, source_target_pairs={{0,1},{1,0},{2,3},{3,2},{4,5},{5,4},{6,7},{7,6},{8,9},{9,8},{10,11... | collective-permute-start | bytes 2457608 | tf_op jit(solution)/shard_map/ppermute | solution.py:539
  45.9 11.4 %collective-permute-start.17 = (bf16[160,1280]{1,0:T(8,128)(2,1)S(1)}, bf16[160,1280]{1,0:T(8,128)(2,1)S(1)}, u32[]{:S(2)}, u32[]{:S(2)}) collective-permute-start(bf16[160,1280]{1,0:T(8,128)(2,1)S(1)} %copy-done.2), channel_id=1, source_target_pairs={{0,1},{1,0},{2,3},{3,2},{4,5},{5,4},{6,7},{7,6},{8,9},{9,8},{10,11... | collective-permute-start | bytes 1228808 | tf_op jit(solution)/shard_map/ppermute | solution.py:539
  46.0 11.4 %collective-permute-start.18 = (bf16[160,1280]{1,0:T(8,128)(2,1)S(1)}, bf16[160,1280]{1,0:T(8,128)(2,1)S(1)}, u32[]{:S(2)}, u32[]{:S(2)}) collective-permute-start(bf16[160,1280]{1,0:T(8,128)(2,1)S(1)} %collective-permute-done.13.refs_2_), channel_id=1, source_target_pairs={{0,1},{1,0},{2,3},{3,2},{4,5},{5,4},{6,7},{7,6},{8,9},{9,8},{10,11... | collective-permute-start | bytes 1228808 | tf_op jit(solution)/shard_map/ppermute | solution.py:539
  48.0 11.8 %collective-permute-start.14 = (bf16[1800,128]{1,0:T(8,128)(2,1)S(1)}, bf16[1800,128]{1,0:T(8,128)(2,1)S(1)}, u32[]{:S(2)}, u32[]{:S(2)}) collective-permute-start(bf16[1800,128]{1,0:T(8,128)(2,1)S(1)} %fusion), channel_id=1, source_target_pairs={{0,8},{1,5},{2,10},{3,7},{4,12},{5,1},{6,14},{7,3},{8,0},{9,13},{1... | collective-permute-start | bytes 1382408 | tf_op jit(solution)/shard_map/ppermute | solution.py:571
  50.4 9.4 %collective-permute-start.16 = (bf16[800,256]{1,0:T(8,128)(2,1)S(1)}, bf16[800,256]{1,0:T(8,128)(2,1)S(1)}, u32[]{:S(2)}, u32[]{:S(2)}) collective-permute-start(bf16[800,256]{1,0:T(8,128)(2,1)S(1)} %get-tuple-element.120), channel_id=1, source_target_pairs={{0,2},{1,3},{2,0},{3,1},{4,6},{5,7},{6,4},{7,5},{8,10},{9,11},{10,... | collective-permute-start | bytes 1228808 | tf_op jit(solution)/shard_map/ppermute | solution.py:539
  60.0 20.9 %collective-permute-start.20 = (bf16[1800,128]{1,0:T(8,128)(2,1)S(1)}, bf16[1800,128]{1,0:T(8,128)(2,1)S(1)}, u32[]{:S(2)}, u32[]{:S(2)}) collective-permute-start(bf16[1800,128]{1,0:T(8,128)(2,1)S(1)} %fusion.2), channel_id=1, source_target_pairs={{0,16},{4,20},{8,24},{12,28},{16,0},{20,4},{24,8},{28,12},{1,17},{... | collective-permute-start | bytes 1382408 | tf_op jit(solution)/shard_map/ppermute | solution.py:539
  65.6 8.6 %collective-permute-start.19 = (bf16[2,400,128]{2,1,0:T(8,128)(2,1)}, bf16[2,400,128]{2,1,0:T(8,128)(2,1)S(1)}, u32[]{:S(2)}, u32[]{:S(2)}) collective-permute-start(bf16[2,400,128]{2,1,0:T(8,128)(2,1)} %get-tuple-element.96), channel_id=1, source_target_pairs={{0,4},{1,9},{2,6},{3,11},{4,0},{5,13},{6,2},{7,15},{8,12},{9,1},{1... | collective-permute-start | bytes 614408 | tf_op jit(solution)/shard_map/ppermute | solution.py:571
  70.6 15.5 %copy-start.15 = (f32[400,128]{1,0:T(8,128)S(1)}, f32[400,128]{1,0:T(8,128)}, u32[]{:S(2)}) copy-start(f32[400,128]{1,0:T(8,128)} %get-tuple-element.101) | copy-start | bytes 614404
  73.3 18.6 %copy-start.16 = (f32[400,128]{1,0:T(8,128)S(1)}, f32[400,128]{1,0:T(8,128)}, u32[]{:S(2)}) copy-start(f32[400,128]{1,0:T(8,128)} %get-tuple-element.99) | copy-start | bytes 614404
  81.1 9.5 %collective-permute-start.22 = (bf16[1800,128]{1,0:T(8,128)(2,1)S(1)}, bf16[1800,128]{1,0:T(8,128)(2,1)S(1)}, u32[]{:S(2)}, u32[]{:S(2)}) collective-permute-start(bf16[1800,128]{1,0:T(8,128)(2,1)S(1)} %add_convert_fusion), channel_id=1, source_target_pairs={{0,8},{1,5},{2,10},{3,7},{4,12},{5,1},{6,14},{7,3},{8,0},{9,13},{1... | collective-permute-start | bytes 1382408 | tf_op jit(solution)/shard_map/ppermute | solution.py:571
  81.1 7.5 %collective-permute-start.25 = (bf16[160,256]{1,0:T(8,128)(2,1)S(1)}, bf16[160,256]{1,0:T(8,128)(2,1)S(1)}, u32[]{:S(2)}, u32[]{:S(2)}) collective-permute-start(bf16[160,256]{1,0:T(8,128)(2,1)S(1)} %copy-done.31), channel_id=1, source_target_pairs={{0,3},{1,2},{2,1},{3,0},{4,7},{5,6},{6,5},{7,4},{8,11},{9,10},{10,... | collective-permute-start | bytes 245768 | tf_op jit(solution)/shard_map/ppermute | solution.py:539
  85.5 5.0 %collective-permute-start.24 = (bf16[160,256]{1,0:T(8,128)(2,1)S(1)}, bf16[160,256]{1,0:T(8,128)(2,1)S(1)}, u32[]{:S(2)}, u32[]{:S(2)}) collective-permute-start(bf16[160,256]{1,0:T(8,128)(2,1)S(1)} %copy-done.30), channel_id=1, source_target_pairs={{0,2},{1,3},{2,0},{3,1},{4,6},{5,7},{6,4},{7,5},{8,10},{9,11},{10,... | collective-permute-start | bytes 245768 | tf_op jit(solution)/shard_map/ppermute | solution.py:539
  86.0 4.5 %collective-permute-start.23 = (bf16[160,256]{1,0:T(8,128)(2,1)S(1)}, bf16[160,256]{1,0:T(8,128)(2,1)S(1)}, u32[]{:S(2)}, u32[]{:S(2)}) collective-permute-start(bf16[160,256]{1,0:T(8,128)(2,1)S(1)} %copy-done.29), channel_id=1, source_target_pairs={{0,1},{1,0},{2,3},{3,2},{4,5},{5,4},{6,7},{7,6},{8,9},{9,8},{10,11... | collective-permute-start | bytes 245768 | tf_op jit(solution)/shard_map/ppermute | solution.py:539
  86.1 5.7 %collective-permute-start.21 = (bf16[400,128]{1,0:T(8,128)(2,1)S(1)}, bf16[400,128]{1,0:T(8,128)(2,1)S(1)}, u32[]{:S(2)}, u32[]{:S(2)}) collective-permute-start(bf16[400,128]{1,0:T(8,128)(2,1)S(1)} %fusion.4), channel_id=1, source_target_pairs={{0,8},{1,5},{2,10},{3,7},{4,12},{5,1},{6,14},{7,3},{8,0},{9,13},{1... | collective-permute-start | bytes 307208 | tf_op jit(solution)/shard_map/ppermute | solution.py:571
  90.7 22.9 %collective-permute-start.26 = (bf16[2,1800,128]{2,1,0:T(8,128)(2,1)S(1)}, bf16[2,1800,128]{2,1,0:T(8,128)(2,1)S(1)}, u32[]{:S(2)}, u32[]{:S(2)}) collective-permute-start(bf16[2,1800,128]{2,1,0:T(8,128)(2,1)S(1)} %pad_maximum_fusion.p_ref), channel_id=1, source_target_pairs={{0,4},{1,9},{2,6},{3,11},{4,0},{5,13},{6,2},{7,15},{8,12},{9,1},{1... | collective-permute-start | bytes 2764808 | tf_op jit(solution)/shard_map/ppermute | solution.py:571
  91.9 13.6 %collective-permute-start.27 = (bf16[400,128]{1,0:T(8,128)(2,1)S(1)}, bf16[400,128]{1,0:T(8,128)(2,1)S(1)}, u32[]{:S(2)}, u32[]{:S(2)}) collective-permute-start(bf16[400,128]{1,0:T(8,128)(2,1)S(1)} %fusion.6), channel_id=1, source_target_pairs={{0,16},{4,20},{8,24},{12,28},{16,0},{20,4},{24,8},{28,12},{1,17},{... | collective-permute-start | bytes 307208 | tf_op jit(solution)/shard_map/ppermute | solution.py:539
  105.5 4.4 %collective-permute-start.28 = (bf16[400,128]{1,0:T(8,128)(2,1)S(1)}, bf16[400,128]{1,0:T(8,128)(2,1)S(1)}, u32[]{:S(2)}, u32[]{:S(2)}) collective-permute-start(bf16[400,128]{1,0:T(8,128)(2,1)S(1)} %add_convert_fusion.1), channel_id=1, source_target_pairs={{0,8},{1,5},{2,10},{3,7},{4,12},{5,1},{6,14},{7,3},{8,0},{9,13},{1... | collective-permute-start | bytes 307208 | tf_op jit(solution)/shard_map/ppermute | solution.py:571
  110.0 7.7 %collective-permute-start.29 = (bf16[2,400,128]{2,1,0:T(8,128)(2,1)S(1)}, bf16[2,400,128]{2,1,0:T(8,128)(2,1)S(1)}, u32[]{:S(2)}, u32[]{:S(2)}) collective-permute-start(bf16[2,400,128]{2,1,0:T(8,128)(2,1)S(1)} %pad_maximum_fusion.1.refs_0_), channel_id=1, source_target_pairs={{0,4},{1,9},{2,6},{3,11},{4,0},{5,13},{6,2},{7,15},{8,12},{9,1},{1... | collective-permute-start | bytes 614408 | tf_op jit(solution)/shard_map/ppermute | solution.py:571
  (33 other events, 210.2 us)

commit v7 on v6

--- a/solution.py
+++ b/solution.py
@@ -627,7 +627,7 @@
     last_g = hop(mid_g, 2)
     keep, last, got = sum_scatter(keep, send)
     own_input = image_grad(after(ids, last), hidden_grad, own_images, w_tap, width)
-    last_g = after(last_g, own_input[0], got, *skips)
+    last_g = after(last_g, own_input[0], *skips)
     sum_g = (keep_0 + got_g[0].astype(F32) + last_g.astype(F32)).astype(BF)
 
     beyond = sum_beyond_block(sum_g)

time: 121 us -> 118 us (0.975)
  waiting for transfers between devices: 27.5 us -> 24.4 us
    ppermute x22, waiting for transfers between devices: 24.4 us -> 21.8 us  [flip(): lax.ppermute(value, axis, [(i, i ^ bit) for i in range(lax.axis_size(axis...]
    ppermute x8, starting transfers between devices: 10.2 us -> 11.5 us  [hop(): return lax.ppermute(value, ('rep', 'shard'), pairs)]
    ppermute x22, starting transfers between devices: 22.8 us -> 21.5 us  [flip(): lax.ppermute(value, axis, [(i, i ^ bit) for i in range(lax.axis_size(axis...]
  transfers between devices with their start and end apart: 30 -> 30, of which waited for: 12 -> 10; matrix products, arithmetic and copies ran while one was open for 2% -> 2% of each run, Pallas kernels for 42% -> 43%
where the time goes in v7:
time: 118 us
  Pallas kernels  52.8 us (45%)
  starting transfers between devices  33 us (28%)
  waiting for transfers between devices  24.4 us (21%)
  local copies, waits for them, and re-layouts  4.62 us (4%)
  other arithmetic  2.28 us (2%)
    pallas_call x12, Pallas kernels, call(): pl.pallas_call(body, out_shape=outs, in_specs=specs, out_specs=jax.tree.m...  46.1 us
    ppermute x22, waiting for transfers between devices, flip(): lax.ppermute(value, axis, [(i, i ^ bit) for i in range(lax.axis_size(axis...  21.8 us
    ppermute x22, starting transfers between devices, flip(): lax.ppermute(value, axis, [(i, i ^ bit) for i in range(lax.axis_size(axis...  21.5 us
    ppermute x8, starting transfers between devices, hop(): return lax.ppermute(value, ('rep', 'shard'), pairs)  11.5 us
    pallas_call x2, Pallas kernels, place_grad(): pl.pallas_call(body, out_shape=shape((rows, chans), F32) if final else [s...  6.76 us
    unnamed x70, local copies, waits for them, and re-layouts  4.62 us
    ppermute x8, waiting for transfers between devices, hop(): return lax.ppermute(value, ('rep', 'shard'), pairs)  2.51 us
  transfers between devices with their start and end apart: 30, of which 10 were waited for; matrix products, arithmetic and copies ran while one was open for 2% of the time, Pallas kernels for 43%

profile of v7, /device:TPU:1, one launch (start us, length us, event | category | flops | bytes accessed | tf_op | source)
XLA Modules:
  0.0 118.0 jit_solution(7531978725220851421)
XLA Ops:
  0.7 2.1 %collective-permute-start.4 = (bf16[64,1280]{1,0:T(8,128)(2,1)}, bf16[64,1280]{1,0:T(8,128)(2,1)S(1)}, u32[]{:S(2)}, u32[]{:S(2)}) collective-permute-start(bf16[64,1280]{1,0:T(8,128)(2,1)} %bitcast.40), channel_id=1, source_target_pairs={{0,2},{1,3},{2,0},{3,1},{4,6},{5,7},{6,4},{7,5},{8,10},{9,11},{10,... | collective-permute-start | bytes 491528 | tf_op jit(solution)/shard_map/ppermute | solution.py:539
  3.4 1.9 %turn_images.1 = (bf16[160,256]{1,0:T(8,128)(2,1)}, bf16[160,256]{1,0:T(8,128)(2,1)}, bf16[160,256]{1,0:T(8,128)(2,1)}, bf16[160,256]{1,0:T(8,128)(2,1)}) custom-call(s32[2]{0:T(128)} %pad_add_fusion.id_ref, bf16[256,640]{1,0:T(8,128)(2,1)} %bitcast.35), custom_call_target="tpu_custom_call" | custom-call | bytes 655360 | tf_op jit(solution)/shard_map/turn_images/pallas_call | solution.py:30
  5.3 2.5 %collective-permute-start.2 = (bf16[160,256]{1,0:T(8,128)(2,1)}, bf16[160,256]{1,0:T(8,128)(2,1)S(1)}, u32[]{:S(2)}, u32[]{:S(2)}) collective-permute-start(bf16[160,256]{1,0:T(8,128)(2,1)} %get-tuple-element.65), channel_id=1, source_target_pairs={{0,3},{1,2},{2,1},{3,0},{4,7},{5,6},{6,5},{7,4},{8,11},{9,10},{10,... | collective-permute-start | bytes 245768 | tf_op jit(solution)/shard_map/ppermute | solution.py:539
  7.8 4.1 %turn_filters.1 = (bf16[1440,640]{1,0:T(8,128)(2,1)}, bf16[640,1440]{1,0:T(8,128)(2,1)}) custom-call(bf16[1440,640]{1,0:T(8,128)(2,1)} %w_ref), custom_call_target="tpu_custom_call" | custom-call | bytes 5529600 | tf_op jit(solution)/shard_map/turn_filters/pallas_call | solution.py:30
  13.8 1.2 %collective-permute-done.refs_1_ = bf16[160,256]{1,0:T(8,128)(2,1)S(1)} collective-permute-done((bf16[160,256]{1,0:T(8,128)(2,1)}, bf16[160,256]{1,0:T(8,128)(2,1)S(1)}, u32[]{:S(2)}, u32[]{:S(2)}) %collective-permute-start) | collective-permute-done | bytes 81952 | tf_op jit(solution)/shard_map/ppermute | solution.py:539
  16.3 2.3 %back_product.1 = (bf16[160,256]{1,0:T(8,128)(2,1)}, bf16[256,1280]{1,0:T(8,128)(2,1)}) custom-call(s32[2]{0:T(128)} %pad_add_fusion.id_ref, bf16[160,1280]{1,0:T(8,128)(2,1)} %refs_0_, bf16[64,1280]{1,0:T(8,128)(2,1)} %bitcast.41, bf16[64,1280]{1,0:T(8,128)(2,1)} %copy-done.20, bf16[64,1280]{1,0:T(8,128)(2,1)} %copy-done.19, bf16[64,1280]{1,0:T(8,128)(2,1)} %copy-done.21), custom_call_target="tpu_custom_call" | custom-call | flops 104857600 | bytes 655360 | tf_op jit(solution)/shard_map/back_product/pallas_call | solution.py:30
  21.1 3.6 %make_patches.1.p_ref = bf16[1440,1024]{1,0:T(8,128)(2,1)} custom-call(bf16[160,256]{1,0:T(8,128)(2,1)} %get-tuple-element.69.refs_0_, bf16[160,256]{1,0:T(8,128)(2,1)} %copy-done.14, bf16[160,256]{1,0:T(8,128)(2,1)} %copy-done.12, bf16[160,256]{1,0:T(8,128)(2,1)} %copy-done.13), custom_call_target="tpu_custom_call" | custom-call | bytes 3276800 | tf_op jit(solution)/shard_map/make_patches/pallas_call | solution.py:30
  27.7 7.4 %filter_grad.1 = (bf16[1024,640]{1,0:T(8,128)(2,1)}, f32[1800,128]{1,0:T(8,128)}, f32[1800,128]{1,0:T(8,128)}, bf16[2,1800,128]{2,1,0:T(8,128)(2,1)}) custom-call(s32[2]{0:T(128)} %pad_add_fusion.id_ref, bf16[1440,1024]{1,0:T(8,128)(2,1)} %make_patches.1.p_ref, bf16[256,640]{1,0:T(8,128)(2,1)} %bitcast.45, bf16[256,640]{1,0:T(8,128)(2,1)} %copy-done.27, ...), custom_call_target="tpu_custom_call" | custom-call | flops 1887436800 | bytes 5386240 | tf_op jit(solution)/shard_map/filter_grad/pallas_call | solution.py:30
  35.1 1.3 %collective-permute-start.12 = (bf16[2,1800,128]{2,1,0:T(8,128)(2,1)}, bf16[2,1800,128]{2,1,0:T(8,128)(2,1)S(1)}, u32[]{:S(2)}, u32[]{:S(2)}) collective-permute-start(bf16[2,1800,128]{2,1,0:T(8,128)(2,1)} %get-tuple-element.79), channel_id=1, source_target_pairs={{0,4},{1,9},{2,6},{3,11},{4,0},{5,13},{6,2},{7,15},{8,12},{9,1},{1... | collective-permute-start | bytes 2764808 | tf_op jit(solution)/shard_map/ppermute | solution.py:571
  36.7 8.4 %forward.1 = (f32[800,256]{1,0:T(8,128)}, f32[800,256]{1,0:T(8,128)}, bf16[2,800,256]{2,1,0:T(8,128)(2,1)}) custom-call(s32[2]{0:T(128)} %pad_add_fusion.id_ref, bf16[640,1440]{1,0:T(8,128)(2,1)} %get-tuple-element.82.w_ref, bf16[1440,1024]{1,0:T(8,128)(2,1)} %make_patches.1.p_ref), custom_call_target="tpu_custom_call" | custom-call | flops 2642411520 | bytes 1966080 | tf_op jit(solution)/shard_map/forward/pallas_call | solution.py:30
  46.4 1.5 %collective-permute-done.12 = bf16[2,1800,128]{2,1,0:T(8,128)(2,1)S(1)} collective-permute-done((bf16[2,1800,128]{2,1,0:T(8,128)(2,1)}, bf16[2,1800,128]{2,1,0:T(8,128)(2,1)S(1)}, u32[]{:S(2)}, u32[]{:S(2)}) %collective-permute-start.12) | collective-permute-done | bytes 921632 | tf_op jit(solution)/shard_map/ppermute | solution.py:571
  48.0 1.4 %collective-permute-start.14 = (bf16[1800,128]{1,0:T(8,128)(2,1)S(1)}, bf16[1800,128]{1,0:T(8,128)(2,1)S(1)}, u32[]{:S(2)}, u32[]{:S(2)}) collective-permute-start(bf16[1800,128]{1,0:T(8,128)(2,1)S(1)} %fusion), channel_id=1, source_target_pairs={{0,8},{1,5},{2,10},{3,7},{4,12},{5,1},{6,14},{7,3},{8,0},{9,13},{1... | collective-permute-start | bytes 1382408 | tf_op jit(solution)/shard_map/ppermute | solution.py:571
  49.4 1.1 convert_add_fusion.2
  51.3 6.0 %image_grad.1 = (bf16[160,256]{1,0:T(8,128)(2,1)}, bf16[160,256]{1,0:T(8,128)(2,1)}, bf16[160,256]{1,0:T(8,128)(2,1)}, bf16[160,256]{1,0:T(8,128)(2,1)}) custom-call(s32[2]{0:T(128)} %pad_add_fusion.id_ref, bf16[1024,640]{1,0:T(8,128)(2,1)} %get-tuple-element.88.h_ref, bf16[1440,640]{1,0:T(8,128)(2,1)} %get-tuple-element.75.w_ref, ...), custom_call_target="tpu_custom_call" | custom-call | flops 1887436800 | bytes 1310720 | tf_op jit(solution)/shard_map/image_grad/pallas_call | solution.py:30
  57.6 2.4 %collective-permute-start.20 = (bf16[1800,128]{1,0:T(8,128)(2,1)S(1)}, bf16[1800,128]{1,0:T(8,128)(2,1)S(1)}, u32[]{:S(2)}, u32[]{:S(2)}) collective-permute-start(bf16[1800,128]{1,0:T(8,128)(2,1)S(1)} %fusion.2), channel_id=1, source_target_pairs={{0,16},{4,20},{8,24},{12,28},{16,0},{20,4},{24,8},{28,12},{1,17},{... | collective-permute-start | bytes 1382408 | tf_op jit(solution)/shard_map/ppermute | solution.py:539
  60.7 3.3 %skip_grad_term.1 = (f32[400,128]{1,0:T(8,128)}, f32[400,128]{1,0:T(8,128)}, bf16[2,400,128]{2,1,0:T(8,128)(2,1)}) custom-call(s32[2]{0:T(128)} %pad_add_fusion.id_ref, f32[800,256]{1,0:T(8,128)} %get-tuple-element.119.k_ref, bf16[800,256]{1,0:T(8,128)(2,1)} %copy-done.1, bf16[256,1280]{1,0:T(8,128)(2,1)} %get-tuple-element.95.c_ref, ...), custom_call_target="tpu_custom_call" | custom-call | flops 104857600 | bytes 819200 | tf_op jit(solution)/shard_map/skip_grad_term/pallas_call | solution.py:30
  64.0 2.5 %collective-permute-start.19 = (bf16[2,400,128]{2,1,0:T(8,128)(2,1)}, bf16[2,400,128]{2,1,0:T(8,128)(2,1)S(1)}, u32[]{:S(2)}, u32[]{:S(2)}) collective-permute-start(bf16[2,400,128]{2,1,0:T(8,128)(2,1)} %get-tuple-element.96), channel_id=1, source_target_pairs={{0,4},{1,9},{2,6},{3,11},{4,0},{5,13},{6,2},{7,15},{8,12},{9,1},{1... | collective-permute-start | bytes 614408 | tf_op jit(solution)/shard_map/ppermute | solution.py:571
  66.5 2.4 %finish_hidden.1 = (bf16[256,640]{1,0:T(8,128)(2,1)}, bf16[64,640]{1,0:T(8,128)(2,1)}) custom-call(bf16[256,640]{1,0:T(8,128)(2,1)} %bitcast.36, f32[800,256]{1,0:T(8,128)} %get-tuple-element.119.k_ref, bf16[800,256]{1,0:T(8,128)(2,1)} %copy-done.1), custom_call_target="tpu_custom_call" | custom-call | flops 20971520 | bytes 1638400 | tf_op jit(solution)/shard_map/finish_hidden/pallas_call | solution.py:30
  68.9 2.7 %project.1 = bf16[64,1280]{1,0:T(8,128)(2,1)} custom-call(s32[2]{0:T(128)} %pad_add_fusion.id_ref, bf16[64,640]{1,0:T(8,128)(2,1)} %get-tuple-element.97.s_ref, bf16[160,1280]{1,0:T(8,128)(2,1)} %refs_0_, bf16[160,1280]{1,0:T(8,128)(2,1)} %copy-done.10, bf16[160,1280]{1,0:T(8,128)(2,1)} %copy-done.9, bf16[160,1280]{1,0:T(8,128)(2,1)} %copy-done.11), custom_call_target="tpu_custom_call" | custom-call | flops 104857600 | bytes 1638400 | tf_op jit(solution)/shard_map/project/pallas_call | solution.py:30
  71.6 1.0 collective-permute-done.19
  72.6 7.2 %collective-permute-done.20 = bf16[1800,128]{1,0:T(8,128)(2,1)S(1)} collective-permute-done((bf16[1800,128]{1,0:T(8,128)(2,1)S(1)}, bf16[1800,128]{1,0:T(8,128)(2,1)S(1)}, u32[]{:S(2)}, u32[]{:S(2)}) %collective-permute-start.20) | collective-permute-done | bytes 460832 | tf_op jit(solution)/shard_map/ppermute | solution.py:539
  80.1 2.6 %collective-permute-start.25 = (bf16[160,256]{1,0:T(8,128)(2,1)S(1)}, bf16[160,256]{1,0:T(8,128)(2,1)S(1)}, u32[]{:S(2)}, u32[]{:S(2)}) collective-permute-start(bf16[160,256]{1,0:T(8,128)(2,1)S(1)} %copy-done.31), channel_id=1, source_target_pairs={{0,3},{1,2},{2,1},{3,0},{4,7},{5,6},{6,5},{7,4},{8,11},{9,10},{10,... | collective-permute-start | bytes 245768 | tf_op jit(solution)/shard_map/ppermute | solution.py:539
  83.9 1.5 %collective-permute-done.25.refs_3_ = bf16[160,256]{1,0:T(8,128)(2,1)S(1)} collective-permute-done((bf16[160,256]{1,0:T(8,128)(2,1)S(1)}, bf16[160,256]{1,0:T(8,128)(2,1)S(1)}, u32[]{:S(2)}, u32[]{:S(2)}) %collective-permute-start.25) | collective-permute-done | bytes 81952 | tf_op jit(solution)/shard_map/ppermute | solution.py:539
  85.4 2.3 %collective-permute-done.24.refs_2_ = bf16[160,256]{1,0:T(8,128)(2,1)S(1)} collective-permute-done((bf16[160,256]{1,0:T(8,128)(2,1)S(1)}, bf16[160,256]{1,0:T(8,128)(2,1)S(1)}, u32[]{:S(2)}, u32[]{:S(2)}) %collective-permute-start.24) | collective-permute-done | bytes 81952 | tf_op jit(solution)/shard_map/ppermute | solution.py:539
  87.9 1.4 %collective-permute-start.26 = (bf16[2,1800,128]{2,1,0:T(8,128)(2,1)S(1)}, bf16[2,1800,128]{2,1,0:T(8,128)(2,1)S(1)}, u32[]{:S(2)}, u32[]{:S(2)}) collective-permute-start(bf16[2,1800,128]{2,1,0:T(8,128)(2,1)S(1)} %pad_maximum_fusion.p_ref), channel_id=1, source_target_pairs={{0,4},{1,9},{2,6},{3,11},{4,0},{5,13},{6,2},{7,15},{8,12},{9,1},{1... | collective-permute-start | bytes 2764808 | tf_op jit(solution)/shard_map/ppermute | solution.py:571
  89.3 3.2 %collective-permute-start.27 = (bf16[400,128]{1,0:T(8,128)(2,1)S(1)}, bf16[400,128]{1,0:T(8,128)(2,1)S(1)}, u32[]{:S(2)}, u32[]{:S(2)}) collective-permute-start(bf16[400,128]{1,0:T(8,128)(2,1)S(1)} %fusion.6), channel_id=1, source_target_pairs={{0,16},{4,20},{8,24},{12,28},{16,0},{20,4},{24,8},{28,12},{1,17},{... | collective-permute-start | bytes 307208 | tf_op jit(solution)/shard_map/ppermute | solution.py:539
  92.5 2.0 %finish_images.1 = bf16[256,640]{1,0:T(8,128)(2,1)} custom-call(s32[2]{0:T(128)} %pad_add_fusion.id_ref, bf16[160,256]{1,0:T(8,128)(2,1)} %get-tuple-element.103.refs_0_, bf16[160,256]{1,0:T(8,128)(2,1)} %copy-done.24, bf16[160,256]{1,0:T(8,128)(2,1)} %copy-done.23, bf16[160,256]{1,0:T(8,128)(2,1)} %copy-done.22), custom_call_target="tpu_custom_call" | custom-call | bytes 655360 | tf_op jit(solution)/shard_map/finish_images/pallas_call | solution.py:30
  94.5 8.5 %collective-permute-done.27 = bf16[400,128]{1,0:T(8,128)(2,1)S(1)} collective-permute-done((bf16[400,128]{1,0:T(8,128)(2,1)S(1)}, bf16[400,128]{1,0:T(8,128)(2,1)S(1)}, u32[]{:S(2)}, u32[]{:S(2)}) %collective-permute-start.27) | collective-permute-done | bytes 102432 | tf_op jit(solution)/shard_map/ppermute | solution.py:539
  103.4 3.7 %place_grad.2 = (f32[1440,640]{1,0:T(8,128)}, f32[4,360,128]{2,1,0:T(8,128)}) custom-call(s32[2]{0:T(128)} %pad_add_fusion.id_ref, bf16[2,1800,128]{2,1,0:T(8,128)(2,1)} %copy-done), custom_call_target="tpu_custom_call" | custom-call | bytes 2764800 | tf_op jit(solution)/shard_map/place_grad/pallas_call | solution.py:342
  107.2 4.0 %collective-permute-start.29 = (bf16[2,400,128]{2,1,0:T(8,128)(2,1)S(1)}, bf16[2,400,128]{2,1,0:T(8,128)(2,1)S(1)}, u32[]{:S(2)}, u32[]{:S(2)}) collective-permute-start(bf16[2,400,128]{2,1,0:T(8,128)(2,1)S(1)} %pad_maximum_fusion.1.refs_0_), channel_id=1, source_target_pairs={{0,4},{1,9},{2,6},{3,11},{4,0},{5,13},{6,2},{7,15},{8,12},{9,1},{1... | collective-permute-start | bytes 614408 | tf_op jit(solution)/shard_map/ppermute | solution.py:571
  112.1 3.1 %place_grad.3 = f32[1440,640]{1,0:T(8,128)} custom-call(s32[2]{0:T(128)} %pad_add_fusion.id_ref, bf16[2,1800,128]{2,1,0:T(8,128)(2,1)} %copy-done.5, f32[1440,640]{1,0:T(8,128)} %get-tuple-element.115.refs_0_, f32[4,360,128]{2,1,0:T(8,128)} %get-tuple-element.116.refs_1_), custom_call_target="tpu_custom_call", output_to_operand_aliasing={{}: (2, {})} | custom-call | bytes 2764800 | tf_op jit(solution)/shard_map/place_grad/pallas_call | solution.py:342
  115.9 2.0 %place_skip.1 = f32[160,1280]{1,0:T(8,128)} custom-call(s32[2]{0:T(128)} %pad_add_fusion.id_ref, bf16[2,400,128]{2,1,0:T(8,128)(2,1)} %copy-done.8, bf16[2,400,128]{2,1,0:T(8,128)(2,1)} %copy-done.17), custom_call_target="tpu_custom_call" | custom-call | bytes 1228800 | tf_op jit(solution)/shard_map/place_skip/pallas_call | solution.py:30
  (122 shorter events, 16.6 us)
Async XLA Ops:
  0.7 12.6 %collective-permute-start.4 = (bf16[64,1280]{1,0:T(8,128)(2,1)}, bf16[64,1280]{1,0:T(8,128)(2,1)S(1)}, u32[]{:S(2)}, u32[]{:S(2)}) collective-permute-start(bf16[64,1280]{1,0:T(8,128)(2,1)} %bitcast.40), channel_id=1, source_target_pairs={{0,2},{1,3},{2,0},{3,1},{4,6},{5,7},{6,4},{7,5},{8,10},{9,11},{10,... | collective-permute-start | bytes 491528 | tf_op jit(solution)/shard_map/ppermute | solution.py:539
  5.2 6.7 %collective-permute-start.1 = (bf16[160,256]{1,0:T(8,128)(2,1)}, bf16[160,256]{1,0:T(8,128)(2,1)S(1)}, u32[]{:S(2)}, u32[]{:S(2)}) collective-permute-start(bf16[160,256]{1,0:T(8,128)(2,1)} %get-tuple-element.64), channel_id=1, source_target_pairs={{0,2},{1,3},{2,0},{3,1},{4,6},{5,7},{6,4},{7,5},{8,10},{9,11},{10,... | collective-permute-start | bytes 245768 | tf_op jit(solution)/shard_map/ppermute | solution.py:539
  5.3 6.7 %collective-permute-start.2 = (bf16[160,256]{1,0:T(8,128)(2,1)}, bf16[160,256]{1,0:T(8,128)(2,1)S(1)}, u32[]{:S(2)}, u32[]{:S(2)}) collective-permute-start(bf16[160,256]{1,0:T(8,128)(2,1)} %get-tuple-element.65), channel_id=1, source_target_pairs={{0,3},{1,2},{2,1},{3,0},{4,7},{5,6},{6,5},{7,4},{8,11},{9,10},{10,... | collective-permute-start | bytes 245768 | tf_op jit(solution)/shard_map/ppermute | solution.py:539
  12.0 12.7 %collective-permute-start.7 = (bf16[256,640]{1,0:T(8,128)(2,1)S(1)}, bf16[256,640]{1,0:T(8,128)(2,1)S(1)}, u32[]{:S(2)}, u32[]{:S(2)}) collective-permute-start(bf16[256,640]{1,0:T(8,128)(2,1)S(1)} %bitcast.46), channel_id=1, source_target_pairs={{0,2},{1,3},{2,0},{3,1},{4,6},{5,7},{6,4},{7,5},{8,10},{9,11},{10,... | collective-permute-start | bytes 983048 | tf_op jit(solution)/shard_map/ppermute | solution.py:539
  12.6 2.4 %collective-permute-start.3 = (bf16[64,1280]{1,0:T(8,128)(2,1)S(1)}, bf16[64,1280]{1,0:T(8,128)(2,1)S(1)}, u32[]{:S(2)}, u32[]{:S(2)}) collective-permute-start(bf16[64,1280]{1,0:T(8,128)(2,1)S(1)} %bitcast.42), channel_id=1, source_target_pairs={{0,1},{1,0},{2,3},{3,2},{4,5},{5,4},{6,7},{7,6},{8,9},{9,8},{10,11... | collective-permute-start | bytes 491528 | tf_op jit(solution)/shard_map/ppermute | solution.py:539
  13.2 1.7 %collective-permute-start.5 = (bf16[64,1280]{1,0:T(8,128)(2,1)S(1)}, bf16[64,1280]{1,0:T(8,128)(2,1)S(1)}, u32[]{:S(2)}, u32[]{:S(2)}) collective-permute-start(bf16[64,1280]{1,0:T(8,128)(2,1)S(1)} %collective-permute-done.4.refs_2_), channel_id=1, source_target_pairs={{0,1},{1,0},{2,3},{3,2},{4,5},{5,4},{6,7},{7,6},{8,9},{9,8},{10,11... | collective-permute-start | bytes 491528 | tf_op jit(solution)/shard_map/ppermute | solution.py:539
  13.3 1.6 %collective-permute-start = (bf16[160,256]{1,0:T(8,128)(2,1)}, bf16[160,256]{1,0:T(8,128)(2,1)S(1)}, u32[]{:S(2)}, u32[]{:S(2)}) collective-permute-start(bf16[160,256]{1,0:T(8,128)(2,1)} %get-tuple-element.63), channel_id=1, source_target_pairs={{0,1},{1,0},{2,3},{3,2},{4,5},{5,4},{6,7},{7,6},{8,9},{9,8},{10,11... | collective-permute-start | bytes 245768 | tf_op jit(solution)/shard_map/ppermute | solution.py:539
  18.6 6.1 %collective-permute-start.10 = (bf16[160,256]{1,0:T(8,128)(2,1)}, bf16[160,256]{1,0:T(8,128)(2,1)S(1)}, u32[]{:S(2)}, u32[]{:S(2)}) collective-permute-start(bf16[160,256]{1,0:T(8,128)(2,1)} %get-tuple-element.68.refs_4_), channel_id=1, source_target_pairs={{0,3},{1,2},{2,1},{3,0},{4,7},{5,6},{6,5},{7,4},{8,11},{9,10},{10,... | collective-permute-start | bytes 245768 | tf_op jit(solution)/shard_map/ppermute | solution.py:539
  19.3 5.4 %collective-permute-start.8 = (bf16[160,256]{1,0:T(8,128)(2,1)}, bf16[160,256]{1,0:T(8,128)(2,1)S(1)}, u32[]{:S(2)}, u32[]{:S(2)}) collective-permute-start(bf16[160,256]{1,0:T(8,128)(2,1)} %get-tuple-element.68.refs_4_), channel_id=1, source_target_pairs={{0,1},{1,0},{2,3},{3,2},{4,5},{5,4},{6,7},{7,6},{8,9},{9,8},{10,11... | collective-permute-start | bytes 245768 | tf_op jit(solution)/shard_map/ppermute | solution.py:539
  19.6 5.3 %collective-permute-start.9 = (bf16[160,256]{1,0:T(8,128)(2,1)}, bf16[160,256]{1,0:T(8,128)(2,1)S(1)}, u32[]{:S(2)}, u32[]{:S(2)}) collective-permute-start(bf16[160,256]{1,0:T(8,128)(2,1)} %get-tuple-element.68.refs_4_), channel_id=1, source_target_pairs={{0,2},{1,3},{2,0},{3,1},{4,6},{5,7},{6,4},{7,5},{8,10},{9,11},{10,... | collective-permute-start | bytes 245768 | tf_op jit(solution)/shard_map/ppermute | solution.py:539
  20.5 5.7 %collective-permute-start.6 = (bf16[256,640]{1,0:T(8,128)(2,1)S(1)}, bf16[256,640]{1,0:T(8,128)(2,1)S(1)}, u32[]{:S(2)}, u32[]{:S(2)}) collective-permute-start(bf16[256,640]{1,0:T(8,128)(2,1)S(1)} %bitcast.47), channel_id=1, source_target_pairs={{0,1},{1,0},{2,3},{3,2},{4,5},{5,4},{6,7},{7,6},{8,9},{9,8},{10,11... | collective-permute-start | bytes 983048 | tf_op jit(solution)/shard_map/ppermute | solution.py:539
  24.9 2.0 %collective-permute-start.11 = (bf16[256,640]{1,0:T(8,128)(2,1)S(1)}, bf16[256,640]{1,0:T(8,128)(2,1)S(1)}, u32[]{:S(2)}, u32[]{:S(2)}) collective-permute-start(bf16[256,640]{1,0:T(8,128)(2,1)S(1)} %collective-permute-done.7.refs_2_), channel_id=1, source_target_pairs={{0,1},{1,0},{2,3},{3,2},{4,5},{5,4},{6,7},{7,6},{8,9},{9,8},{10,11... | collective-permute-start | bytes 983048 | tf_op jit(solution)/shard_map/ppermute | solution.py:539
  25.6 11.0 %collective-permute-start.13 = (bf16[160,1280]{1,0:T(8,128)(2,1)S(1)}, bf16[160,1280]{1,0:T(8,128)(2,1)S(1)}, u32[]{:S(2)}, u32[]{:S(2)}) collective-permute-start(bf16[160,1280]{1,0:T(8,128)(2,1)S(1)} %copy-done.2), channel_id=1, source_target_pairs={{0,2},{1,3},{2,0},{3,1},{4,6},{5,7},{6,4},{7,5},{8,10},{9,11},{10,... | collective-permute-start | bytes 1228808 | tf_op jit(solution)/shard_map/ppermute | solution.py:539
  35.1 12.8 %collective-permute-start.12 = (bf16[2,1800,128]{2,1,0:T(8,128)(2,1)}, bf16[2,1800,128]{2,1,0:T(8,128)(2,1)S(1)}, u32[]{:S(2)}, u32[]{:S(2)}) collective-permute-start(bf16[2,1800,128]{2,1,0:T(8,128)(2,1)} %get-tuple-element.79), channel_id=1, source_target_pairs={{0,4},{1,9},{2,6},{3,11},{4,0},{5,13},{6,2},{7,15},{8,12},{9,1},{1... | collective-permute-start | bytes 2764808 | tf_op jit(solution)/shard_map/ppermute | solution.py:571
  45.0 4.3 %collective-permute-start.15 = (bf16[2,800,256]{2,1,0:T(8,128)(2,1)}, bf16[2,800,256]{2,1,0:T(8,128)(2,1)S(1)}, u32[]{:S(2)}, u32[]{:S(2)}) collective-permute-start(bf16[2,800,256]{2,1,0:T(8,128)(2,1)} %get-tuple-element.83), channel_id=1, source_target_pairs={{0,1},{1,0},{2,3},{3,2},{4,5},{5,4},{6,7},{7,6},{8,9},{9,8},{10,11... | collective-permute-start | bytes 2457608 | tf_op jit(solution)/shard_map/ppermute | solution.py:539
  45.9 11.4 %collective-permute-start.16 = (bf16[160,1280]{1,0:T(8,128)(2,1)S(1)}, bf16[160,1280]{1,0:T(8,128)(2,1)S(1)}, u32[]{:S(2)}, u32[]{:S(2)}) collective-permute-start(bf16[160,1280]{1,0:T(8,128)(2,1)S(1)} %copy-done.2), channel_id=1, source_target_pairs={{0,1},{1,0},{2,3},{3,2},{4,5},{5,4},{6,7},{7,6},{8,9},{9,8},{10,11... | collective-permute-start | bytes 1228808 | tf_op jit(solution)/shard_map/ppermute | solution.py:539
  46.0 11.4 %collective-permute-start.17 = (bf16[160,1280]{1,0:T(8,128)(2,1)S(1)}, bf16[160,1280]{1,0:T(8,128)(2,1)S(1)}, u32[]{:S(2)}, u32[]{:S(2)}) collective-permute-start(bf16[160,1280]{1,0:T(8,128)(2,1)S(1)} %collective-permute-done.13.refs_2_), channel_id=1, source_target_pairs={{0,1},{1,0},{2,3},{3,2},{4,5},{5,4},{6,7},{7,6},{8,9},{9,8},{10,11... | collective-permute-start | bytes 1228808 | tf_op jit(solution)/shard_map/ppermute | solution.py:539
  48.0 9.4 %collective-permute-start.14 = (bf16[1800,128]{1,0:T(8,128)(2,1)S(1)}, bf16[1800,128]{1,0:T(8,128)(2,1)S(1)}, u32[]{:S(2)}, u32[]{:S(2)}) collective-permute-start(bf16[1800,128]{1,0:T(8,128)(2,1)S(1)} %fusion), channel_id=1, source_target_pairs={{0,8},{1,5},{2,10},{3,7},{4,12},{5,1},{6,14},{7,3},{8,0},{9,13},{1... | collective-permute-start | bytes 1382408 | tf_op jit(solution)/shard_map/ppermute | solution.py:571
  50.4 9.5 %collective-permute-start.18 = (bf16[800,256]{1,0:T(8,128)(2,1)S(1)}, bf16[800,256]{1,0:T(8,128)(2,1)S(1)}, u32[]{:S(2)}, u32[]{:S(2)}) collective-permute-start(bf16[800,256]{1,0:T(8,128)(2,1)S(1)} %get-tuple-element.120), channel_id=1, source_target_pairs={{0,2},{1,3},{2,0},{3,1},{4,6},{5,7},{6,4},{7,5},{8,10},{9,11},{10,... | collective-permute-start | bytes 1228808 | tf_op jit(solution)/shard_map/ppermute | solution.py:539
  57.6 22.2 %collective-permute-start.20 = (bf16[1800,128]{1,0:T(8,128)(2,1)S(1)}, bf16[1800,128]{1,0:T(8,128)(2,1)S(1)}, u32[]{:S(2)}, u32[]{:S(2)}) collective-permute-start(bf16[1800,128]{1,0:T(8,128)(2,1)S(1)} %fusion.2), channel_id=1, source_target_pairs={{0,16},{4,20},{8,24},{12,28},{16,0},{20,4},{24,8},{28,12},{1,17},{... | collective-permute-start | bytes 1382408 | tf_op jit(solution)/shard_map/ppermute | solution.py:539
  64.0 8.6 %collective-permute-start.19 = (bf16[2,400,128]{2,1,0:T(8,128)(2,1)}, bf16[2,400,128]{2,1,0:T(8,128)(2,1)S(1)}, u32[]{:S(2)}, u32[]{:S(2)}) collective-permute-start(bf16[2,400,128]{2,1,0:T(8,128)(2,1)} %get-tuple-element.96), channel_id=1, source_target_pairs={{0,4},{1,9},{2,6},{3,11},{4,0},{5,13},{6,2},{7,15},{8,12},{9,1},{1... | collective-permute-start | bytes 614408 | tf_op jit(solution)/shard_map/ppermute | solution.py:571
  71.6 17.7 %copy-start.16 = (f32[400,128]{1,0:T(8,128)S(1)}, f32[400,128]{1,0:T(8,128)}, u32[]{:S(2)}) copy-start(f32[400,128]{1,0:T(8,128)} %get-tuple-element.99) | copy-start | bytes 614404
  79.9 7.8 %collective-permute-start.22 = (bf16[1800,128]{1,0:T(8,128)(2,1)S(1)}, bf16[1800,128]{1,0:T(8,128)(2,1)S(1)}, u32[]{:S(2)}, u32[]{:S(2)}) collective-permute-start(bf16[1800,128]{1,0:T(8,128)(2,1)S(1)} %add_convert_fusion), channel_id=1, source_target_pairs={{0,8},{1,5},{2,10},{3,7},{4,12},{5,1},{6,14},{7,3},{8,0},{9,13},{1... | collective-permute-start | bytes 1382408 | tf_op jit(solution)/shard_map/ppermute | solution.py:571
  80.1 5.3 %collective-permute-start.25 = (bf16[160,256]{1,0:T(8,128)(2,1)S(1)}, bf16[160,256]{1,0:T(8,128)(2,1)S(1)}, u32[]{:S(2)}, u32[]{:S(2)}) collective-permute-start(bf16[160,256]{1,0:T(8,128)(2,1)S(1)} %copy-done.31), channel_id=1, source_target_pairs={{0,3},{1,2},{2,1},{3,0},{4,7},{5,6},{6,5},{7,4},{8,11},{9,10},{10,... | collective-permute-start | bytes 245768 | tf_op jit(solution)/shard_map/ppermute | solution.py:539
  82.7 5.0 %collective-permute-start.24 = (bf16[160,256]{1,0:T(8,128)(2,1)S(1)}, bf16[160,256]{1,0:T(8,128)(2,1)S(1)}, u32[]{:S(2)}, u32[]{:S(2)}) collective-permute-start(bf16[160,256]{1,0:T(8,128)(2,1)S(1)} %copy-done.30), channel_id=1, source_target_pairs={{0,2},{1,3},{2,0},{3,1},{4,6},{5,7},{6,4},{7,5},{8,10},{9,11},{10,... | collective-permute-start | bytes 245768 | tf_op jit(solution)/shard_map/ppermute | solution.py:539
  83.6 4.1 %collective-permute-start.23 = (bf16[160,256]{1,0:T(8,128)(2,1)S(1)}, bf16[160,256]{1,0:T(8,128)(2,1)S(1)}, u32[]{:S(2)}, u32[]{:S(2)}) collective-permute-start(bf16[160,256]{1,0:T(8,128)(2,1)S(1)} %copy-done.29), channel_id=1, source_target_pairs={{0,1},{1,0},{2,3},{3,2},{4,5},{5,4},{6,7},{7,6},{8,9},{9,8},{10,11... | collective-permute-start | bytes 245768 | tf_op jit(solution)/shard_map/ppermute | solution.py:539
  83.7 5.6 %collective-permute-start.21 = (bf16[400,128]{1,0:T(8,128)(2,1)S(1)}, bf16[400,128]{1,0:T(8,128)(2,1)S(1)}, u32[]{:S(2)}, u32[]{:S(2)}) collective-permute-start(bf16[400,128]{1,0:T(8,128)(2,1)S(1)} %fusion.4), channel_id=1, source_target_pairs={{0,8},{1,5},{2,10},{3,7},{4,12},{5,1},{6,14},{7,3},{8,0},{9,13},{1... | collective-permute-start | bytes 307208 | tf_op jit(solution)/shard_map/ppermute | solution.py:571
  87.8 15.6 %copy-start = (bf16[2,1800,128]{2,1,0:T(8,128)(2,1)}, bf16[2,1800,128]{2,1,0:T(8,128)(2,1)S(1)}, u32[]{:S(2)}) copy-start(bf16[2,1800,128]{2,1,0:T(8,128)(2,1)S(1)} %pad_maximum_fusion.p_ref) | copy-start | bytes 2764804
  87.9 23.3 %collective-permute-start.26 = (bf16[2,1800,128]{2,1,0:T(8,128)(2,1)S(1)}, bf16[2,1800,128]{2,1,0:T(8,128)(2,1)S(1)}, u32[]{:S(2)}, u32[]{:S(2)}) collective-permute-start(bf16[2,1800,128]{2,1,0:T(8,128)(2,1)S(1)} %pad_maximum_fusion.p_ref), channel_id=1, source_target_pairs={{0,4},{1,9},{2,6},{3,11},{4,0},{5,13},{6,2},{7,15},{8,12},{9,1},{1... | collective-permute-start | bytes 2764808 | tf_op jit(solution)/shard_map/ppermute | solution.py:571
  89.3 13.6 %collective-permute-start.27 = (bf16[400,128]{1,0:T(8,128)(2,1)S(1)}, bf16[400,128]{1,0:T(8,128)(2,1)S(1)}, u32[]{:S(2)}, u32[]{:S(2)}) collective-permute-start(bf16[400,128]{1,0:T(8,128)(2,1)S(1)} %fusion.6), channel_id=1, source_target_pairs={{0,16},{4,20},{8,24},{12,28},{16,0},{20,4},{24,8},{28,12},{1,17},{... | collective-permute-start | bytes 307208 | tf_op jit(solution)/shard_map/ppermute | solution.py:539
  103.0 4.1 %collective-permute-start.28 = (bf16[400,128]{1,0:T(8,128)(2,1)S(1)}, bf16[400,128]{1,0:T(8,128)(2,1)S(1)}, u32[]{:S(2)}, u32[]{:S(2)}) collective-permute-start(bf16[400,128]{1,0:T(8,128)(2,1)S(1)} %add_convert_fusion.1), channel_id=1, source_target_pairs={{0,8},{1,5},{2,10},{3,7},{4,12},{5,1},{6,14},{7,3},{8,0},{9,13},{1... | collective-permute-start | bytes 307208 | tf_op jit(solution)/shard_map/ppermute | solution.py:571
  107.2 8.1 %collective-permute-start.29 = (bf16[2,400,128]{2,1,0:T(8,128)(2,1)S(1)}, bf16[2,400,128]{2,1,0:T(8,128)(2,1)S(1)}, u32[]{:S(2)}, u32[]{:S(2)}) collective-permute-start(bf16[2,400,128]{2,1,0:T(8,128)(2,1)S(1)} %pad_maximum_fusion.1.refs_0_), channel_id=1, source_target_pairs={{0,4},{1,9},{2,6},{3,11},{4,0},{5,13},{6,2},{7,15},{8,12},{9,1},{1... | collective-permute-start | bytes 614408 | tf_op jit(solution)/shard_map/ppermute | solution.py:571
  (33 other events, 203.3 us)
